TPU v7x, 256 devices: a whole 4x4x8 slice. The times are simulated.
256 devices in a mesh: blk: 32 (over z, y_lo, core), head: 8 (over y_hi, x).
Axes of the slice: x: 4, y: 4 (y_hi: 2, y_lo: 2; y = y_hi * 2 + y_lo), z: 8, core: 2. Of those that a mesh axis runs over, the one named last changes fastest.
Arguments:
- hidden: bfloat16 [2048, 5120], P('blk'), may hold values from -6 to 6
- norm_gain: float32 [5120], replicated, may hold values from 0.1 to 1.9
- w_query: bfloat16 [5120, 5120], P('blk', 'head'), may hold values from -0.078125 to 0.078125
- key_projection_weight: bfloat16 [5120, 1024], P('blk', 'head'), may hold values from -0.3125 to 0.3125
- value_projection_weight: bfloat16 [5120, 1024], P('blk', 'head'), may hold values from -0.078125 to 0.078125
- w_out: bfloat16 [5120, 5120], P('head', 'blk'), may hold values from -0.078125 to 0.078125
- cache_keys: bfloat16 [8, 65536, 128], P('head', 'blk'), may hold values from -1024 to 1024
- earlier_values: bfloat16 [8, 65536, 128], P('head', 'blk'), may hold values from -6 to 6
- cache_len: int32 [32], P('blk'), may hold values from 512 to 2048, as said below
- stretch_start: int32 [1], replicated, may hold values from 0 to 4194303
Outputs:
- attention_out: bfloat16 [2048, 5120], P('head', 'blk')
Inputs may be any that keep to these rules, and one draw needn't show every extreme that they name: Cache shard s holds valid entries at its first cache_len[s] positions, the rest are ignored; at least one shard is full.
All inputs are finite; a program needn't handle non-finite values.
Results may differ from a plain program's by a relative error of at most 0.023.
The roundings to bfloat16 on the way count: a program that leaves them out, or rounds other values in their place, can miss the bound.
Values may be sent and summed in bfloat16 or wider, within the bound.
No kernel may reach another device: no remote copies, remote signals or barrier semaphores. Data moves between devices by JAX's collectives and lax.ppermute only.
A program may use at most 192 MiB of HBM per device.

v0:
```python
import functools

import jax
import jax.numpy as jnp
from jax import lax
from jax.experimental import pallas as pl
from jax.experimental.pallas import tpu as pltpu
from jax.sharding import Mesh
from jax.sharding import PartitionSpec as P

BLK = ("z", "y", "c")
BF = jnp.bfloat16
F32 = jnp.float32
NEG = -1e30
KEYS = 512


def shift(x, axis, d):
    n = lax.axis_size(axis)
    return lax.ppermute(x, axis, [(i, (i + d) % n) for i in range(n)])


def ring(x, axis, beside=None):
    n = lax.axis_size(axis)
    ahead, behind = [x], [x]
    for step in range(n // 2):
        if beside and step in beside:
            ahead[-1], beside[step] = lax.optimization_barrier((ahead[-1], beside[step]))
        ahead.append(shift(ahead[-1], axis, 1))
        if step < (n - 1) // 2:
            behind.append(shift(behind[-1], axis, -1))
        if beside and step == 0:
            ahead[-1], behind[-1] = lax.optimization_barrier((ahead[-1], behind[-1]))
    return ahead + behind[:0:-1]


def nt(a, b):
    return lax.dot_general(a, b, (((1,), (1,)), ((), ())), preferred_element_type=F32)


def tn(a, b):
    return lax.dot_general(a, b, (((0,), (0,)), ((), ())), preferred_element_type=F32)


VM = pl.BlockSpec(memory_space=pltpu.VMEM)
SM = pl.BlockSpec(memory_space=pltpu.SMEM)


def params(mib=56):
    return pltpu.CompilerParams(vmem_limit_bytes=mib << 20)


def side_by_side(arrays):
    rows = arrays[0].shape[0]
    widths = [a.shape[1] for a in arrays]

    def body(*refs):
        out, at = refs[-1], 0
        for ref, width in zip(refs[:-1], widths):
            out[:, at : at + width] = ref[...]
            at += width

    return pl.pallas_call(
        body,
        out_shape=jax.ShapeDtypeStruct((rows, sum(widths)), arrays[0].dtype),
        in_specs=[VM] * len(arrays),
        out_specs=VM,
        compiler_params=params(),
        name="side_by_side",
    )(*arrays)


def project(where, x, blocks):
    rows, _ = x.shape
    n = len(blocks)
    r, cols = blocks[0].shape
    t = rows // 4

    def kernel(where_ref, x_ref, *refs):
        w_refs, (keep, send, whole, total) = refs[:n], refs[n:]
        z, c = where_ref[0], where_ref[2]
        for d in range(n):
            at = lax.rem(z + (n - d), n)
            whole[pl.ds(pl.multiple_of(at * r, 16), r), :] = w_refs[d][...]
        total[...] = jnp.dot(x_ref[...], whole[...], preferred_element_type=F32).reshape(4, t, cols)
        for y in range(2):
            keep[y] = total[2 * y + c]
            send[y] = total[2 * y + 1 - c]

    half = jax.ShapeDtypeStruct((2, t, cols), F32)
    return pl.pallas_call(
        kernel,
        out_shape=[half, half],
        in_specs=[SM, VM] + [VM] * n,
        out_specs=[VM, VM],
        scratch_shapes=[pltpu.VMEM((n * r, cols), BF), pltpu.VMEM((4, t, cols), F32)],
        compiler_params=params(),
        name="project",
    )(where, x, *blocks)


def sum_cores(where, kept, came, q_cols):
    _, t, cols = kept.shape

    def kernel(where_ref, a_ref, b_ref, near, away, rest):
        y = where_ref[1]
        near[...] = a_ref[y, :, :q_cols] + b_ref[y, :, :q_cols]
        away[...] = a_ref[1 - y, :, :q_cols] + b_ref[1 - y, :, :q_cols]
        rest[...] = a_ref[:, :, q_cols:] + b_ref[:, :, q_cols:]

    q = jax.ShapeDtypeStruct((t, q_cols), F32)
    return pl.pallas_call(
        kernel,
        out_shape=[q, q, jax.ShapeDtypeStruct((2, t, cols - q_cols), F32)],
        in_specs=[SM, VM, VM],
        out_specs=[VM, VM, VM],
        compiler_params=params(),
        name="sum_cores",
    )(where, kept, came)


def norm_cut(hidden, gain, n):
    t, model = hidden.shape
    width = model // (4 * n)

    def kernel(h_ref, g_ref, out):
        x = h_ref[...].astype(F32)
        normed = (
            x * lax.rsqrt(jnp.mean(x * x, axis=-1, keepdims=True) + 1e-05) * g_ref[...]
        ).astype(BF)
        for k in range(n):
            for j in range(4):
                at = (4 * k + j) * width
                out[j, :, k * width : (k + 1) * width] = normed[:, at : at + width]

    return pl.pallas_call(
        kernel,
        out_shape=jax.ShapeDtypeStruct((4, t, n * width), BF),
        in_specs=[VM, VM],
        out_specs=VM,
        compiler_params=params(),
        name="norm_cut",
    )(hidden, gain.reshape(1, model))


TAIL = 16


def join_cache(keys, values, length):
    rows, d = keys.shape

    def kernel(len_ref, k_ref, v_ref, out):
        out[0:rows, :] = k_ref[...]
        out[rows : 2 * rows, :] = v_ref[...]
        lane = lax.broadcasted_iota(jnp.int32, (TAIL, d), 1)
        digits = jnp.where(lane == 0, len_ref[0] // 64, lax.rem(len_ref[0], 64))
        out[2 * rows :, :] = digits.astype(F32).astype(BF)

    return pl.pallas_call(
        kernel,
        out_shape=jax.ShapeDtypeStruct((2 * rows + TAIL, d), keys.dtype),
        in_specs=[SM, VM, VM],
        out_specs=VM,
        compiler_params=params(),
        name="join_cache",
    )(length, keys, values)


def attend(where, chunks, dists, caches, new_pairs):
    n = len(chunks)
    t, width = chunks[0].shape
    d = caches[0].shape[1]
    each = (caches[0].shape[0] - TAIL) // 2
    ns = len(caches)
    room = ns * each + 4 * KEYS
    g = width // d
    rows = n * g * t
    fresh = new_pairs[0][0].shape[0]

    def kernel(where_ref, *refs):
        q_refs = refs[:n]
        c_refs = refs[n : n + ns]
        nk0, nv0, nk1, nv1 = refs[n + ns : n + ns + 4]
        out = refs[n + ns + 4]
        q_all, m, l, acc, s_a, s_b, token, stats, k_ref, v_ref = refs[n + ns + 5 :]
        top_key = c_refs[0][0:1, :]
        at = jnp.int32(0)
        counted = jnp.int32(0)
        lane = lax.broadcasted_iota(jnp.int32, (TAIL, d), 1)
        row = lax.broadcasted_iota(jnp.int32, (TAIL, d), 0)
        place = jnp.where(row > 0, 0.0, jnp.where(lane == 0, 64.0, jnp.where(lane == 1, 1.0, 0.0)))
        for i in range(ns):
            digits = c_refs[i][2 * each : 2 * each + TAIL, :].astype(F32)
            length = jnp.sum(digits * place).astype(jnp.int32)
            counted = counted + length
            at = pl.multiple_of(at, 16)
            k_ref[pl.ds(at, each), :] = c_refs[i][0:each, :]
            v_ref[pl.ds(at, each), :] = c_refs[i][each : 2 * each, :]
            whole = length // 16
            odd = length - whole * 16
            tail = pl.multiple_of(at + whole * 16, 16)

            @pl.when(odd > 0)
            def _():
                valid = lax.broadcasted_iota(jnp.int32, (16, d), 0) < odd
                k_tile = k_ref[pl.ds(tail, 16), :].astype(F32)
                v_tile = v_ref[pl.ds(tail, 16), :].astype(F32)
                k_ref[pl.ds(tail, 16), :] = jnp.where(valid, k_tile, top_key.astype(F32)).astype(BF)
                v_ref[pl.ds(tail, 16), :] = jnp.where(valid, v_tile, 0.0).astype(BF)

            at = at + ((length + 15) // 16) * 16
        used = pl.multiple_of(at, 16)
        k_ref[pl.ds(used, 2 * KEYS), :] = jnp.broadcast_to(top_key, (2 * KEYS, d))
        v_ref[pl.ds(used, 2 * KEYS), :] = jnp.zeros((2 * KEYS, d), BF)
        z, y, c = where_ref[0], where_ref[1], where_ref[2]
        nz = where_ref[3]
        for i in range(n):
            base = lax.rem(z + nz - dists[i], nz) * (4 * t) + (2 * y + c) * t
            for h in range(g):
                at = (i * g + h) * t
                q_all[at : at + t, :] = q_refs[i][:, h * d : (h + 1) * d]
            span = slice(i * g * t, (i + 1) * g * t)
            token[:, span] = base + lax.rem(lax.broadcasted_iota(jnp.int32, (1, g * t), 1), t)
        m[...] = jnp.full(m.shape, NEG, F32)
        l[...] = jnp.zeros(l.shape, F32)
        acc[...] = jnp.zeros(acc.shape, F32)

        def scores(at):
            return nt(k_ref[pl.ds(pl.multiple_of(at, KEYS), KEYS), :], q_all[...])

        def absorb(s, values):
            before = m[...]
            now = jnp.maximum(before, jnp.max(s, axis=0, keepdims=True))
            fade = jnp.exp(before - now)
            p = jnp.exp(s - now)
            l[...] = l[...] * fade + jnp.sum(p, axis=0, keepdims=True)
            m[...] = now
            acc[...] = acc[...] * fade + tn(values, p.astype(BF))

        def values_at(at):
            return v_ref[pl.ds(pl.multiple_of(at, KEYS), KEYS), :]

        pairs = (used + 2 * KEYS - 1) // (2 * KEYS)
        s_a[...] = scores(0)

        def visit(u, _):
            at = u * (2 * KEYS)
            s_b[...] = scores(at + KEYS)
            absorb(s_a[...], values_at(at))
            s_a[...] = scores(at + 2 * KEYS)
            absorb(s_b[...], values_at(at + KEYS))
            return 0

        lax.fori_loop(0, pairs, visit, 0)
        extra = (pairs * (2 * KEYS) - counted).astype(F32)
        first = nt(k_ref[0:8, :], q_all[...])[0:1]
        l[...] = l[...] - extra * jnp.exp(first - m[...])
        for part, (nk, nv) in enumerate(((nk0, nv0), (nk1, nv1))):
            row = lax.broadcasted_iota(jnp.int32, (fresh, 1), 0)
            side = c if part == 0 else 1 - c
            key_token = z * (4 * t) + (row // t) * (2 * t) + side * t + lax.rem(row, t)
            s = nt(nk[...], q_all[...])
            s = jnp.where(key_token <= token[...], s, NEG)
            absorb(s, nv[...])
        top = m[...]
        top_hi = top.astype(BF).astype(F32)
        top_lo = (top - top_hi).astype(BF).astype(F32)
        scale = jnp.exp(top - (top_hi + top_lo))
        den = l[...] * scale
        den_hi = den.astype(BF).astype(F32)
        den_lo = den - den_hi
        numer = (acc[...] * scale).T
        stats[...] = jnp.zeros(stats.shape, F32)
        for i in range(n):
            owner = lax.rem(z + nz - dists[i], nz)
            for h in range(g):
                at = slice((i * g + h) * t, (i * g + h + 1) * t)
                out[:, owner, :, h * d : (h + 1) * d] = numer[at].reshape(n, t // n, d).astype(BF)
                for k, row in enumerate((top_hi, top_lo, den_hi, den_lo)):
                    stats[8 * k + h : 8 * k + h + 1, :] = row[:, at]
            out[:, owner, :, g * d :] = stats[...].T.reshape(n, t // n, 128).astype(BF)

    return pl.pallas_call(
        kernel,
        out_shape=jax.ShapeDtypeStruct((n, n, t // n, width + 128), BF),
        in_specs=[SM] + [VM] * (n + ns + 4),
        out_specs=VM,
        scratch_shapes=[
            pltpu.VMEM((rows, d), BF),
            pltpu.VMEM((1, rows), F32),
            pltpu.VMEM((1, rows), F32),
            pltpu.VMEM((d, rows), F32),
            pltpu.VMEM((KEYS, rows), F32),
            pltpu.VMEM((KEYS, rows), F32),
            pltpu.VMEM((1, rows), jnp.int32),
            pltpu.VMEM((128, t), F32),
            pltpu.VMEM((room, d), BF),
            pltpu.VMEM((room, d), BF),
        ],
        compiler_params=params(),
        name="attend",
    )(where, *chunks, *caches, *new_pairs[0], *new_pairs[1])


def merge(parts, d):
    n, t, width = parts.shape
    g = (width - 128) // d

    def kernel(ins, out):
        stats = [ins[i, :, g * d :].astype(F32) for i in range(n)]
        for h in range(g):
            tops = [s[:, h : h + 1] + s[:, 8 + h : 9 + h] for s in stats]
            dens = [s[:, 16 + h : 17 + h] + s[:, 24 + h : 25 + h] for s in stats]
            top = functools.reduce(jnp.maximum, tops)
            shares = [jnp.exp(a - top) for a in tops]
            den = sum(w * a for w, a in zip(shares, dens))
            num = sum(w * ins[i, :, h * d : (h + 1) * d].astype(F32) for i, w in enumerate(shares))
            out[:, h * d : (h + 1) * d] = (num / den).astype(BF)

    return pl.pallas_call(
        kernel,
        out_shape=jax.ShapeDtypeStruct((t, g * d), BF),
        in_specs=[VM],
        out_specs=VM,
        compiler_params=params(),
        name="merge",
    )(parts)


def project_out(where, contexts, weights, n):
    t, inner = contexts[0].shape
    cols = weights.shape[0]
    part = t // n

    def kernel(where_ref, *refs):
        c_refs, (w_ref, out, tokens) = refs[:4], refs[4:]
        here = 2 * where_ref[1] + where_ref[2]
        for f in range(4):
            tokens[:, f ^ here] = c_refs[f][...].reshape(n, part, inner).astype(F32)
        rows = tokens[...].reshape(4 * t, inner).astype(BF)
        out[...] = nt(rows, w_ref[...]).astype(BF).reshape(n, 4 * part, cols)

    return pl.pallas_call(
        kernel,
        out_shape=jax.ShapeDtypeStruct((n, 4 * part, cols), BF),
        in_specs=[SM] + [VM] * 5,
        out_specs=VM,
        scratch_shapes=[pltpu.VMEM((n, 4, part, inner), F32)],
        compiler_params=params(),
        name="project_out",
    )(where, *contexts, weights)


def sum_heads(parts, n):
    heads, rows, cols = parts.shape
    width = cols // n

    def kernel(p_ref, out):
        total = p_ref[0].astype(F32)
        for i in range(1, heads):
            total = total + p_ref[i].astype(F32)
        for k in range(n):
            out[k] = total[:, k * width : (k + 1) * width].astype(BF)

    return pl.pallas_call(
        kernel,
        out_shape=jax.ShapeDtypeStruct((n, rows, width), BF),
        in_specs=[VM],
        out_specs=VM,
        compiler_params=params(),
        name="sum_heads",
    )(parts)


def per_device(
    hidden,
    norm_gain,
    w_query,
    key_projection_weight,
    value_projection_weight,
    w_out,
    cache_keys,
    earlier_values,
    cache_len,
    stretch_start,
):
    t, model = hidden.shape
    d = cache_keys.shape[2]
    q_cols = w_query.shape[1]
    kv_cols = key_projection_weight.shape[1]
    nz = lax.axis_size("z")
    z, y, c = lax.axis_index("z"), lax.axis_index("y"), lax.axis_index("c")
    where = jnp.stack([z, y, c, jnp.int32(nz)]).astype(jnp.int32)

    cut = norm_cut(hidden, norm_gain, nz)
    x = lax.all_to_all(cut, ("y", "c"), 0, 0, tiled=True).reshape(4 * t, model // 4)
    near = join_cache(cache_keys[0], earlier_values[0], cache_len)

    weights = side_by_side([w_query, key_projection_weight, value_projection_weight])
    beside = {1: near, 2: x}
    blocks = ring(weights, "z", beside)
    near, x = beside[1], beside[2]

    beside = shift(near, "y", 1)
    x, beside = lax.optimization_barrier((x, beside))
    caches = [near, beside, shift(near, "c", 1), shift(beside, "c", 1)]

    keep, send = project(where, x, blocks)
    out_cols, keep = lax.optimization_barrier((w_out.T, keep))
    out_cols = lax.all_gather(out_cols, "z", axis=0, tiled=True)

    q_near, q_away, kv = sum_cores(where, keep, shift(send, "c", 1), q_cols)
    queries = (q_near + shift(q_away, "y", 1)).astype(BF)
    fresh = (kv + shift(kv, "y", 1)).astype(BF).reshape(2 * t, 2 * kv_cols)
    other = shift(fresh, "c", 1)
    new_pairs = [(f[:, :kv_cols], f[:, kv_cols:]) for f in (fresh, other)]

    token = lax.axis_index(BLK) * t + jnp.arange(t, dtype=jnp.int32)
    positions = stretch_start[0] + token
    temper = jnp.log(((positions + 1) // 8192).astype(F32) + 1.0) * 0.1 + 1.0
    scaled = (
        lax.optimization_barrier(queries).astype(F32) * (temper * d ** (-0.5))[:, None]
    ).astype(BF)

    chunks = ring(scaled, "z")
    chunks, caches = lax.optimization_barrier((chunks, caches))
    partial = attend(where, chunks, list(range(nz)), caches, new_pairs)
    returned = lax.all_to_all(partial, "z", 0, 0, tiled=True)
    context = merge(returned.reshape(nz, t, -1), d)
    context_y = shift(context, "y", 1)
    contexts = [context, shift(context, "c", 1), context_y, shift(context_y, "c", 1)]
    terms = project_out(where, contexts, out_cols, nz)
    shares = lax.all_to_all(terms, "head", 0, 0, tiled=True)
    final = lax.all_to_all(sum_heads(shares, nz), "z", 0, 0, tiled=True)
    final = final.reshape(nz, 4, t // nz, -1).transpose(1, 0, 2, 3)
    return final.reshape(4 * t, -1)


def solution(mesh):
    finer = Mesh(mesh.devices.reshape(8, 2, 2, mesh.shape["head"]), ("z", "y", "c", "head"))
    return jax.shard_map(
        per_device,
        mesh=finer,
        in_specs=(
            P(BLK, None),
            P(),
            P(BLK, "head"),
            P(BLK, "head"),
            P(BLK, "head"),
            P("head", BLK),
            P("head", BLK, None),
            P("head", BLK, None),
            P(BLK),
            P(),
        ),
        out_specs=P("head", BLK),
        check_vma=False,
    )
```

profile of v0, /device:TPU:2, one launch (start us, length us, event | category | flops | bytes accessed | tf_op | source)
XLA Modules:
  0.0 209.3 jit_solution(16466408817184867928)
XLA Ops:
  6.5 1.7 side_by_side.1.refs_0_
  8.2 1.9 collective-permute-start
  10.2 3.9 %collective-permute-start.1 = (bf16[160,896]{1,0:T(8,128)(2,1)}, bf16[160,896]{1,0:T(8,128)(2,1)S(1)}, u32[]{:S(2)}, u32[]{:S(2)}) collective-permute-start(bf16[160,896]{1,0:T(8,128)(2,1)} %side_by_side.1.refs_0_), channel_id=1, source_target_pairs={{0,224},{32,0},{64,32},{96,64},{128,96},{160,128},{192,160},{224,1... | collective-permute-start | bytes 860168 | tf_op jit(solution)/shard_map/ppermute | solution.py:20
  14.1 2.5 %norm_cut.1 = bf16[4,64,1280]{2,1,0:T(8,128)(2,1)} custom-call(bf16[64,5120]{1,0:T(8,128)(2,1)} %h_ref.1, f32[1,5120]{1,0:T(1,128)} %bitcast.25), custom_call_target="tpu_custom_call" | custom-call | tf_op jit(solution)/shard_map/norm_cut/pallas_call | solution.py:136
  16.6 3.5 %all-to-all-start = ((bf16[4,64,1280]{2,1,0:T(8,128)(2,1)}), bf16[4,64,1280]{2,1,0:T(8,128)(2,1)S(1)}, u32[]{:S(2)}, u32[]{:S(2)}) async-start(bf16[4,64,1280]{2,1,0:T(8,128)(2,1)} %norm_cut.1), calls=%async_computation | async-start | bytes 1310720 | tf_op jit(solution)/shard_map/all_to_all | solution.py:396
  20.7 2.3 %join_cache.1.refs_8_ = bf16[4112,128]{1,0:T(8,128)(2,1)} custom-call(s32[1]{0:T(128)S(6)} %copy.14.len_ref, bf16[2048,128]{1,0:T(8,128)(2,1)} %bitcast.18, bf16[2048,128]{1,0:T(8,128)(2,1)} %bitcast.19), custom_call_target="tpu_custom_call" | custom-call | tf_op jit(solution)/shard_map/join_cache/pallas_call | solution.py:159
  23.0 2.0 collective-permute-start.3
  25.1 3.2 %collective-permute-start.6 = (bf16[160,896]{1,0:T(8,128)(2,1)S(1)}, bf16[160,896]{1,0:T(8,128)(2,1)S(1)}, u32[]{:S(2)}, u32[]{:S(2)}) collective-permute-start(bf16[160,896]{1,0:T(8,128)(2,1)S(1)} %collective-permute-done.1.refs_7_), channel_id=1, source_target_pairs={{0,224},{32,0},{64,32},{96,64},{128,96},{160,128},{192,160},{224,1... | collective-permute-start | bytes 860168 | tf_op jit(solution)/shard_map/ppermute | solution.py:20
  28.3 2.4 %all-to-all-done = bf16[4,64,1280]{2,1,0:T(8,128)(2,1)S(1)} async-done(((bf16[4,64,1280]{2,1,0:T(8,128)(2,1)}), bf16[4,64,1280]{2,1,0:T(8,128)(2,1)S(1)}, u32[]{:S(2)}, u32[]{:S(2)}) %all-to-all-start) | async-done | bytes 655392 | tf_op jit(solution)/shard_map/all_to_all | solution.py:396
  30.7 4.1 %collective-permute-done.2.refs_2_ = bf16[160,896]{1,0:T(8,128)(2,1)S(1)} collective-permute-done((bf16[160,896]{1,0:T(8,128)(2,1)S(1)}, bf16[160,896]{1,0:T(8,128)(2,1)S(1)}, u32[]{:S(2)}, u32[]{:S(2)}) %collective-permute-start.2) | collective-permute-done | bytes 286752 | tf_op jit(solution)/shard_map/ppermute | solution.py:20
  34.9 3.2 %collective-permute-start.7 = (bf16[160,896]{1,0:T(8,128)(2,1)S(1)}, bf16[160,896]{1,0:T(8,128)(2,1)S(1)}, u32[]{:S(2)}, u32[]{:S(2)}) collective-permute-start(bf16[160,896]{1,0:T(8,128)(2,1)S(1)} %collective-permute-done.6.refs_6_), channel_id=1, source_target_pairs={{0,224},{32,0},{64,32},{96,64},{128,96},{160,128},{192,160},{224,1... | collective-permute-start | bytes 860168 | tf_op jit(solution)/shard_map/ppermute | solution.py:20
  38.1 5.7 %collective-permute-done.4.refs_3_ = bf16[160,896]{1,0:T(8,128)(2,1)S(1)} collective-permute-done((bf16[160,896]{1,0:T(8,128)(2,1)S(1)}, bf16[160,896]{1,0:T(8,128)(2,1)S(1)}, u32[]{:S(2)}, u32[]{:S(2)}) %collective-permute-start.4) | collective-permute-done | bytes 286752 | tf_op jit(solution)/shard_map/ppermute | solution.py:20
  44.5 8.4 %collective-permute-done.3.refs_9_ = bf16[4112,128]{1,0:T(8,128)(2,1)S(1)} collective-permute-done((bf16[4112,128]{1,0:T(8,128)(2,1)}, bf16[4112,128]{1,0:T(8,128)(2,1)S(1)}, u32[]{:S(2)}, u32[]{:S(2)}) %collective-permute-start.3) | collective-permute-done | bytes 1052704 | tf_op jit(solution)/shard_map/ppermute | solution.py:20
  53.6 3.8 %project.1 = (f32[2,64,896]{2,1,0:T(8,128)}, f32[2,64,896]{2,1,0:T(8,128)}) custom-call(s32[4]{0:T(128)} %pad_add_fusion.where_ref, bf16[256,1280]{1,0:T(8,128)(2,1)} %bitcast.17, bf16[160,896]{1,0:T(8,128)(2,1)} %side_by_side.1.refs_0_, bf16[160,896]{1,0:T(8,128)(2,1)} %copy-done.7, bf16[160,896]{1,0:T(8,128)(2,1)} %copy-done.9, ...), custom_call_target="tpu_custom_call" | custom-call | tf_op jit(solution)/shard_map/project/pallas_call | solution.py:91
  57.3 2.0 collective-permute-done.8.b_ref
  60.1 2.0 sum_cores.1
  65.4 3.9 %collective-permute-done.9 = f32[64,640]{1,0:T(8,128)S(1)} collective-permute-done((f32[64,640]{1,0:T(8,128)}, f32[64,640]{1,0:T(8,128)S(1)}, u32[]{:S(2)}, u32[]{:S(2)}) %collective-permute-start.9) | collective-permute-done | bytes 163872 | tf_op jit(solution)/shard_map/ppermute | solution.py:20
  70.5 3.2 %collective-permute-start.14 = (bf16[64,640]{1,0:T(8,128)(2,1)S(1)}, bf16[64,640]{1,0:T(8,128)(2,1)S(1)}, u32[]{:S(2)}, u32[]{:S(2)}) collective-permute-start(bf16[64,640]{1,0:T(8,128)(2,1)S(1)} %multiply_convert_fusion.refs_0_), channel_id=1, source_target_pairs={{0,224},{32,0},{64,32},{96,64},{128,96},{160,128},{192,160},{224,1... | collective-permute-start | bytes 245768 | tf_op jit(solution)/shard_map/ppermute | solution.py:20
  73.7 2.4 %collective-permute-done.10.refs_1_ = bf16[64,640]{1,0:T(8,128)(2,1)S(1)} collective-permute-done((bf16[64,640]{1,0:T(8,128)(2,1)S(1)}, bf16[64,640]{1,0:T(8,128)(2,1)S(1)}, u32[]{:S(2)}, u32[]{:S(2)}) %collective-permute-start.10) | collective-permute-done | bytes 81952 | tf_op jit(solution)/shard_map/ppermute | solution.py:20
  77.2 3.6 %collective-permute-start.15 = (bf16[64,640]{1,0:T(8,128)(2,1)S(1)}, bf16[64,640]{1,0:T(8,128)(2,1)S(1)}, u32[]{:S(2)}, u32[]{:S(2)}) collective-permute-start(bf16[64,640]{1,0:T(8,128)(2,1)S(1)} %collective-permute-done.14.refs_7_), channel_id=1, source_target_pairs={{0,224},{32,0},{64,32},{96,64},{128,96},{160,128},{192,160},{224,1... | collective-permute-start | bytes 245768 | tf_op jit(solution)/shard_map/ppermute | solution.py:20
  82.6 2.2 %collective-permute-done.15.refs_6_ = bf16[64,640]{1,0:T(8,128)(2,1)S(1)} collective-permute-done((bf16[64,640]{1,0:T(8,128)(2,1)S(1)}, bf16[64,640]{1,0:T(8,128)(2,1)S(1)}, u32[]{:S(2)}, u32[]{:S(2)}) %collective-permute-start.15) | collective-permute-done | bytes 81952 | tf_op jit(solution)/shard_map/ppermute | solution.py:20
  84.8 3.7 %collective-permute-start.16 = (bf16[64,640]{1,0:T(8,128)(2,1)S(1)}, bf16[64,640]{1,0:T(8,128)(2,1)S(1)}, u32[]{:S(2)}, u32[]{:S(2)}) collective-permute-start(bf16[64,640]{1,0:T(8,128)(2,1)S(1)} %collective-permute-done.15.refs_6_), channel_id=1, source_target_pairs={{0,224},{32,0},{64,32},{96,64},{128,96},{160,128},{192,160},{224,1... | collective-permute-start | bytes 245768 | tf_op jit(solution)/shard_map/ppermute | solution.py:20
  89.9 2.2 %collective-permute-done.16.refs_5_ = bf16[64,640]{1,0:T(8,128)(2,1)S(1)} collective-permute-done((bf16[64,640]{1,0:T(8,128)(2,1)S(1)}, bf16[64,640]{1,0:T(8,128)(2,1)S(1)}, u32[]{:S(2)}, u32[]{:S(2)}) %collective-permute-start.16) | collective-permute-done | bytes 81952 | tf_op jit(solution)/shard_map/ppermute | solution.py:20
  92.1 3.2 %collective-permute-done.13.refs_4_ = bf16[64,640]{1,0:T(8,128)(2,1)S(1)} collective-permute-done((bf16[64,640]{1,0:T(8,128)(2,1)S(1)}, bf16[64,640]{1,0:T(8,128)(2,1)S(1)}, u32[]{:S(2)}, u32[]{:S(2)}) %collective-permute-start.13) | collective-permute-done | bytes 81952 | tf_op jit(solution)/shard_map/ppermute | solution.py:20
  96.2 30.2 %attend.1 = bf16[8,8,8,768]{3,2,1,0:T(8,128)(2,1)} custom-call(s32[4]{0:T(128)} %pad_add_fusion.where_ref, bf16[64,640]{1,0:T(8,128)(2,1)} %copy-done.6, bf16[64,640]{1,0:T(8,128)(2,1)} %copy-done.16, bf16[64,640]{1,0:T(8,128)(2,1)} %copy-done.18, bf16[64,640]{1,0:T(8,128)(2,1)} %copy-done.20, bf16[64,640]{1,0:T(8,128)(2,1)} %copy-done.22, ...), custom_call_target="tpu_custom_call" | custom-call | tf_op jit(solution)/shard_map/attend/pallas_call | solution.py:283
  126.4 29.9 %all_to_all.20 = bf16[8,8,8,768]{3,2,1,0:T(8,128)(2,1)} all-to-all(bf16[8,8,8,768]{3,2,1,0:T(8,128)(2,1)} %attend.1), channel_id=1, replica_groups=mesh['z'=8,'y'=2,'c'=2,'head'=8] {'z'}, dimensions={0} | all-to-all | bytes 1572864 | tf_op jit(solution)/shard_map/all_to_all | solution.py:428
  156.3 2.4 %merge.1.refs_0_ = bf16[64,640]{1,0:T(8,128)(2,1)} custom-call(bf16[8,64,768]{2,1,0:T(8,128)(2,1)} %bitcast.16), custom_call_target="tpu_custom_call" | custom-call | tf_op jit(solution)/shard_map/merge/pallas_call | solution.py:320
  158.9 4.5 %collective-permute-done.22.refs_2_ = bf16[64,640]{1,0:T(8,128)(2,1)S(1)} collective-permute-done((bf16[64,640]{1,0:T(8,128)(2,1)}, bf16[64,640]{1,0:T(8,128)(2,1)S(1)}, u32[]{:S(2)}, u32[]{:S(2)}) %collective-permute-start.22) | collective-permute-done | bytes 81952 | tf_op jit(solution)/shard_map/ppermute | solution.py:20
  165.3 3.2 %project_out.1 = bf16[8,32,1280]{2,1,0:T(8,128)(2,1)} custom-call(s32[4]{0:T(128)} %pad_add_fusion.where_ref, bf16[64,640]{1,0:T(8,128)(2,1)} %merge.1.refs_0_, bf16[64,640]{1,0:T(8,128)(2,1)} %copy-done.14, bf16[64,640]{1,0:T(8,128)(2,1)} %copy-done.13, bf16[64,640]{1,0:T(8,128)(2,1)} %copy-done.15, bf16[1280,640]{1,0:T(8,128)(2,1)} %all-gather.2.cloned.1.call-done.refs_4_), custom_call_target="tpu_custom_call" | custom-call | tf_op jit(solution)/shard_map/project_out/pallas_call | solution.py:343
  168.5 19.0 %all_to_all.21.p_ref = bf16[8,32,1280]{2,1,0:T(8,128)(2,1)} all-to-all(bf16[8,32,1280]{2,1,0:T(8,128)(2,1)} %project_out.1), channel_id=1, replica_groups=mesh['z'=8,'y'=2,'c'=2,'head'=8] {'head'}, dimensions={0} | all-to-all | bytes 1310720 | tf_op jit(solution)/shard_map/all_to_all | solution.py:433
  187.5 1.9 sum_heads.1
  189.4 12.3 %all_to_all.22 = bf16[8,32,160]{2,1,0:T(8,128)(2,1)S(1)} all-to-all(bf16[8,32,160]{2,1,0:T(8,128)(2,1)} %sum_heads.1), channel_id=1, replica_groups=mesh['z'=8,'y'=2,'c'=2,'head'=8] {'z'}, dimensions={0} | all-to-all | bytes 163840 | tf_op jit(solution)/shard_map/all_to_all | solution.py:434
  (88 shorter events, 13.9 us)
Async XLA Ops:
  8.2 14.8 %collective-permute-start = (bf16[160,896]{1,0:T(8,128)(2,1)}, bf16[160,896]{1,0:T(8,128)(2,1)S(1)}, u32[]{:S(2)}, u32[]{:S(2)}) collective-permute-start(bf16[160,896]{1,0:T(8,128)(2,1)} %side_by_side.1.refs_0_), channel_id=1, source_target_pairs={{0,32},{32,64},{64,96},{96,128},{128,160},{160,192},{192,224},{224... | collective-permute-start | bytes 860168 | tf_op jit(solution)/shard_map/ppermute | solution.py:20
  10.2 12.9 %collective-permute-start.1 = (bf16[160,896]{1,0:T(8,128)(2,1)}, bf16[160,896]{1,0:T(8,128)(2,1)S(1)}, u32[]{:S(2)}, u32[]{:S(2)}) collective-permute-start(bf16[160,896]{1,0:T(8,128)(2,1)} %side_by_side.1.refs_0_), channel_id=1, source_target_pairs={{0,224},{32,0},{64,32},{96,64},{128,96},{160,128},{192,160},{224,1... | collective-permute-start | bytes 860168 | tf_op jit(solution)/shard_map/ppermute | solution.py:20
  16.6 14.2 %all-to-all-start = ((bf16[4,64,1280]{2,1,0:T(8,128)(2,1)}), bf16[4,64,1280]{2,1,0:T(8,128)(2,1)S(1)}, u32[]{:S(2)}, u32[]{:S(2)}) async-start(bf16[4,64,1280]{2,1,0:T(8,128)(2,1)} %norm_cut.1), calls=%async_computation | async-start | bytes 1310720 | tf_op jit(solution)/shard_map/all_to_all | solution.py:396
  20.0 144.6 %all-gather.2.cloned.1.call-start = ((), (), s32[]{:S(2)}) async-start(), calls=%async_computation.4 | async-start | bytes 1843200 | tf_op jit(solution)/shard_map/all_gather | solution.py:410
  23.0 29.8 %copy-start.7 = (bf16[160,896]{1,0:T(8,128)(2,1)}, bf16[160,896]{1,0:T(8,128)(2,1)S(1)}, u32[]{:S(2)}) copy-start(bf16[160,896]{1,0:T(8,128)(2,1)S(1)} %collective-permute-done.refs_1_) | copy-start | bytes 860164
  23.0 29.8 %copy-start.8 = (bf16[160,896]{1,0:T(8,128)(2,1)}, bf16[160,896]{1,0:T(8,128)(2,1)S(1)}, u32[]{:S(2)}) copy-start(bf16[160,896]{1,0:T(8,128)(2,1)S(1)} %collective-permute-done.1.refs_7_) | copy-start | bytes 860164
  23.0 29.8 %collective-permute-start.3 = (bf16[4112,128]{1,0:T(8,128)(2,1)}, bf16[4112,128]{1,0:T(8,128)(2,1)S(1)}, u32[]{:S(2)}, u32[]{:S(2)}) collective-permute-start(bf16[4112,128]{1,0:T(8,128)(2,1)} %join_cache.1.refs_8_), channel_id=1, source_target_pairs={{0,16},{16,0},{1,17},{17,1},{2,18},{18,2},{3,19},{19,3},{4,20},{20... | collective-permute-start | bytes 3158024 | tf_op jit(solution)/shard_map/ppermute | solution.py:20
  25.1 9.8 %collective-permute-start.2 = (bf16[160,896]{1,0:T(8,128)(2,1)S(1)}, bf16[160,896]{1,0:T(8,128)(2,1)S(1)}, u32[]{:S(2)}, u32[]{:S(2)}) collective-permute-start(bf16[160,896]{1,0:T(8,128)(2,1)S(1)} %collective-permute-done.refs_1_), channel_id=1, source_target_pairs={{0,32},{32,64},{64,96},{96,128},{128,160},{160,192},{192,224},{224... | collective-permute-start | bytes 860168 | tf_op jit(solution)/shard_map/ppermute | solution.py:20
  25.1 9.8 %collective-permute-start.6 = (bf16[160,896]{1,0:T(8,128)(2,1)S(1)}, bf16[160,896]{1,0:T(8,128)(2,1)S(1)}, u32[]{:S(2)}, u32[]{:S(2)}) collective-permute-start(bf16[160,896]{1,0:T(8,128)(2,1)S(1)} %collective-permute-done.1.refs_7_), channel_id=1, source_target_pairs={{0,224},{32,0},{64,32},{96,64},{128,96},{160,128},{192,160},{224,1... | collective-permute-start | bytes 860168 | tf_op jit(solution)/shard_map/ppermute | solution.py:20
  30.7 22.1 %copy-start.1 = (bf16[4,64,1280]{2,1,0:T(8,128)(2,1)}, bf16[4,64,1280]{2,1,0:T(8,128)(2,1)S(1)}, u32[]{:S(2)}) copy-start(bf16[4,64,1280]{2,1,0:T(8,128)(2,1)S(1)} %all-to-all-done) | copy-start | bytes 1966084
  34.9 8.9 %collective-permute-start.4 = (bf16[160,896]{1,0:T(8,128)(2,1)S(1)}, bf16[160,896]{1,0:T(8,128)(2,1)S(1)}, u32[]{:S(2)}, u32[]{:S(2)}) collective-permute-start(bf16[160,896]{1,0:T(8,128)(2,1)S(1)} %collective-permute-done.2.refs_2_), channel_id=1, source_target_pairs={{0,32},{32,64},{64,96},{96,128},{128,160},{160,192},{192,224},{224... | collective-permute-start | bytes 860168 | tf_op jit(solution)/shard_map/ppermute | solution.py:20
  34.9 17.9 %collective-permute-start.7 = (bf16[160,896]{1,0:T(8,128)(2,1)S(1)}, bf16[160,896]{1,0:T(8,128)(2,1)S(1)}, u32[]{:S(2)}, u32[]{:S(2)}) collective-permute-start(bf16[160,896]{1,0:T(8,128)(2,1)S(1)} %collective-permute-done.6.refs_6_), channel_id=1, source_target_pairs={{0,224},{32,0},{64,32},{96,64},{128,96},{160,128},{192,160},{224,1... | collective-permute-start | bytes 860168 | tf_op jit(solution)/shard_map/ppermute | solution.py:20
  43.8 9.0 %collective-permute-start.5 = (bf16[160,896]{1,0:T(8,128)(2,1)S(1)}, bf16[160,896]{1,0:T(8,128)(2,1)}, u32[]{:S(2)}, u32[]{:S(2)}) collective-permute-start(bf16[160,896]{1,0:T(8,128)(2,1)S(1)} %collective-permute-done.4.refs_3_), channel_id=1, source_target_pairs={{0,32},{32,64},{64,96},{96,128},{128,160},{160,192},{192,224},{224... | collective-permute-start | bytes 860168 | tf_op jit(solution)/shard_map/ppermute | solution.py:20
  57.3 2.0 collective-permute-start.8
  62.1 7.3 %collective-permute-start.9 = (f32[64,640]{1,0:T(8,128)}, f32[64,640]{1,0:T(8,128)S(1)}, u32[]{:S(2)}, u32[]{:S(2)}) collective-permute-start(f32[64,640]{1,0:T(8,128)} %get-tuple-element.43), channel_id=1, source_target_pairs={{0,16},{16,0},{1,17},{17,1},{2,18},{18,2},{3,19},{19,3},{4,20},{20... | collective-permute-start | bytes 491528 | tf_op jit(solution)/shard_map/ppermute | solution.py:20
  63.2 26.7 %collective-permute-start.17 = (bf16[4112,128]{1,0:T(8,128)(2,1)S(1)}, bf16[4112,128]{1,0:T(8,128)(2,1)S(1)}, u32[]{:S(2)}, u32[]{:S(2)}) collective-permute-start(bf16[4112,128]{1,0:T(8,128)(2,1)S(1)} %copy-done), channel_id=1, source_target_pairs={{0,8},{8,0},{1,9},{9,1},{2,10},{10,2},{3,11},{11,3},{4,12},{12,4},... | collective-permute-start | bytes 3158024 | tf_op jit(solution)/shard_map/ppermute | solution.py:20
  63.3 31.9 %collective-permute-start.18 = (bf16[4112,128]{1,0:T(8,128)(2,1)S(1)}, bf16[4112,128]{1,0:T(8,128)(2,1)S(1)}, u32[]{:S(2)}, u32[]{:S(2)}) collective-permute-start(bf16[4112,128]{1,0:T(8,128)(2,1)S(1)} %collective-permute-done.3.refs_9_), channel_id=1, source_target_pairs={{0,8},{8,0},{1,9},{9,1},{2,10},{10,2},{3,11},{11,3},{4,12},{12,4},... | collective-permute-start | bytes 3158024 | tf_op jit(solution)/shard_map/ppermute | solution.py:20
  63.8 12.4 %collective-permute-start.19 = (f32[2,64,256]{2,1,0:T(8,128)}, f32[2,64,256]{2,1,0:T(8,128)S(1)}, u32[]{:S(2)}, u32[]{:S(2)}) collective-permute-start(f32[2,64,256]{2,1,0:T(8,128)} %get-tuple-element.57), channel_id=1, source_target_pairs={{0,16},{16,0},{1,17},{17,1},{2,18},{18,2},{3,19},{19,3},{4,20},{20... | collective-permute-start | bytes 393224 | tf_op jit(solution)/shard_map/ppermute | solution.py:20
  70.4 24.8 %copy-start.6 = (bf16[64,640]{1,0:T(8,128)(2,1)}, bf16[64,640]{1,0:T(8,128)(2,1)S(1)}, u32[]{:S(2)}) copy-start(bf16[64,640]{1,0:T(8,128)(2,1)S(1)} %multiply_convert_fusion.refs_0_) | copy-start | bytes 245764
  70.4 5.7 %collective-permute-start.10 = (bf16[64,640]{1,0:T(8,128)(2,1)S(1)}, bf16[64,640]{1,0:T(8,128)(2,1)S(1)}, u32[]{:S(2)}, u32[]{:S(2)}) collective-permute-start(bf16[64,640]{1,0:T(8,128)(2,1)S(1)} %multiply_convert_fusion.refs_0_), channel_id=1, source_target_pairs={{0,32},{32,64},{64,96},{96,128},{128,160},{160,192},{192,224},{224... | collective-permute-start | bytes 245768 | tf_op jit(solution)/shard_map/ppermute | solution.py:20
  70.5 6.7 %collective-permute-start.14 = (bf16[64,640]{1,0:T(8,128)(2,1)S(1)}, bf16[64,640]{1,0:T(8,128)(2,1)S(1)}, u32[]{:S(2)}, u32[]{:S(2)}) collective-permute-start(bf16[64,640]{1,0:T(8,128)(2,1)S(1)} %multiply_convert_fusion.refs_0_), channel_id=1, source_target_pairs={{0,224},{32,0},{64,32},{96,64},{128,96},{160,128},{192,160},{224,1... | collective-permute-start | bytes 245768 | tf_op jit(solution)/shard_map/ppermute | solution.py:20
  76.1 19.1 %copy-start.16 = (bf16[64,640]{1,0:T(8,128)(2,1)}, bf16[64,640]{1,0:T(8,128)(2,1)S(1)}, u32[]{:S(2)}) copy-start(bf16[64,640]{1,0:T(8,128)(2,1)S(1)} %collective-permute-done.10.refs_1_) | copy-start | bytes 245764
  76.1 5.8 %collective-permute-start.11 = (bf16[64,640]{1,0:T(8,128)(2,1)S(1)}, bf16[64,640]{1,0:T(8,128)(2,1)S(1)}, u32[]{:S(2)}, u32[]{:S(2)}) collective-permute-start(bf16[64,640]{1,0:T(8,128)(2,1)S(1)} %collective-permute-done.10.refs_1_), channel_id=1, source_target_pairs={{0,32},{32,64},{64,96},{96,128},{128,160},{160,192},{192,224},{224... | collective-permute-start | bytes 245768 | tf_op jit(solution)/shard_map/ppermute | solution.py:20
  77.1 12.1 %collective-permute-start.20 = (bf16[128,256]{1,0:T(8,128)(2,1)S(1)}, bf16[128,256]{1,0:T(8,128)(2,1)S(1)}, u32[]{:S(2)}, u32[]{:S(2)}) collective-permute-start(bf16[128,256]{1,0:T(8,128)(2,1)S(1)} %bitcast.22), channel_id=1, source_target_pairs={{0,8},{8,0},{1,9},{9,1},{2,10},{10,2},{3,11},{11,3},{4,12},{12,4},... | collective-permute-start | bytes 196616 | tf_op jit(solution)/shard_map/ppermute | solution.py:20
  77.2 18.0 %copy-start.17 = (bf16[64,640]{1,0:T(8,128)(2,1)}, bf16[64,640]{1,0:T(8,128)(2,1)S(1)}, u32[]{:S(2)}) copy-start(bf16[64,640]{1,0:T(8,128)(2,1)S(1)} %collective-permute-done.14.refs_7_) | copy-start | bytes 245764
  77.2 7.6 %collective-permute-start.15 = (bf16[64,640]{1,0:T(8,128)(2,1)S(1)}, bf16[64,640]{1,0:T(8,128)(2,1)S(1)}, u32[]{:S(2)}, u32[]{:S(2)}) collective-permute-start(bf16[64,640]{1,0:T(8,128)(2,1)S(1)} %collective-permute-done.14.refs_7_), channel_id=1, source_target_pairs={{0,224},{32,0},{64,32},{96,64},{128,96},{160,128},{192,160},{224,1... | collective-permute-start | bytes 245768 | tf_op jit(solution)/shard_map/ppermute | solution.py:20
  82.0 7.2 %collective-permute-start.12 = (bf16[64,640]{1,0:T(8,128)(2,1)S(1)}, bf16[64,640]{1,0:T(8,128)(2,1)S(1)}, u32[]{:S(2)}, u32[]{:S(2)}) collective-permute-start(bf16[64,640]{1,0:T(8,128)(2,1)S(1)} %collective-permute-done.11.refs_2_), channel_id=1, source_target_pairs={{0,32},{32,64},{64,96},{96,128},{128,160},{160,192},{192,224},{224... | collective-permute-start | bytes 245768 | tf_op jit(solution)/shard_map/ppermute | solution.py:20
  84.8 7.2 %collective-permute-start.16 = (bf16[64,640]{1,0:T(8,128)(2,1)S(1)}, bf16[64,640]{1,0:T(8,128)(2,1)S(1)}, u32[]{:S(2)}, u32[]{:S(2)}) collective-permute-start(bf16[64,640]{1,0:T(8,128)(2,1)S(1)} %collective-permute-done.15.refs_6_), channel_id=1, source_target_pairs={{0,224},{32,0},{64,32},{96,64},{128,96},{160,128},{192,160},{224,1... | collective-permute-start | bytes 245768 | tf_op jit(solution)/shard_map/ppermute | solution.py:20
  89.2 6.0 %collective-permute-start.13 = (bf16[64,640]{1,0:T(8,128)(2,1)S(1)}, bf16[64,640]{1,0:T(8,128)(2,1)S(1)}, u32[]{:S(2)}, u32[]{:S(2)}) collective-permute-start(bf16[64,640]{1,0:T(8,128)(2,1)S(1)} %collective-permute-done.12.refs_3_), channel_id=1, source_target_pairs={{0,32},{32,64},{64,96},{96,128},{128,160},{160,192},{192,224},{224... | collective-permute-start | bytes 245768 | tf_op jit(solution)/shard_map/ppermute | solution.py:20
  158.7 4.7 %collective-permute-start.22 = (bf16[64,640]{1,0:T(8,128)(2,1)}, bf16[64,640]{1,0:T(8,128)(2,1)S(1)}, u32[]{:S(2)}, u32[]{:S(2)}) collective-permute-start(bf16[64,640]{1,0:T(8,128)(2,1)} %merge.1.refs_0_), channel_id=1, source_target_pairs={{0,16},{16,0},{1,17},{17,1},{2,18},{18,2},{3,19},{19,3},{4,20},{20... | collective-permute-start | bytes 245768 | tf_op jit(solution)/shard_map/ppermute | solution.py:20
  158.9 4.5 %collective-permute-start.21 = (bf16[64,640]{1,0:T(8,128)(2,1)}, bf16[64,640]{1,0:T(8,128)(2,1)S(1)}, u32[]{:S(2)}, u32[]{:S(2)}) collective-permute-start(bf16[64,640]{1,0:T(8,128)(2,1)} %merge.1.refs_0_), channel_id=1, source_target_pairs={{0,8},{8,0},{1,9},{9,1},{2,10},{10,2},{3,11},{11,3},{4,12},{12,4},... | collective-permute-start | bytes 245768 | tf_op jit(solution)/shard_map/ppermute | solution.py:20
  163.4 1.3 collective-permute-start.23
  (17 other events, 106.1 us)
Sparse Core Ops, SparseCore 0:
  63.3 42.2 all-gather.1
where the time goes:
time: 210 us; the launch traced here: 209 us
  blocking collectives  61.3 us (29%)
  Pallas kernels  49.8 us (24%)
  waiting for transfers between devices  44.1 us (21%)
  starting transfers between devices  31.4 us (15%)
  between operations  15 us (7%)
  local copies, waits for them, and re-layouts  5.16 us (2%)
  other arithmetic  2.62 us (1%)
    ppermute x24, waiting for transfers between devices, shift(): return lax.ppermute(x, axis, [(i, (i + d) % n) for i in range(n)])  41.6 us
    pallas_call x1, Pallas kernels, attend(): pl.pallas_call(kernel, out_shape=jax.ShapeDtypeStruct((n, n, t // n, widt...  30.2 us
    all_to_all x1, blocking collectives, per_device(): returned = lax.all_to_all(partial, 'z', 0, 0, tiled=True)  29.9 us
    ppermute x24, starting transfers between devices, shift(): return lax.ppermute(x, axis, [(i, (i + d) % n) for i in range(n)])  27.9 us
    all_to_all x1, blocking collectives, per_device(): shares = lax.all_to_all(terms, 'head', 0, 0, tiled=True)  19 us
    all_to_all x1, blocking collectives, per_device(): final = lax.all_to_all(sum_heads(shares, nz), 'z', 0, 0, tiled=True)  12.3 us
  transfers between devices with their start and end apart: 26, of which 14 were waited for; matrix products, arithmetic and copies ran while one was open for 2% of the time, Pallas kernels for 18%

commit v1 on v0

--- a/solution.py
+++ b/solution.py
@@ -13,6 +13,7 @@
 F32 = jnp.float32
 NEG = -1e30
 KEYS = 512
+SPAN = 256
 
 
 def shift(x, axis, d):
@@ -146,56 +147,53 @@
 TAIL = 16
 
 
-def join_cache(keys, values, length):
+def with_length(keys, length):
     rows, d = keys.shape
 
-    def kernel(len_ref, k_ref, v_ref, out):
+    def kernel(len_ref, k_ref, out):
         out[0:rows, :] = k_ref[...]
-        out[rows : 2 * rows, :] = v_ref[...]
         lane = lax.broadcasted_iota(jnp.int32, (TAIL, d), 1)
         digits = jnp.where(lane == 0, len_ref[0] // 64, lax.rem(len_ref[0], 64))
-        out[2 * rows :, :] = digits.astype(F32).astype(BF)
-
-    return pl.pallas_call(
-        kernel,
-        out_shape=jax.ShapeDtypeStruct((2 * rows + TAIL, d), keys.dtype),
-        in_specs=[SM, VM, VM],
-        out_specs=VM,
-        compiler_params=params(),
-        name="join_cache",
-    )(length, keys, values)
-
-
-def attend(where, chunks, dists, caches, new_pairs):
+        out[rows:, :] = digits.astype(F32).astype(BF)
+
+    return pl.pallas_call(
+        kernel,
+        out_shape=jax.ShapeDtypeStruct((rows + TAIL, d), keys.dtype),
+        in_specs=[SM, VM],
+        out_specs=VM,
+        compiler_params=params(),
+        name="with_length",
+    )(length, keys)
+
+
+def attend(where, chunks, dists, keys, values, new_pairs):
     n = len(chunks)
     t, width = chunks[0].shape
-    d = caches[0].shape[1]
-    each = (caches[0].shape[0] - TAIL) // 2
-    ns = len(caches)
-    room = ns * each + 4 * KEYS
+    each, d = values[0].shape
+    ns = len(keys)
+    room = ns * each + 2 * KEYS
     g = width // d
     rows = n * g * t
     fresh = new_pairs[0][0].shape[0]
 
     def kernel(where_ref, *refs):
         q_refs = refs[:n]
-        c_refs = refs[n : n + ns]
-        nk0, nv0, nk1, nv1 = refs[n + ns : n + ns + 4]
-        out = refs[n + ns + 4]
-        q_all, m, l, acc, s_a, s_b, token, stats, k_ref, v_ref = refs[n + ns + 5 :]
-        top_key = c_refs[0][0:1, :]
+        k_in, v_in, refs = refs[n : n + ns], refs[n + ns : n + 2 * ns], refs[n + 2 * ns :]
+        nk0, nv0, nk1, nv1 = refs[:4]
+        out, q_all, m, l, acc, s_a, s_b, token, stats, k_ref, v_ref = refs[4:]
+        top_key = k_in[0][0:1, :]
         at = jnp.int32(0)
         counted = jnp.int32(0)
         lane = lax.broadcasted_iota(jnp.int32, (TAIL, d), 1)
         row = lax.broadcasted_iota(jnp.int32, (TAIL, d), 0)
         place = jnp.where(row > 0, 0.0, jnp.where(lane == 0, 64.0, jnp.where(lane == 1, 1.0, 0.0)))
         for i in range(ns):
-            digits = c_refs[i][2 * each : 2 * each + TAIL, :].astype(F32)
+            digits = k_in[i][each : each + TAIL, :].astype(F32)
             length = jnp.sum(digits * place).astype(jnp.int32)
             counted = counted + length
             at = pl.multiple_of(at, 16)
-            k_ref[pl.ds(at, each), :] = c_refs[i][0:each, :]
-            v_ref[pl.ds(at, each), :] = c_refs[i][each : 2 * each, :]
+            k_ref[pl.ds(at, each), :] = k_in[i][0:each, :]
+            v_ref[pl.ds(at, each), :] = v_in[i][...]
             whole = length // 16
             odd = length - whole * 16
             tail = pl.multiple_of(at + whole * 16, 16)
@@ -210,8 +208,8 @@
 
             at = at + ((length + 15) // 16) * 16
         used = pl.multiple_of(at, 16)
-        k_ref[pl.ds(used, 2 * KEYS), :] = jnp.broadcast_to(top_key, (2 * KEYS, d))
-        v_ref[pl.ds(used, 2 * KEYS), :] = jnp.zeros((2 * KEYS, d), BF)
+        k_ref[pl.ds(used, KEYS), :] = jnp.broadcast_to(top_key, (KEYS, d))
+        v_ref[pl.ds(used, KEYS), :] = jnp.zeros((KEYS, d), BF)
         z, y, c = where_ref[0], where_ref[1], where_ref[2]
         nz = where_ref[3]
         for i in range(n):
@@ -225,43 +223,49 @@
         l[...] = jnp.zeros(l.shape, F32)
         acc[...] = jnp.zeros(acc.shape, F32)
 
-        def scores(at):
-            return nt(k_ref[pl.ds(pl.multiple_of(at, KEYS), KEYS), :], q_all[...])
-
-        def absorb(s, values):
-            before = m[...]
+        def absorb(s, values, cs):
+            before = m[:, cs]
             now = jnp.maximum(before, jnp.max(s, axis=0, keepdims=True))
             fade = jnp.exp(before - now)
             p = jnp.exp(s - now)
-            l[...] = l[...] * fade + jnp.sum(p, axis=0, keepdims=True)
-            m[...] = now
-            acc[...] = acc[...] * fade + tn(values, p.astype(BF))
-
-        def values_at(at):
-            return v_ref[pl.ds(pl.multiple_of(at, KEYS), KEYS), :]
-
-        pairs = (used + 2 * KEYS - 1) // (2 * KEYS)
-        s_a[...] = scores(0)
+            l[:, cs] = l[:, cs] * fade + jnp.sum(p, axis=0, keepdims=True)
+            m[:, cs] = now
+            acc[:, cs] = acc[:, cs] * fade + tn(values, p.astype(BF))
+
+        def block(ref, u):
+            return ref[pl.ds(pl.multiple_of(u * KEYS, KEYS), KEYS), :]
+
+        spans = [slice(lo, lo + SPAN) for lo in range(0, rows, SPAN)]
+        blocks = (used + KEYS - 1) // KEYS
+        for cs in spans:
+            s_a[:, cs] = nt(block(k_ref, 0), q_all[cs, :])
 
         def visit(u, _):
-            at = u * (2 * KEYS)
-            s_b[...] = scores(at + KEYS)
-            absorb(s_a[...], values_at(at))
-            s_a[...] = scores(at + 2 * KEYS)
-            absorb(s_b[...], values_at(at + KEYS))
+            for now, then, at in ((s_a, s_b, 2 * u), (s_b, s_a, 2 * u + 1)):
+                k_next, v_here = block(k_ref, at + 1), block(v_ref, at)
+                for cs in spans:
+                    then[:, cs] = nt(k_next, q_all[cs, :])
+                    absorb(now[:, cs], v_here, cs)
             return 0
 
-        lax.fori_loop(0, pairs, visit, 0)
-        extra = (pairs * (2 * KEYS) - counted).astype(F32)
+        lax.fori_loop(0, blocks // 2, visit, 0)
+
+        @pl.when(lax.rem(blocks, 2) == 1)
+        def _():
+            v_last = block(v_ref, blocks - 1)
+            for cs in spans:
+                absorb(s_a[:, cs], v_last, cs)
+
+        extra = (blocks * KEYS - counted).astype(F32)
         first = nt(k_ref[0:8, :], q_all[...])[0:1]
         l[...] = l[...] - extra * jnp.exp(first - m[...])
         for part, (nk, nv) in enumerate(((nk0, nv0), (nk1, nv1))):
             row = lax.broadcasted_iota(jnp.int32, (fresh, 1), 0)
             side = c if part == 0 else 1 - c
             key_token = z * (4 * t) + (row // t) * (2 * t) + side * t + lax.rem(row, t)
-            s = nt(nk[...], q_all[...])
-            s = jnp.where(key_token <= token[...], s, NEG)
-            absorb(s, nv[...])
+            for cs in spans:
+                s = nt(nk[...], q_all[cs, :])
+                absorb(jnp.where(key_token <= token[:, cs], s, NEG), nv[...], cs)
         top = m[...]
         top_hi = top.astype(BF).astype(F32)
         top_lo = (top - top_hi).astype(BF).astype(F32)
@@ -283,7 +287,7 @@
     return pl.pallas_call(
         kernel,
         out_shape=jax.ShapeDtypeStruct((n, n, t // n, width + 128), BF),
-        in_specs=[SM] + [VM] * (n + ns + 4),
+        in_specs=[SM] + [VM] * (n + 2 * ns + 4),
         out_specs=VM,
         scratch_shapes=[
             pltpu.VMEM((rows, d), BF),
@@ -299,7 +303,7 @@
         ],
         compiler_params=params(),
         name="attend",
-    )(where, *chunks, *caches, *new_pairs[0], *new_pairs[1])
+    )(where, *chunks, *keys, *values, *new_pairs[0], *new_pairs[1])
 
 
 def merge(parts, d):
@@ -394,16 +398,14 @@
 
     cut = norm_cut(hidden, norm_gain, nz)
     x = lax.all_to_all(cut, ("y", "c"), 0, 0, tiled=True).reshape(4 * t, model // 4)
-    near = join_cache(cache_keys[0], earlier_values[0], cache_len)
+    near = with_length(cache_keys[0], cache_len)
 
     weights = side_by_side([w_query, key_projection_weight, value_projection_weight])
-    beside = {1: near, 2: x}
-    blocks = ring(weights, "z", beside)
-    near, x = beside[1], beside[2]
-
-    beside = shift(near, "y", 1)
-    x, beside = lax.optimization_barrier((x, beside))
-    caches = [near, beside, shift(near, "c", 1), shift(beside, "c", 1)]
+    links = {2: x, 3: shift(near, "y", 1)}
+    blocks = ring(weights, "z", links)
+    x, beside = links[2], links[3]
+
+    keys = [near, beside, shift(near, "c", 1), shift(beside, "c", 1)]
 
     keep, send = project(where, x, blocks)
     out_cols, keep = lax.optimization_barrier((w_out.T, keep))
@@ -411,6 +413,9 @@
 
     q_near, q_away, kv = sum_cores(where, keep, shift(send, "c", 1), q_cols)
     queries = (q_near + shift(q_away, "y", 1)).astype(BF)
+    near, queries = lax.optimization_barrier((earlier_values[0], queries))
+    beside = shift(near, "y", 1)
+    values = [near, beside, shift(near, "c", 1), shift(beside, "c", 1)]
     fresh = (kv + shift(kv, "y", 1)).astype(BF).reshape(2 * t, 2 * kv_cols)
     other = shift(fresh, "c", 1)
     new_pairs = [(f[:, :kv_cols], f[:, kv_cols:]) for f in (fresh, other)]
@@ -423,8 +428,7 @@
     ).astype(BF)
 
     chunks = ring(scaled, "z")
-    chunks, caches = lax.optimization_barrier((chunks, caches))
-    partial = attend(where, chunks, list(range(nz)), caches, new_pairs)
+    partial = attend(where, chunks, list(range(nz)), keys, values, new_pairs)
     returned = lax.all_to_all(partial, "z", 0, 0, tiled=True)
     context = merge(returned.reshape(nz, t, -1), d)
     context_y = shift(context, "y", 1)

time: 210 us -> 211 us (level)
  blocking collectives: 61.3 us -> 69.2 us
  Pallas kernels: 49.8 us -> 42.3 us
  waiting for transfers between devices: 44.1 us -> 46.7 us
    all_to_all x1, blocking collectives: 29.9 us -> 37.4 us  [per_device(): returned = lax.all_to_all(partial, 'z', 0, 0, tiled=True)]
    pallas_call x1, Pallas kernels: 30.2 us -> 23.1 us  [attend(): pl.pallas_call(kernel, out_shape=jax.ShapeDtypeStruct((n, n, t // n, widt...]
    ppermute x24 -> x27, waiting for transfers between devices: 41.6 us -> 44.5 us  [shift(): return lax.ppermute(x, axis, [(i, (i + d) % n) for i in range(n)])]
    ppermute x24 -> x27, starting transfers between devices: 27.9 us -> 26.9 us  [shift(): return lax.ppermute(x, axis, [(i, (i + d) % n) for i in range(n)])]
  transfers between devices with their start and end apart: 26 -> 29, of which waited for: 14 -> 15; matrix products, arithmetic and copies ran while one was open for 2% -> 2% of each run, Pallas kernels for 18% -> 14%
where the time goes in v1:
time: 211 us
  blocking collectives  69.2 us (33%)
  waiting for transfers between devices  46.7 us (22%)
  Pallas kernels  42.3 us (20%)
  starting transfers between devices  30.4 us (14%)
  between operations  15 us (7%)
  local copies, waits for them, and re-layouts  4.43 us (2%)
  other arithmetic  2.7 us (1%)
    ppermute x27, waiting for transfers between devices, shift(): return lax.ppermute(x, axis, [(i, (i + d) % n) for i in range(n)])  44.5 us
    all_to_all x1, blocking collectives, per_device(): returned = lax.all_to_all(partial, 'z', 0, 0, tiled=True)  37.4 us
    ppermute x27, starting transfers between devices, shift(): return lax.ppermute(x, axis, [(i, (i + d) % n) for i in range(n)])  26.9 us
    pallas_call x1, Pallas kernels, attend(): pl.pallas_call(kernel, out_shape=jax.ShapeDtypeStruct((n, n, t // n, widt...  23.1 us
    all_to_all x1, blocking collectives, per_device(): shares = lax.all_to_all(terms, 'head', 0, 0, tiled=True)  19.5 us
    all_to_all x1, blocking collectives, per_device(): final = lax.all_to_all(sum_heads(shares, nz), 'z', 0, 0, tiled=True)  12.3 us
  transfers between devices with their start and end apart: 29, of which 15 were waited for; matrix products, arithmetic and copies ran while one was open for 2% of the time, Pallas kernels for 14%

profile of v1, /device:TPU:2, one launch (start us, length us, event | category | flops | bytes accessed | tf_op | source)
XLA Modules:
  0.0 210.8 jit_solution(3104765539525633300)
XLA Ops:
  6.5 1.7 side_by_side.1.refs_0_
  8.2 1.9 collective-permute-start
  10.2 3.9 %collective-permute-start.1 = (bf16[160,896]{1,0:T(8,128)(2,1)}, bf16[160,896]{1,0:T(8,128)(2,1)S(1)}, u32[]{:S(2)}, u32[]{:S(2)}) collective-permute-start(bf16[160,896]{1,0:T(8,128)(2,1)} %side_by_side.1.refs_0_), channel_id=1, source_target_pairs={{0,224},{32,0},{64,32},{96,64},{128,96},{160,128},{192,160},{224,1... | collective-permute-start | bytes 860168 | tf_op jit(solution)/shard_map/ppermute | solution.py:21
  14.1 2.4 %norm_cut.1 = bf16[4,64,1280]{2,1,0:T(8,128)(2,1)} custom-call(bf16[64,5120]{1,0:T(8,128)(2,1)} %h_ref.1, f32[1,5120]{1,0:T(1,128)} %bitcast.27), custom_call_target="tpu_custom_call" | custom-call | tf_op jit(solution)/shard_map/norm_cut/pallas_call | solution.py:137
  16.5 3.5 %all-to-all-start = ((bf16[4,64,1280]{2,1,0:T(8,128)(2,1)}), bf16[4,64,1280]{2,1,0:T(8,128)(2,1)S(1)}, u32[]{:S(2)}, u32[]{:S(2)}) async-start(bf16[4,64,1280]{2,1,0:T(8,128)(2,1)} %norm_cut.1), calls=%async_computation | async-start | bytes 1310720 | tf_op jit(solution)/shard_map/all_to_all | solution.py:400
  21.9 1.9 with_length.1.refs_8_
  23.8 1.6 collective-permute-start.4
  25.4 3.2 %collective-permute-start.6 = (bf16[160,896]{1,0:T(8,128)(2,1)S(1)}, bf16[160,896]{1,0:T(8,128)(2,1)S(1)}, u32[]{:S(2)}, u32[]{:S(2)}) collective-permute-start(bf16[160,896]{1,0:T(8,128)(2,1)S(1)} %collective-permute-done.1.refs_7_), channel_id=1, source_target_pairs={{0,224},{32,0},{64,32},{96,64},{128,96},{160,128},{192,160},{224,1... | collective-permute-start | bytes 860168 | tf_op jit(solution)/shard_map/ppermute | solution.py:21
  28.6 2.2 %all-to-all-done = bf16[4,64,1280]{2,1,0:T(8,128)(2,1)S(1)} async-done(((bf16[4,64,1280]{2,1,0:T(8,128)(2,1)}), bf16[4,64,1280]{2,1,0:T(8,128)(2,1)S(1)}, u32[]{:S(2)}, u32[]{:S(2)}) %all-to-all-start) | async-done | bytes 655392 | tf_op jit(solution)/shard_map/all_to_all | solution.py:400
  30.8 2.9 %collective-permute-done.6.refs_6_ = bf16[160,896]{1,0:T(8,128)(2,1)S(1)} collective-permute-done((bf16[160,896]{1,0:T(8,128)(2,1)S(1)}, bf16[160,896]{1,0:T(8,128)(2,1)S(1)}, u32[]{:S(2)}, u32[]{:S(2)}) %collective-permute-start.6) | collective-permute-done | bytes 286752 | tf_op jit(solution)/shard_map/ppermute | solution.py:21
  33.7 3.7 %collective-permute-start.7 = (bf16[160,896]{1,0:T(8,128)(2,1)S(1)}, bf16[160,896]{1,0:T(8,128)(2,1)}, u32[]{:S(2)}, u32[]{:S(2)}) collective-permute-start(bf16[160,896]{1,0:T(8,128)(2,1)S(1)} %collective-permute-done.6.refs_6_), channel_id=1, source_target_pairs={{0,224},{32,0},{64,32},{96,64},{128,96},{160,128},{192,160},{224,1... | collective-permute-start | bytes 860168 | tf_op jit(solution)/shard_map/ppermute | solution.py:21
  37.4 4.1 %collective-permute-done.4.refs_9_ = bf16[2064,128]{1,0:T(8,128)(2,1)S(1)} collective-permute-done((bf16[2064,128]{1,0:T(8,128)(2,1)}, bf16[2064,128]{1,0:T(8,128)(2,1)S(1)}, u32[]{:S(2)}, u32[]{:S(2)}) %collective-permute-start.4) | collective-permute-done | bytes 528416 | tf_op jit(solution)/shard_map/ppermute | solution.py:21
  42.3 9.1 %collective-permute-done.5.refs_4_ = bf16[160,896]{1,0:T(8,128)(2,1)} collective-permute-done((bf16[160,896]{1,0:T(8,128)(2,1)}, bf16[160,896]{1,0:T(8,128)(2,1)}, u32[]{:S(2)}, u32[]{:S(2)}) %collective-permute-start.5) | collective-permute-done | bytes 286752 | tf_op jit(solution)/shard_map/ppermute | solution.py:21
  51.5 3.7 %project.1 = (f32[2,64,896]{2,1,0:T(8,128)}, f32[2,64,896]{2,1,0:T(8,128)}) custom-call(s32[4]{0:T(128)} %pad_add_fusion.where_ref, bf16[256,1280]{1,0:T(8,128)(2,1)} %bitcast.17, bf16[160,896]{1,0:T(8,128)(2,1)} %side_by_side.1.refs_0_, bf16[160,896]{1,0:T(8,128)(2,1)} %copy-done.11, bf16[160,896]{1,0:T(8,128)(2,1)} %copy-done.13, ...), custom_call_target="tpu_custom_call" | custom-call | tf_op jit(solution)/shard_map/project/pallas_call | solution.py:92
  55.3 2.0 collective-permute-done.8.b_ref
  58.1 2.0 sum_cores.1
  61.4 1.5 collective-permute-start.22
  62.9 4.4 %collective-permute-done.9 = f32[64,640]{1,0:T(8,128)S(1)} collective-permute-done((f32[64,640]{1,0:T(8,128)}, f32[64,640]{1,0:T(8,128)S(1)}, u32[]{:S(2)}, u32[]{:S(2)}) %collective-permute-start.9) | collective-permute-done | bytes 163872 | tf_op jit(solution)/shard_map/ppermute | solution.py:21
  70.3 3.3 %collective-permute-start.14 = (bf16[64,640]{1,0:T(8,128)(2,1)S(1)}, bf16[64,640]{1,0:T(8,128)(2,1)S(1)}, u32[]{:S(2)}, u32[]{:S(2)}) collective-permute-start(bf16[64,640]{1,0:T(8,128)(2,1)S(1)} %multiply_convert_fusion.refs_0_), channel_id=1, source_target_pairs={{0,224},{32,0},{64,32},{96,64},{128,96},{160,128},{192,160},{224,1... | collective-permute-start | bytes 245768 | tf_op jit(solution)/shard_map/ppermute | solution.py:21
  75.4 5.3 %collective-permute-done.19.refs_13_ = bf16[2048,128]{1,0:T(8,128)(2,1)S(1)} collective-permute-done((bf16[2048,128]{1,0:T(8,128)(2,1)S(1)}, bf16[2048,128]{1,0:T(8,128)(2,1)S(1)}, u32[]{:S(2)}, u32[]{:S(2)}) %collective-permute-start.19) | collective-permute-done | bytes 524320 | tf_op jit(solution)/shard_map/ppermute | solution.py:21
  83.4 3.5 %collective-permute-done.15.refs_6_ = bf16[64,640]{1,0:T(8,128)(2,1)S(1)} collective-permute-done((bf16[64,640]{1,0:T(8,128)(2,1)S(1)}, bf16[64,640]{1,0:T(8,128)(2,1)S(1)}, u32[]{:S(2)}, u32[]{:S(2)}) %collective-permute-start.15) | collective-permute-done | bytes 81952 | tf_op jit(solution)/shard_map/ppermute | solution.py:21
  86.9 2.5 %collective-permute-start.16 = (bf16[64,640]{1,0:T(8,128)(2,1)S(1)}, bf16[64,640]{1,0:T(8,128)(2,1)S(1)}, u32[]{:S(2)}, u32[]{:S(2)}) collective-permute-start(bf16[64,640]{1,0:T(8,128)(2,1)S(1)} %collective-permute-done.15.refs_6_), channel_id=1, source_target_pairs={{0,224},{32,0},{64,32},{96,64},{128,96},{160,128},{192,160},{224,1... | collective-permute-start | bytes 245768 | tf_op jit(solution)/shard_map/ppermute | solution.py:21
  90.1 2.3 %collective-permute-done.16.refs_5_ = bf16[64,640]{1,0:T(8,128)(2,1)S(1)} collective-permute-done((bf16[64,640]{1,0:T(8,128)(2,1)S(1)}, bf16[64,640]{1,0:T(8,128)(2,1)S(1)}, u32[]{:S(2)}, u32[]{:S(2)}) %collective-permute-start.16) | collective-permute-done | bytes 81952 | tf_op jit(solution)/shard_map/ppermute | solution.py:21
  92.4 3.3 %collective-permute-done.13.refs_4_ = bf16[64,640]{1,0:T(8,128)(2,1)S(1)} collective-permute-done((bf16[64,640]{1,0:T(8,128)(2,1)S(1)}, bf16[64,640]{1,0:T(8,128)(2,1)S(1)}, u32[]{:S(2)}, u32[]{:S(2)}) %collective-permute-start.13) | collective-permute-done | bytes 81952 | tf_op jit(solution)/shard_map/ppermute | solution.py:21
  96.8 23.1 %attend.1 = bf16[8,8,8,768]{3,2,1,0:T(8,128)(2,1)} custom-call(s32[4]{0:T(128)} %pad_add_fusion.where_ref, bf16[64,640]{1,0:T(8,128)(2,1)} %copy-done.10, bf16[64,640]{1,0:T(8,128)(2,1)} %copy-done.18, bf16[64,640]{1,0:T(8,128)(2,1)} %copy-done.20, bf16[64,640]{1,0:T(8,128)(2,1)} %copy-done.22, bf16[64,640]{1,0:T(8,128)(2,1)} %copy-done.24, ...), custom_call_target="tpu_custom_call" | custom-call | tf_op jit(solution)/shard_map/attend/pallas_call | solution.py:287
  119.9 37.4 %all_to_all.20 = bf16[8,8,8,768]{3,2,1,0:T(8,128)(2,1)} all-to-all(bf16[8,8,8,768]{3,2,1,0:T(8,128)(2,1)} %attend.1), channel_id=1, replica_groups=mesh['z'=8,'y'=2,'c'=2,'head'=8] {'z'}, dimensions={0} | all-to-all | bytes 1572864 | tf_op jit(solution)/shard_map/all_to_all | solution.py:432
  157.3 2.4 %merge.1.refs_0_ = bf16[64,640]{1,0:T(8,128)(2,1)} custom-call(bf16[8,64,768]{2,1,0:T(8,128)(2,1)} %bitcast.16), custom_call_target="tpu_custom_call" | custom-call | tf_op jit(solution)/shard_map/merge/pallas_call | solution.py:324
  160.5 3.8 %collective-permute-done.25.refs_2_ = bf16[64,640]{1,0:T(8,128)(2,1)S(1)} collective-permute-done((bf16[64,640]{1,0:T(8,128)(2,1)}, bf16[64,640]{1,0:T(8,128)(2,1)S(1)}, u32[]{:S(2)}, u32[]{:S(2)}) %collective-permute-start.25) | collective-permute-done | bytes 81952 | tf_op jit(solution)/shard_map/ppermute | solution.py:21
  166.3 3.2 %project_out.1 = bf16[8,32,1280]{2,1,0:T(8,128)(2,1)} custom-call(s32[4]{0:T(128)} %pad_add_fusion.where_ref, bf16[64,640]{1,0:T(8,128)(2,1)} %merge.1.refs_0_, bf16[64,640]{1,0:T(8,128)(2,1)} %copy-done.16, bf16[64,640]{1,0:T(8,128)(2,1)} %copy-done.15, bf16[64,640]{1,0:T(8,128)(2,1)} %copy-done.17, bf16[1280,640]{1,0:T(8,128)(2,1)} %all-gather.2.cloned.1.call-done.refs_4_), custom_call_target="tpu_custom_call" | custom-call | tf_op jit(solution)/shard_map/project_out/pallas_call | solution.py:347
  169.4 19.5 %all_to_all.21.p_ref = bf16[8,32,1280]{2,1,0:T(8,128)(2,1)} all-to-all(bf16[8,32,1280]{2,1,0:T(8,128)(2,1)} %project_out.1), channel_id=1, replica_groups=mesh['z'=8,'y'=2,'c'=2,'head'=8] {'head'}, dimensions={0} | all-to-all | bytes 1310720 | tf_op jit(solution)/shard_map/all_to_all | solution.py:437
  189.0 1.9 sum_heads.1
  190.9 12.3 %all_to_all.22 = bf16[8,32,160]{2,1,0:T(8,128)(2,1)S(1)} all-to-all(bf16[8,32,160]{2,1,0:T(8,128)(2,1)} %sum_heads.1), channel_id=1, replica_groups=mesh['z'=8,'y'=2,'c'=2,'head'=8] {'z'}, dimensions={0} | all-to-all | bytes 163840 | tf_op jit(solution)/shard_map/all_to_all | solution.py:438
  (98 shorter events, 16.0 us)
Async XLA Ops:
  8.2 12.9 %collective-permute-start = (bf16[160,896]{1,0:T(8,128)(2,1)}, bf16[160,896]{1,0:T(8,128)(2,1)S(1)}, u32[]{:S(2)}, u32[]{:S(2)}) collective-permute-start(bf16[160,896]{1,0:T(8,128)(2,1)} %side_by_side.1.refs_0_), channel_id=1, source_target_pairs={{0,32},{32,64},{64,96},{96,128},{128,160},{160,192},{192,224},{224... | collective-permute-start | bytes 860168 | tf_op jit(solution)/shard_map/ppermute | solution.py:21
  10.2 11.0 %collective-permute-start.1 = (bf16[160,896]{1,0:T(8,128)(2,1)}, bf16[160,896]{1,0:T(8,128)(2,1)S(1)}, u32[]{:S(2)}, u32[]{:S(2)}) collective-permute-start(bf16[160,896]{1,0:T(8,128)(2,1)} %side_by_side.1.refs_0_), channel_id=1, source_target_pairs={{0,224},{32,0},{64,32},{96,64},{128,96},{160,128},{192,160},{224,1... | collective-permute-start | bytes 860168 | tf_op jit(solution)/shard_map/ppermute | solution.py:21
  16.5 14.2 %all-to-all-start = ((bf16[4,64,1280]{2,1,0:T(8,128)(2,1)}), bf16[4,64,1280]{2,1,0:T(8,128)(2,1)S(1)}, u32[]{:S(2)}, u32[]{:S(2)}) async-start(bf16[4,64,1280]{2,1,0:T(8,128)(2,1)} %norm_cut.1), calls=%async_computation | async-start | bytes 1310720 | tf_op jit(solution)/shard_map/all_to_all | solution.py:400
  20.0 144.3 %all-gather.2.cloned.1.call-start = ((), (), s32[]{:S(2)}) async-start(), calls=%async_computation.4 | async-start | bytes 1843200 | tf_op jit(solution)/shard_map/all_gather | solution.py:412
  21.1 30.3 %copy-start.11 = (bf16[160,896]{1,0:T(8,128)(2,1)}, bf16[160,896]{1,0:T(8,128)(2,1)S(1)}, u32[]{:S(2)}) copy-start(bf16[160,896]{1,0:T(8,128)(2,1)S(1)} %collective-permute-done.refs_1_) | copy-start | bytes 860164
  21.1 30.3 %copy-start.12 = (bf16[160,896]{1,0:T(8,128)(2,1)}, bf16[160,896]{1,0:T(8,128)(2,1)S(1)}, u32[]{:S(2)}) copy-start(bf16[160,896]{1,0:T(8,128)(2,1)S(1)} %collective-permute-done.1.refs_7_) | copy-start | bytes 860164
  21.1 9.6 %collective-permute-start.2 = (bf16[160,896]{1,0:T(8,128)(2,1)S(1)}, bf16[160,896]{1,0:T(8,128)(2,1)S(1)}, u32[]{:S(2)}, u32[]{:S(2)}) collective-permute-start(bf16[160,896]{1,0:T(8,128)(2,1)S(1)} %collective-permute-done.refs_1_), channel_id=1, source_target_pairs={{0,32},{32,64},{64,96},{96,128},{128,160},{160,192},{192,224},{224... | collective-permute-start | bytes 860168 | tf_op jit(solution)/shard_map/ppermute | solution.py:21
  23.8 17.8 %collective-permute-start.4 = (bf16[2064,128]{1,0:T(8,128)(2,1)}, bf16[2064,128]{1,0:T(8,128)(2,1)S(1)}, u32[]{:S(2)}, u32[]{:S(2)}) collective-permute-start(bf16[2064,128]{1,0:T(8,128)(2,1)} %with_length.1.refs_8_), channel_id=1, source_target_pairs={{0,16},{16,0},{1,17},{17,1},{2,18},{18,2},{3,19},{19,3},{4,20},{20... | collective-permute-start | bytes 1585160 | tf_op jit(solution)/shard_map/ppermute | solution.py:21
  25.4 8.4 %collective-permute-start.6 = (bf16[160,896]{1,0:T(8,128)(2,1)S(1)}, bf16[160,896]{1,0:T(8,128)(2,1)S(1)}, u32[]{:S(2)}, u32[]{:S(2)}) collective-permute-start(bf16[160,896]{1,0:T(8,128)(2,1)S(1)} %collective-permute-done.1.refs_7_), channel_id=1, source_target_pairs={{0,224},{32,0},{64,32},{96,64},{128,96},{160,128},{192,160},{224,1... | collective-permute-start | bytes 860168 | tf_op jit(solution)/shard_map/ppermute | solution.py:21
  30.7 10.8 %collective-permute-start.3 = (bf16[160,896]{1,0:T(8,128)(2,1)S(1)}, bf16[160,896]{1,0:T(8,128)(2,1)}, u32[]{:S(2)}, u32[]{:S(2)}) collective-permute-start(bf16[160,896]{1,0:T(8,128)(2,1)S(1)} %collective-permute-done.2.refs_2_), channel_id=1, source_target_pairs={{0,32},{32,64},{64,96},{96,128},{128,160},{160,192},{192,224},{224... | collective-permute-start | bytes 860168 | tf_op jit(solution)/shard_map/ppermute | solution.py:21
  33.7 8.6 %collective-permute-start.7 = (bf16[160,896]{1,0:T(8,128)(2,1)S(1)}, bf16[160,896]{1,0:T(8,128)(2,1)}, u32[]{:S(2)}, u32[]{:S(2)}) collective-permute-start(bf16[160,896]{1,0:T(8,128)(2,1)S(1)} %collective-permute-done.6.refs_6_), channel_id=1, source_target_pairs={{0,224},{32,0},{64,32},{96,64},{128,96},{160,128},{192,160},{224,1... | collective-permute-start | bytes 860168 | tf_op jit(solution)/shard_map/ppermute | solution.py:21
  41.6 33.2 %copy-start.2 = (bf16[2064,128]{1,0:T(8,128)(2,1)}, bf16[2064,128]{1,0:T(8,128)(2,1)S(1)}, u32[]{:S(2)}) copy-start(bf16[2064,128]{1,0:T(8,128)(2,1)S(1)} %collective-permute-done.4.refs_9_) | copy-start | bytes 1585156
  41.6 9.9 %collective-permute-start.5 = (bf16[160,896]{1,0:T(8,128)(2,1)}, bf16[160,896]{1,0:T(8,128)(2,1)}, u32[]{:S(2)}, u32[]{:S(2)}) collective-permute-start(bf16[160,896]{1,0:T(8,128)(2,1)} %collective-permute-done.3.refs_3_), channel_id=1, source_target_pairs={{0,32},{32,64},{64,96},{96,128},{128,160},{160,192},{192,224},{224... | collective-permute-start | bytes 860168 | tf_op jit(solution)/shard_map/ppermute | solution.py:21
  55.3 2.0 collective-permute-start.8
  60.1 7.3 %collective-permute-start.9 = (f32[64,640]{1,0:T(8,128)}, f32[64,640]{1,0:T(8,128)S(1)}, u32[]{:S(2)}, u32[]{:S(2)}) collective-permute-start(f32[64,640]{1,0:T(8,128)} %get-tuple-element.29), channel_id=1, source_target_pairs={{0,16},{16,0},{1,17},{17,1},{2,18},{18,2},{3,19},{19,3},{4,20},{20... | collective-permute-start | bytes 491528 | tf_op jit(solution)/shard_map/ppermute | solution.py:21
  60.7 14.1 %collective-permute-start.17 = (bf16[2064,128]{1,0:T(8,128)(2,1)S(1)}, bf16[2064,128]{1,0:T(8,128)(2,1)S(1)}, u32[]{:S(2)}, u32[]{:S(2)}) collective-permute-start(bf16[2064,128]{1,0:T(8,128)(2,1)S(1)} %copy-done.1), channel_id=1, source_target_pairs={{0,8},{8,0},{1,9},{9,1},{2,10},{10,2},{3,11},{11,3},{4,12},{12,4},... | collective-permute-start | bytes 1585160 | tf_op jit(solution)/shard_map/ppermute | solution.py:21
  61.4 7.9 %collective-permute-start.22 = (f32[2,64,256]{2,1,0:T(8,128)}, f32[2,64,256]{2,1,0:T(8,128)S(1)}, u32[]{:S(2)}, u32[]{:S(2)}) collective-permute-start(f32[2,64,256]{2,1,0:T(8,128)} %get-tuple-element.33), channel_id=1, source_target_pairs={{0,16},{16,0},{1,17},{17,1},{2,18},{18,2},{3,19},{19,3},{4,20},{20... | collective-permute-start | bytes 393224 | tf_op jit(solution)/shard_map/ppermute | solution.py:21
  68.3 12.4 %collective-permute-start.19 = (bf16[2048,128]{1,0:T(8,128)(2,1)S(1)}, bf16[2048,128]{1,0:T(8,128)(2,1)S(1)}, u32[]{:S(2)}, u32[]{:S(2)}) collective-permute-start(bf16[2048,128]{1,0:T(8,128)(2,1)S(1)} %bitcast.19), channel_id=1, source_target_pairs={{0,16},{16,0},{1,17},{17,1},{2,18},{18,2},{3,19},{19,3},{4,20},{20... | collective-permute-start | bytes 1572872 | tf_op jit(solution)/shard_map/ppermute | solution.py:21
  69.1 5.7 %collective-permute-start.10 = (bf16[64,640]{1,0:T(8,128)(2,1)S(1)}, bf16[64,640]{1,0:T(8,128)(2,1)S(1)}, u32[]{:S(2)}, u32[]{:S(2)}) collective-permute-start(bf16[64,640]{1,0:T(8,128)(2,1)S(1)} %multiply_convert_fusion.refs_0_), channel_id=1, source_target_pairs={{0,32},{32,64},{64,96},{96,128},{128,160},{160,192},{192,224},{224... | collective-permute-start | bytes 245768 | tf_op jit(solution)/shard_map/ppermute | solution.py:21
  70.2 4.7 %collective-permute-start.23 = (bf16[128,256]{1,0:T(8,128)(2,1)S(1)}, bf16[128,256]{1,0:T(8,128)(2,1)S(1)}, u32[]{:S(2)}, u32[]{:S(2)}) collective-permute-start(bf16[128,256]{1,0:T(8,128)(2,1)S(1)} %bitcast.24), channel_id=1, source_target_pairs={{0,8},{8,0},{1,9},{9,1},{2,10},{10,2},{3,11},{11,3},{4,12},{12,4},... | collective-permute-start | bytes 196616 | tf_op jit(solution)/shard_map/ppermute | solution.py:21
  70.3 10.4 %collective-permute-start.14 = (bf16[64,640]{1,0:T(8,128)(2,1)S(1)}, bf16[64,640]{1,0:T(8,128)(2,1)S(1)}, u32[]{:S(2)}, u32[]{:S(2)}) collective-permute-start(bf16[64,640]{1,0:T(8,128)(2,1)S(1)} %multiply_convert_fusion.refs_0_), channel_id=1, source_target_pairs={{0,224},{32,0},{64,32},{96,64},{128,96},{160,128},{192,160},{224,1... | collective-permute-start | bytes 245768 | tf_op jit(solution)/shard_map/ppermute | solution.py:21
  74.8 6.9 %collective-permute-start.11 = (bf16[64,640]{1,0:T(8,128)(2,1)S(1)}, bf16[64,640]{1,0:T(8,128)(2,1)S(1)}, u32[]{:S(2)}, u32[]{:S(2)}) collective-permute-start(bf16[64,640]{1,0:T(8,128)(2,1)S(1)} %collective-permute-done.10.refs_1_), channel_id=1, source_target_pairs={{0,32},{32,64},{64,96},{96,128},{128,160},{160,192},{192,224},{224... | collective-permute-start | bytes 245768 | tf_op jit(solution)/shard_map/ppermute | solution.py:21
  74.8 15.3 %collective-permute-start.18 = (bf16[2064,128]{1,0:T(8,128)(2,1)S(1)}, bf16[2064,128]{1,0:T(8,128)(2,1)S(1)}, u32[]{:S(2)}, u32[]{:S(2)}) collective-permute-start(bf16[2064,128]{1,0:T(8,128)(2,1)S(1)} %collective-permute-done.4.refs_9_), channel_id=1, source_target_pairs={{0,8},{8,0},{1,9},{9,1},{2,10},{10,2},{3,11},{11,3},{4,12},{12,4},... | collective-permute-start | bytes 1585160 | tf_op jit(solution)/shard_map/ppermute | solution.py:21
  74.9 20.8 %collective-permute-start.20 = (bf16[2048,128]{1,0:T(8,128)(2,1)S(1)}, bf16[2048,128]{1,0:T(8,128)(2,1)S(1)}, u32[]{:S(2)}, u32[]{:S(2)}) collective-permute-start(bf16[2048,128]{1,0:T(8,128)(2,1)S(1)} %bitcast.20), channel_id=1, source_target_pairs={{0,8},{8,0},{1,9},{9,1},{2,10},{10,2},{3,11},{11,3},{4,12},{12,4},... | collective-permute-start | bytes 1572872 | tf_op jit(solution)/shard_map/ppermute | solution.py:21
  80.7 15.1 %collective-permute-start.21 = (bf16[2048,128]{1,0:T(8,128)(2,1)S(1)}, bf16[2048,128]{1,0:T(8,128)(2,1)S(1)}, u32[]{:S(2)}, u32[]{:S(2)}) collective-permute-start(bf16[2048,128]{1,0:T(8,128)(2,1)S(1)} %collective-permute-done.19.refs_13_), channel_id=1, source_target_pairs={{0,8},{8,0},{1,9},{9,1},{2,10},{10,2},{3,11},{11,3},{4,12},{12,4},... | collective-permute-start | bytes 1572872 | tf_op jit(solution)/shard_map/ppermute | solution.py:21
  80.7 6.2 %collective-permute-start.15 = (bf16[64,640]{1,0:T(8,128)(2,1)S(1)}, bf16[64,640]{1,0:T(8,128)(2,1)S(1)}, u32[]{:S(2)}, u32[]{:S(2)}) collective-permute-start(bf16[64,640]{1,0:T(8,128)(2,1)S(1)} %collective-permute-done.14.refs_7_), channel_id=1, source_target_pairs={{0,224},{32,0},{64,32},{96,64},{128,96},{160,128},{192,160},{224,1... | collective-permute-start | bytes 245768 | tf_op jit(solution)/shard_map/ppermute | solution.py:21
  81.7 7.8 %collective-permute-start.12 = (bf16[64,640]{1,0:T(8,128)(2,1)S(1)}, bf16[64,640]{1,0:T(8,128)(2,1)S(1)}, u32[]{:S(2)}, u32[]{:S(2)}) collective-permute-start(bf16[64,640]{1,0:T(8,128)(2,1)S(1)} %collective-permute-done.11.refs_2_), channel_id=1, source_target_pairs={{0,32},{32,64},{64,96},{96,128},{128,160},{160,192},{192,224},{224... | collective-permute-start | bytes 245768 | tf_op jit(solution)/shard_map/ppermute | solution.py:21
  86.9 5.5 %collective-permute-start.16 = (bf16[64,640]{1,0:T(8,128)(2,1)S(1)}, bf16[64,640]{1,0:T(8,128)(2,1)S(1)}, u32[]{:S(2)}, u32[]{:S(2)}) collective-permute-start(bf16[64,640]{1,0:T(8,128)(2,1)S(1)} %collective-permute-done.15.refs_6_), channel_id=1, source_target_pairs={{0,224},{32,0},{64,32},{96,64},{128,96},{160,128},{192,160},{224,1... | collective-permute-start | bytes 245768 | tf_op jit(solution)/shard_map/ppermute | solution.py:21
  89.5 6.3 %collective-permute-start.13 = (bf16[64,640]{1,0:T(8,128)(2,1)S(1)}, bf16[64,640]{1,0:T(8,128)(2,1)S(1)}, u32[]{:S(2)}, u32[]{:S(2)}) collective-permute-start(bf16[64,640]{1,0:T(8,128)(2,1)S(1)} %collective-permute-done.12.refs_3_), channel_id=1, source_target_pairs={{0,32},{32,64},{64,96},{96,128},{128,160},{160,192},{192,224},{224... | collective-permute-start | bytes 245768 | tf_op jit(solution)/shard_map/ppermute | solution.py:21
  159.7 4.7 %collective-permute-start.25 = (bf16[64,640]{1,0:T(8,128)(2,1)}, bf16[64,640]{1,0:T(8,128)(2,1)S(1)}, u32[]{:S(2)}, u32[]{:S(2)}) collective-permute-start(bf16[64,640]{1,0:T(8,128)(2,1)} %merge.1.refs_0_), channel_id=1, source_target_pairs={{0,16},{16,0},{1,17},{17,1},{2,18},{18,2},{3,19},{19,3},{4,20},{20... | collective-permute-start | bytes 245768 | tf_op jit(solution)/shard_map/ppermute | solution.py:21
  160.5 3.8 %collective-permute-start.24 = (bf16[64,640]{1,0:T(8,128)(2,1)}, bf16[64,640]{1,0:T(8,128)(2,1)S(1)}, u32[]{:S(2)}, u32[]{:S(2)}) collective-permute-start(bf16[64,640]{1,0:T(8,128)(2,1)} %merge.1.refs_0_), channel_id=1, source_target_pairs={{0,8},{8,0},{1,9},{9,1},{2,10},{10,2},{3,11},{11,3},{4,12},{12,4},... | collective-permute-start | bytes 245768 | tf_op jit(solution)/shard_map/ppermute | solution.py:21
  164.3 1.3 collective-permute-start.26
  (22 other events, 247.7 us)
Sparse Core Ops, SparseCore 0:
  61.5 42.8 all-gather.1

commit v2 on v1

--- a/solution.py
+++ b/solution.py
@@ -401,9 +401,9 @@
     near = with_length(cache_keys[0], cache_len)
 
     weights = side_by_side([w_query, key_projection_weight, value_projection_weight])
-    links = {2: x, 3: shift(near, "y", 1)}
+    links = {2: shift(near, "y", 1), 3: x}
     blocks = ring(weights, "z", links)
-    x, beside = links[2], links[3]
+    beside, x = links[2], links[3]
 
     keys = [near, beside, shift(near, "c", 1), shift(beside, "c", 1)]
 
@@ -411,11 +411,11 @@
     out_cols, keep = lax.optimization_barrier((w_out.T, keep))
     out_cols = lax.all_gather(out_cols, "z", axis=0, tiled=True)
 
-    q_near, q_away, kv = sum_cores(where, keep, shift(send, "c", 1), q_cols)
+    near, _ = lax.optimization_barrier((earlier_values[0], x))
+    beside, came = lax.optimization_barrier((shift(near, "y", 1), shift(send, "c", 1)))
+    values = [near, beside, shift(near, "c", 1), shift(beside, "c", 1)]
+    q_near, q_away, kv = sum_cores(where, keep, came, q_cols)
     queries = (q_near + shift(q_away, "y", 1)).astype(BF)
-    near, queries = lax.optimization_barrier((earlier_values[0], queries))
-    beside = shift(near, "y", 1)
-    values = [near, beside, shift(near, "c", 1), shift(beside, "c", 1)]
     fresh = (kv + shift(kv, "y", 1)).astype(BF).reshape(2 * t, 2 * kv_cols)
     other = shift(fresh, "c", 1)
     new_pairs = [(f[:, :kv_cols], f[:, kv_cols:]) for f in (fresh, other)]

time: 211 us -> 204 us (0.967)
  blocking collectives: 69.2 us -> 58.5 us
  Pallas kernels: 42.3 us -> 48.3 us
  waiting for transfers between devices: 46.7 us -> 41.4 us
  starting transfers between devices: 30.4 us -> 33.7 us
    all_to_all x1, blocking collectives: 37.4 us -> 25.1 us  [per_device(): returned = lax.all_to_all(partial, 'z', 0, 0, tiled=True)]
    pallas_call x1, Pallas kernels: 23.1 us -> 28.9 us  [attend(): pl.pallas_call(kernel, out_shape=jax.ShapeDtypeStruct((n, n, t // n, widt...]
    ppermute x27, starting transfers between devices: 26.9 us -> 30.1 us  [shift(): return lax.ppermute(x, axis, [(i, (i + d) % n) for i in range(n)])]
    ppermute x27, waiting for transfers between devices: 44.5 us -> 41.3 us  [shift(): return lax.ppermute(x, axis, [(i, (i + d) % n) for i in range(n)])]
    all_to_all x1, waiting for transfers between devices: 2.16 us -> 0.01 us  [per_device(): lax.all_to_all(cut, ('y', 'c'), 0, 0, tiled=True).reshape(4 * t, model // 4)]
  transfers between devices with their start and end apart: 29 -> 29, of which waited for: 15 -> 16; matrix products, arithmetic and copies ran while one was open for 2% -> 2% of each run, Pallas kernels for 14% -> 19%
where the time goes in v2:
time: 204 us
  blocking collectives  58.5 us (29%)
  Pallas kernels  48.3 us (24%)
  waiting for transfers between devices  41.4 us (20%)
  starting transfers between devices  33.7 us (17%)
  between operations  15 us (7%)
  local copies, waits for them, and re-layouts  4.25 us (2%)
  other arithmetic  2.58 us (1%)
    ppermute x27, waiting for transfers between devices, shift(): return lax.ppermute(x, axis, [(i, (i + d) % n) for i in range(n)])  41.3 us
    ppermute x27, starting transfers between devices, shift(): return lax.ppermute(x, axis, [(i, (i + d) % n) for i in range(n)])  30.1 us
    pallas_call x1, Pallas kernels, attend(): pl.pallas_call(kernel, out_shape=jax.ShapeDtypeStruct((n, n, t // n, widt...  28.9 us
    all_to_all x1, blocking collectives, per_device(): returned = lax.all_to_all(partial, 'z', 0, 0, tiled=True)  25.1 us
    all_to_all x1, blocking collectives, per_device(): shares = lax.all_to_all(terms, 'head', 0, 0, tiled=True)  21.1 us
    all_to_all x1, blocking collectives, per_device(): final = lax.all_to_all(sum_heads(shares, nz), 'z', 0, 0, tiled=True)  12.3 us
  transfers between devices with their start and end apart: 29, of which 16 were waited for; matrix products, arithmetic and copies ran while one was open for 2% of the time, Pallas kernels for 19%

profile of v2, /device:TPU:2, one launch (start us, length us, event | category | flops | bytes accessed | tf_op | source)
XLA Modules:
  0.0 203.7 jit_solution(1894281413474145700)
XLA Ops:
  6.5 1.7 side_by_side.1.refs_0_
  8.2 1.9 collective-permute-start
  10.1 3.9 %collective-permute-start.1 = (bf16[160,896]{1,0:T(8,128)(2,1)}, bf16[160,896]{1,0:T(8,128)(2,1)S(1)}, u32[]{:S(2)}, u32[]{:S(2)}) collective-permute-start(bf16[160,896]{1,0:T(8,128)(2,1)} %side_by_side.1.refs_0_), channel_id=1, source_target_pairs={{0,224},{32,0},{64,32},{96,64},{128,96},{160,128},{192,160},{224,1... | collective-permute-start | bytes 860168 | tf_op jit(solution)/shard_map/ppermute | solution.py:21
  14.8 1.9 with_length.1.refs_8_
  18.3 2.9 %collective-permute-done.refs_1_ = bf16[160,896]{1,0:T(8,128)(2,1)S(1)} collective-permute-done((bf16[160,896]{1,0:T(8,128)(2,1)}, bf16[160,896]{1,0:T(8,128)(2,1)S(1)}, u32[]{:S(2)}, u32[]{:S(2)}) %collective-permute-start) | collective-permute-done | bytes 286752 | tf_op jit(solution)/shard_map/ppermute | solution.py:21
  21.2 2.6 %norm_cut.1 = bf16[4,64,1280]{2,1,0:T(8,128)(2,1)} custom-call(bf16[64,5120]{1,0:T(8,128)(2,1)} %h_ref.1, f32[1,5120]{1,0:T(1,128)} %bitcast.27), custom_call_target="tpu_custom_call" | custom-call | tf_op jit(solution)/shard_map/norm_cut/pallas_call | solution.py:137
  23.8 3.5 %all-to-all-start = ((bf16[4,64,1280]{2,1,0:T(8,128)(2,1)}), bf16[4,64,1280]{2,1,0:T(8,128)(2,1)S(1)}, u32[]{:S(2)}, u32[]{:S(2)}) async-start(bf16[4,64,1280]{2,1,0:T(8,128)(2,1)} %norm_cut.1), calls=%async_computation | async-start | bytes 1310720 | tf_op jit(solution)/shard_map/all_to_all | solution.py:400
  27.3 3.2 %collective-permute-start.6 = (bf16[160,896]{1,0:T(8,128)(2,1)S(1)}, bf16[160,896]{1,0:T(8,128)(2,1)}, u32[]{:S(2)}, u32[]{:S(2)}) collective-permute-start(bf16[160,896]{1,0:T(8,128)(2,1)S(1)} %collective-permute-done.1.refs_7_), channel_id=1, source_target_pairs={{0,224},{32,0},{64,32},{96,64},{128,96},{160,128},{192,160},{224,1... | collective-permute-start | bytes 860168 | tf_op jit(solution)/shard_map/ppermute | solution.py:21
  30.7 6.7 %collective-permute-done.6.refs_6_ = bf16[160,896]{1,0:T(8,128)(2,1)} collective-permute-done((bf16[160,896]{1,0:T(8,128)(2,1)S(1)}, bf16[160,896]{1,0:T(8,128)(2,1)}, u32[]{:S(2)}, u32[]{:S(2)}) %collective-permute-start.6) | collective-permute-done | bytes 286752 | tf_op jit(solution)/shard_map/ppermute | solution.py:21
  37.4 3.5 %collective-permute-start.7 = (bf16[160,896]{1,0:T(8,128)(2,1)}, bf16[160,896]{1,0:T(8,128)(2,1)}, u32[]{:S(2)}, u32[]{:S(2)}) collective-permute-start(bf16[160,896]{1,0:T(8,128)(2,1)} %collective-permute-done.6.refs_6_), channel_id=1, source_target_pairs={{0,224},{32,0},{64,32},{96,64},{128,96},{160,128},{192,160},{224,1... | collective-permute-start | bytes 860168 | tf_op jit(solution)/shard_map/ppermute | solution.py:21
  41.0 1.8 collective-permute-start.8
  43.4 4.1 %collective-permute-done.7.refs_5_ = bf16[160,896]{1,0:T(8,128)(2,1)} collective-permute-done((bf16[160,896]{1,0:T(8,128)(2,1)}, bf16[160,896]{1,0:T(8,128)(2,1)}, u32[]{:S(2)}, u32[]{:S(2)}) %collective-permute-start.7) | collective-permute-done | bytes 286752 | tf_op jit(solution)/shard_map/ppermute | solution.py:21
  47.5 3.0 %collective-permute-done.5.refs_4_ = bf16[160,896]{1,0:T(8,128)(2,1)} collective-permute-done((bf16[160,896]{1,0:T(8,128)(2,1)}, bf16[160,896]{1,0:T(8,128)(2,1)}, u32[]{:S(2)}, u32[]{:S(2)}) %collective-permute-start.5) | collective-permute-done | bytes 286752 | tf_op jit(solution)/shard_map/ppermute | solution.py:21
  50.5 3.8 %project.1 = (f32[2,64,896]{2,1,0:T(8,128)}, f32[2,64,896]{2,1,0:T(8,128)}) custom-call(s32[4]{0:T(128)} %pad_add_fusion.where_ref, bf16[256,1280]{1,0:T(8,128)(2,1)} %bitcast.17, bf16[160,896]{1,0:T(8,128)(2,1)} %side_by_side.1.refs_0_, bf16[160,896]{1,0:T(8,128)(2,1)} %copy-done.11, bf16[160,896]{1,0:T(8,128)(2,1)} %copy-done.13, ...), custom_call_target="tpu_custom_call" | custom-call | tf_op jit(solution)/shard_map/project/pallas_call | solution.py:92
  54.3 2.0 collective-permute-done.9.b_ref
  57.1 2.0 sum_cores.1
  61.9 4.4 %collective-permute-done.10 = f32[64,640]{1,0:T(8,128)S(1)} collective-permute-done((f32[64,640]{1,0:T(8,128)}, f32[64,640]{1,0:T(8,128)S(1)}, u32[]{:S(2)}, u32[]{:S(2)}) %collective-permute-start.10) | collective-permute-done | bytes 163872 | tf_op jit(solution)/shard_map/ppermute | solution.py:21
  69.3 2.6 %collective-permute-start.15 = (bf16[64,640]{1,0:T(8,128)(2,1)S(1)}, bf16[64,640]{1,0:T(8,128)(2,1)S(1)}, u32[]{:S(2)}, u32[]{:S(2)}) collective-permute-start(bf16[64,640]{1,0:T(8,128)(2,1)S(1)} %multiply_convert_fusion.refs_0_), channel_id=1, source_target_pairs={{0,224},{32,0},{64,32},{96,64},{128,96},{160,128},{192,160},{224,1... | collective-permute-start | bytes 245768 | tf_op jit(solution)/shard_map/ppermute | solution.py:21
  73.7 2.1 %collective-permute-done.15.refs_7_ = bf16[64,640]{1,0:T(8,128)(2,1)S(1)} collective-permute-done((bf16[64,640]{1,0:T(8,128)(2,1)S(1)}, bf16[64,640]{1,0:T(8,128)(2,1)S(1)}, u32[]{:S(2)}, u32[]{:S(2)}) %collective-permute-start.15) | collective-permute-done | bytes 81952 | tf_op jit(solution)/shard_map/ppermute | solution.py:21
  75.8 3.7 %collective-permute-start.16 = (bf16[64,640]{1,0:T(8,128)(2,1)S(1)}, bf16[64,640]{1,0:T(8,128)(2,1)S(1)}, u32[]{:S(2)}, u32[]{:S(2)}) collective-permute-start(bf16[64,640]{1,0:T(8,128)(2,1)S(1)} %collective-permute-done.15.refs_7_), channel_id=1, source_target_pairs={{0,224},{32,0},{64,32},{96,64},{128,96},{160,128},{192,160},{224,1... | collective-permute-start | bytes 245768 | tf_op jit(solution)/shard_map/ppermute | solution.py:21
  80.6 2.5 %collective-permute-done.16.refs_6_ = bf16[64,640]{1,0:T(8,128)(2,1)S(1)} collective-permute-done((bf16[64,640]{1,0:T(8,128)(2,1)S(1)}, bf16[64,640]{1,0:T(8,128)(2,1)S(1)}, u32[]{:S(2)}, u32[]{:S(2)}) %collective-permute-start.16) | collective-permute-done | bytes 81952 | tf_op jit(solution)/shard_map/ppermute | solution.py:21
  83.1 3.7 %collective-permute-start.17 = (bf16[64,640]{1,0:T(8,128)(2,1)S(1)}, bf16[64,640]{1,0:T(8,128)(2,1)S(1)}, u32[]{:S(2)}, u32[]{:S(2)}) collective-permute-start(bf16[64,640]{1,0:T(8,128)(2,1)S(1)} %collective-permute-done.16.refs_6_), channel_id=1, source_target_pairs={{0,224},{32,0},{64,32},{96,64},{128,96},{160,128},{192,160},{224,1... | collective-permute-start | bytes 245768 | tf_op jit(solution)/shard_map/ppermute | solution.py:21
  87.5 2.4 %collective-permute-done.17.refs_5_ = bf16[64,640]{1,0:T(8,128)(2,1)S(1)} collective-permute-done((bf16[64,640]{1,0:T(8,128)(2,1)S(1)}, bf16[64,640]{1,0:T(8,128)(2,1)S(1)}, u32[]{:S(2)}, u32[]{:S(2)}) %collective-permute-start.17) | collective-permute-done | bytes 81952 | tf_op jit(solution)/shard_map/ppermute | solution.py:21
  89.9 3.9 %collective-permute-done.14.refs_4_ = bf16[64,640]{1,0:T(8,128)(2,1)S(1)} collective-permute-done((bf16[64,640]{1,0:T(8,128)(2,1)S(1)}, bf16[64,640]{1,0:T(8,128)(2,1)S(1)}, u32[]{:S(2)}, u32[]{:S(2)}) %collective-permute-start.14) | collective-permute-done | bytes 81952 | tf_op jit(solution)/shard_map/ppermute | solution.py:21
  94.6 28.9 %attend.1 = bf16[8,8,8,768]{3,2,1,0:T(8,128)(2,1)} custom-call(s32[4]{0:T(128)} %pad_add_fusion.where_ref, bf16[64,640]{1,0:T(8,128)(2,1)} %copy-done.10, bf16[64,640]{1,0:T(8,128)(2,1)} %copy-done.17, bf16[64,640]{1,0:T(8,128)(2,1)} %copy-done.19, bf16[64,640]{1,0:T(8,128)(2,1)} %copy-done.21, bf16[64,640]{1,0:T(8,128)(2,1)} %copy-done.23, ...), custom_call_target="tpu_custom_call" | custom-call | tf_op jit(solution)/shard_map/attend/pallas_call | solution.py:287
  123.5 25.1 %all_to_all.20 = bf16[8,8,8,768]{3,2,1,0:T(8,128)(2,1)} all-to-all(bf16[8,8,8,768]{3,2,1,0:T(8,128)(2,1)} %attend.1), channel_id=1, replica_groups=mesh['z'=8,'y'=2,'c'=2,'head'=8] {'z'}, dimensions={0} | all-to-all | bytes 1572864 | tf_op jit(solution)/shard_map/all_to_all | solution.py:432
  148.7 2.4 %merge.1.refs_0_ = bf16[64,640]{1,0:T(8,128)(2,1)} custom-call(bf16[8,64,768]{2,1,0:T(8,128)(2,1)} %bitcast.16), custom_call_target="tpu_custom_call" | custom-call | tf_op jit(solution)/shard_map/merge/pallas_call | solution.py:324
  152.2 3.4 %collective-permute-done.25.refs_2_ = bf16[64,640]{1,0:T(8,128)(2,1)S(1)} collective-permute-done((bf16[64,640]{1,0:T(8,128)(2,1)}, bf16[64,640]{1,0:T(8,128)(2,1)S(1)}, u32[]{:S(2)}, u32[]{:S(2)}) %collective-permute-start.25) | collective-permute-done | bytes 81952 | tf_op jit(solution)/shard_map/ppermute | solution.py:21
  157.6 3.2 %project_out.1 = bf16[8,32,1280]{2,1,0:T(8,128)(2,1)} custom-call(s32[4]{0:T(128)} %pad_add_fusion.where_ref, bf16[64,640]{1,0:T(8,128)(2,1)} %merge.1.refs_0_, bf16[64,640]{1,0:T(8,128)(2,1)} %copy-done.15, bf16[64,640]{1,0:T(8,128)(2,1)} %copy-done.14, bf16[64,640]{1,0:T(8,128)(2,1)} %copy-done.16, bf16[1280,640]{1,0:T(8,128)(2,1)} %all-gather.2.cloned.1.call-done.refs_4_), custom_call_target="tpu_custom_call" | custom-call | tf_op jit(solution)/shard_map/project_out/pallas_call | solution.py:347
  160.8 21.1 %all_to_all.21.p_ref = bf16[8,32,1280]{2,1,0:T(8,128)(2,1)} all-to-all(bf16[8,32,1280]{2,1,0:T(8,128)(2,1)} %project_out.1), channel_id=1, replica_groups=mesh['z'=8,'y'=2,'c'=2,'head'=8] {'head'}, dimensions={0} | all-to-all | bytes 1310720 | tf_op jit(solution)/shard_map/all_to_all | solution.py:437
  181.9 1.9 sum_heads.1
  183.8 12.3 %all_to_all.22 = bf16[8,32,160]{2,1,0:T(8,128)(2,1)S(1)} all-to-all(bf16[8,32,160]{2,1,0:T(8,128)(2,1)} %sum_heads.1), channel_id=1, replica_groups=mesh['z'=8,'y'=2,'c'=2,'head'=8] {'z'}, dimensions={0} | all-to-all | bytes 163840 | tf_op jit(solution)/shard_map/all_to_all | solution.py:438
  (96 shorter events, 16.6 us)
Async XLA Ops:
  8.2 12.9 %collective-permute-start = (bf16[160,896]{1,0:T(8,128)(2,1)}, bf16[160,896]{1,0:T(8,128)(2,1)S(1)}, u32[]{:S(2)}, u32[]{:S(2)}) collective-permute-start(bf16[160,896]{1,0:T(8,128)(2,1)} %side_by_side.1.refs_0_), channel_id=1, source_target_pairs={{0,32},{32,64},{64,96},{96,128},{128,160},{160,192},{192,224},{224... | collective-permute-start | bytes 860168 | tf_op jit(solution)/shard_map/ppermute | solution.py:21
  10.1 11.0 %collective-permute-start.1 = (bf16[160,896]{1,0:T(8,128)(2,1)}, bf16[160,896]{1,0:T(8,128)(2,1)S(1)}, u32[]{:S(2)}, u32[]{:S(2)}) collective-permute-start(bf16[160,896]{1,0:T(8,128)(2,1)} %side_by_side.1.refs_0_), channel_id=1, source_target_pairs={{0,224},{32,0},{64,32},{96,64},{128,96},{160,128},{192,160},{224,1... | collective-permute-start | bytes 860168 | tf_op jit(solution)/shard_map/ppermute | solution.py:21
  16.7 13.9 %collective-permute-start.3 = (bf16[2064,128]{1,0:T(8,128)(2,1)}, bf16[2064,128]{1,0:T(8,128)(2,1)S(1)}, u32[]{:S(2)}, u32[]{:S(2)}) collective-permute-start(bf16[2064,128]{1,0:T(8,128)(2,1)} %with_length.1.refs_8_), channel_id=1, source_target_pairs={{0,16},{16,0},{1,17},{17,1},{2,18},{18,2},{3,19},{19,3},{4,20},{20... | collective-permute-start | bytes 1585160 | tf_op jit(solution)/shard_map/ppermute | solution.py:21
  21.1 29.4 %copy-start.11 = (bf16[160,896]{1,0:T(8,128)(2,1)}, bf16[160,896]{1,0:T(8,128)(2,1)S(1)}, u32[]{:S(2)}) copy-start(bf16[160,896]{1,0:T(8,128)(2,1)S(1)} %collective-permute-done.refs_1_) | copy-start | bytes 860164
  21.1 9.5 %collective-permute-start.2 = (bf16[160,896]{1,0:T(8,128)(2,1)S(1)}, bf16[160,896]{1,0:T(8,128)(2,1)S(1)}, u32[]{:S(2)}, u32[]{:S(2)}) collective-permute-start(bf16[160,896]{1,0:T(8,128)(2,1)S(1)} %collective-permute-done.refs_1_), channel_id=1, source_target_pairs={{0,32},{32,64},{64,96},{96,128},{128,160},{160,192},{192,224},{224... | collective-permute-start | bytes 860168 | tf_op jit(solution)/shard_map/ppermute | solution.py:21
  23.8 17.1 %all-to-all-start = ((bf16[4,64,1280]{2,1,0:T(8,128)(2,1)}), bf16[4,64,1280]{2,1,0:T(8,128)(2,1)S(1)}, u32[]{:S(2)}, u32[]{:S(2)}) async-start(bf16[4,64,1280]{2,1,0:T(8,128)(2,1)} %norm_cut.1), calls=%async_computation | async-start | bytes 1310720 | tf_op jit(solution)/shard_map/all_to_all | solution.py:400
  27.3 129.7 %all-gather.2.cloned.1.call-start = ((), (), s32[]{:S(2)}) async-start(), calls=%async_computation.4 | async-start | bytes 1843200 | tf_op jit(solution)/shard_map/all_gather | solution.py:412
  27.3 10.1 %collective-permute-start.6 = (bf16[160,896]{1,0:T(8,128)(2,1)S(1)}, bf16[160,896]{1,0:T(8,128)(2,1)}, u32[]{:S(2)}, u32[]{:S(2)}) collective-permute-start(bf16[160,896]{1,0:T(8,128)(2,1)S(1)} %collective-permute-done.1.refs_7_), channel_id=1, source_target_pairs={{0,224},{32,0},{64,32},{96,64},{128,96},{160,128},{192,160},{224,1... | collective-permute-start | bytes 860168 | tf_op jit(solution)/shard_map/ppermute | solution.py:21
  30.6 63.1 %copy-start.2 = (bf16[2064,128]{1,0:T(8,128)(2,1)}, bf16[2064,128]{1,0:T(8,128)(2,1)S(1)}, u32[]{:S(2)}) copy-start(bf16[2064,128]{1,0:T(8,128)(2,1)S(1)} %collective-permute-done.3.refs_9_) | copy-start | bytes 1585156
  30.6 10.3 %collective-permute-start.4 = (bf16[160,896]{1,0:T(8,128)(2,1)S(1)}, bf16[160,896]{1,0:T(8,128)(2,1)}, u32[]{:S(2)}, u32[]{:S(2)}) collective-permute-start(bf16[160,896]{1,0:T(8,128)(2,1)S(1)} %collective-permute-done.2.refs_2_), channel_id=1, source_target_pairs={{0,32},{32,64},{64,96},{96,128},{128,160},{160,192},{192,224},{224... | collective-permute-start | bytes 860168 | tf_op jit(solution)/shard_map/ppermute | solution.py:21
  37.4 10.1 %collective-permute-start.7 = (bf16[160,896]{1,0:T(8,128)(2,1)}, bf16[160,896]{1,0:T(8,128)(2,1)}, u32[]{:S(2)}, u32[]{:S(2)}) collective-permute-start(bf16[160,896]{1,0:T(8,128)(2,1)} %collective-permute-done.6.refs_6_), channel_id=1, source_target_pairs={{0,224},{32,0},{64,32},{96,64},{128,96},{160,128},{192,160},{224,1... | collective-permute-start | bytes 860168 | tf_op jit(solution)/shard_map/ppermute | solution.py:21
  40.9 9.6 %collective-permute-start.5 = (bf16[160,896]{1,0:T(8,128)(2,1)}, bf16[160,896]{1,0:T(8,128)(2,1)}, u32[]{:S(2)}, u32[]{:S(2)}) collective-permute-start(bf16[160,896]{1,0:T(8,128)(2,1)} %collective-permute-done.4.refs_3_), channel_id=1, source_target_pairs={{0,32},{32,64},{64,96},{96,128},{128,160},{160,192},{192,224},{224... | collective-permute-start | bytes 860168 | tf_op jit(solution)/shard_map/ppermute | solution.py:21
  41.0 13.3 %collective-permute-start.8 = (bf16[2048,128]{1,0:T(8,128)(2,1)S(1)}, bf16[2048,128]{1,0:T(8,128)(2,1)S(1)}, u32[]{:S(2)}, u32[]{:S(2)}) collective-permute-start(bf16[2048,128]{1,0:T(8,128)(2,1)S(1)} %bitcast.19), channel_id=1, source_target_pairs={{0,16},{16,0},{1,17},{17,1},{2,18},{18,2},{3,19},{19,3},{4,20},{20... | collective-permute-start | bytes 1572872 | tf_op jit(solution)/shard_map/ppermute | solution.py:21
  54.3 2.0 collective-permute-start.9
  54.3 39.5 %copy-start.6 = (bf16[2048,128]{1,0:T(8,128)(2,1)}, bf16[2048,128]{1,0:T(8,128)(2,1)S(1)}, u32[]{:S(2)}) copy-start(bf16[2048,128]{1,0:T(8,128)(2,1)S(1)} %collective-permute-done.8.refs_13_) | copy-start | bytes 1572868
  59.0 7.3 %collective-permute-start.10 = (f32[64,640]{1,0:T(8,128)}, f32[64,640]{1,0:T(8,128)S(1)}, u32[]{:S(2)}, u32[]{:S(2)}) collective-permute-start(f32[64,640]{1,0:T(8,128)} %get-tuple-element.32), channel_id=1, source_target_pairs={{0,16},{16,0},{1,17},{17,1},{2,18},{18,2},{3,19},{19,3},{4,20},{20... | collective-permute-start | bytes 491528 | tf_op jit(solution)/shard_map/ppermute | solution.py:21
  60.5 12.6 %collective-permute-start.18 = (bf16[2064,128]{1,0:T(8,128)(2,1)S(1)}, bf16[2064,128]{1,0:T(8,128)(2,1)S(1)}, u32[]{:S(2)}, u32[]{:S(2)}) collective-permute-start(bf16[2064,128]{1,0:T(8,128)(2,1)S(1)} %copy-done.1), channel_id=1, source_target_pairs={{0,8},{8,0},{1,9},{9,1},{2,10},{10,2},{3,11},{11,3},{4,12},{12,4},... | collective-permute-start | bytes 1585160 | tf_op jit(solution)/shard_map/ppermute | solution.py:21
  61.2 7.1 %collective-permute-start.22 = (f32[2,64,256]{2,1,0:T(8,128)}, f32[2,64,256]{2,1,0:T(8,128)S(1)}, u32[]{:S(2)}, u32[]{:S(2)}) collective-permute-start(f32[2,64,256]{2,1,0:T(8,128)} %get-tuple-element.35), channel_id=1, source_target_pairs={{0,16},{16,0},{1,17},{17,1},{2,18},{18,2},{3,19},{19,3},{4,20},{20... | collective-permute-start | bytes 393224 | tf_op jit(solution)/shard_map/ppermute | solution.py:21
  67.3 5.7 %collective-permute-start.11 = (bf16[64,640]{1,0:T(8,128)(2,1)S(1)}, bf16[64,640]{1,0:T(8,128)(2,1)S(1)}, u32[]{:S(2)}, u32[]{:S(2)}) collective-permute-start(bf16[64,640]{1,0:T(8,128)(2,1)S(1)} %multiply_convert_fusion.refs_0_), channel_id=1, source_target_pairs={{0,32},{32,64},{64,96},{96,128},{128,160},{160,192},{192,224},{224... | collective-permute-start | bytes 245768 | tf_op jit(solution)/shard_map/ppermute | solution.py:21
  69.2 4.4 %collective-permute-start.23 = (bf16[128,256]{1,0:T(8,128)(2,1)S(1)}, bf16[128,256]{1,0:T(8,128)(2,1)S(1)}, u32[]{:S(2)}, u32[]{:S(2)}) collective-permute-start(bf16[128,256]{1,0:T(8,128)(2,1)S(1)} %bitcast.24), channel_id=1, source_target_pairs={{0,8},{8,0},{1,9},{9,1},{2,10},{10,2},{3,11},{11,3},{4,12},{12,4},... | collective-permute-start | bytes 196616 | tf_op jit(solution)/shard_map/ppermute | solution.py:21
  69.3 6.5 %collective-permute-start.15 = (bf16[64,640]{1,0:T(8,128)(2,1)S(1)}, bf16[64,640]{1,0:T(8,128)(2,1)S(1)}, u32[]{:S(2)}, u32[]{:S(2)}) collective-permute-start(bf16[64,640]{1,0:T(8,128)(2,1)S(1)} %multiply_convert_fusion.refs_0_), channel_id=1, source_target_pairs={{0,224},{32,0},{64,32},{96,64},{128,96},{160,128},{192,160},{224,1... | collective-permute-start | bytes 245768 | tf_op jit(solution)/shard_map/ppermute | solution.py:21
  73.1 6.9 %collective-permute-start.12 = (bf16[64,640]{1,0:T(8,128)(2,1)S(1)}, bf16[64,640]{1,0:T(8,128)(2,1)S(1)}, u32[]{:S(2)}, u32[]{:S(2)}) collective-permute-start(bf16[64,640]{1,0:T(8,128)(2,1)S(1)} %collective-permute-done.11.refs_1_), channel_id=1, source_target_pairs={{0,32},{32,64},{64,96},{96,128},{128,160},{160,192},{192,224},{224... | collective-permute-start | bytes 245768 | tf_op jit(solution)/shard_map/ppermute | solution.py:21
  73.1 14.4 %collective-permute-start.19 = (bf16[2064,128]{1,0:T(8,128)(2,1)S(1)}, bf16[2064,128]{1,0:T(8,128)(2,1)S(1)}, u32[]{:S(2)}, u32[]{:S(2)}) collective-permute-start(bf16[2064,128]{1,0:T(8,128)(2,1)S(1)} %collective-permute-done.3.refs_9_), channel_id=1, source_target_pairs={{0,8},{8,0},{1,9},{9,1},{2,10},{10,2},{3,11},{11,3},{4,12},{12,4},... | collective-permute-start | bytes 1585160 | tf_op jit(solution)/shard_map/ppermute | solution.py:21
  73.1 14.4 %collective-permute-start.20 = (bf16[2048,128]{1,0:T(8,128)(2,1)S(1)}, bf16[2048,128]{1,0:T(8,128)(2,1)S(1)}, u32[]{:S(2)}, u32[]{:S(2)}) collective-permute-start(bf16[2048,128]{1,0:T(8,128)(2,1)S(1)} %bitcast.20), channel_id=1, source_target_pairs={{0,8},{8,0},{1,9},{9,1},{2,10},{10,2},{3,11},{11,3},{4,12},{12,4},... | collective-permute-start | bytes 1572872 | tf_op jit(solution)/shard_map/ppermute | solution.py:21
  73.6 20.2 %collective-permute-start.21 = (bf16[2048,128]{1,0:T(8,128)(2,1)S(1)}, bf16[2048,128]{1,0:T(8,128)(2,1)S(1)}, u32[]{:S(2)}, u32[]{:S(2)}) collective-permute-start(bf16[2048,128]{1,0:T(8,128)(2,1)S(1)} %collective-permute-done.8.refs_13_), channel_id=1, source_target_pairs={{0,8},{8,0},{1,9},{9,1},{2,10},{10,2},{3,11},{11,3},{4,12},{12,4},... | collective-permute-start | bytes 1572872 | tf_op jit(solution)/shard_map/ppermute | solution.py:21
  75.8 7.3 %collective-permute-start.16 = (bf16[64,640]{1,0:T(8,128)(2,1)S(1)}, bf16[64,640]{1,0:T(8,128)(2,1)S(1)}, u32[]{:S(2)}, u32[]{:S(2)}) collective-permute-start(bf16[64,640]{1,0:T(8,128)(2,1)S(1)} %collective-permute-done.15.refs_7_), channel_id=1, source_target_pairs={{0,224},{32,0},{64,32},{96,64},{128,96},{160,128},{192,160},{224,1... | collective-permute-start | bytes 245768 | tf_op jit(solution)/shard_map/ppermute | solution.py:21
  79.9 6.9 %collective-permute-start.13 = (bf16[64,640]{1,0:T(8,128)(2,1)S(1)}, bf16[64,640]{1,0:T(8,128)(2,1)S(1)}, u32[]{:S(2)}, u32[]{:S(2)}) collective-permute-start(bf16[64,640]{1,0:T(8,128)(2,1)S(1)} %collective-permute-done.12.refs_2_), channel_id=1, source_target_pairs={{0,32},{32,64},{64,96},{96,128},{128,160},{160,192},{192,224},{224... | collective-permute-start | bytes 245768 | tf_op jit(solution)/shard_map/ppermute | solution.py:21
  83.1 6.8 %collective-permute-start.17 = (bf16[64,640]{1,0:T(8,128)(2,1)S(1)}, bf16[64,640]{1,0:T(8,128)(2,1)S(1)}, u32[]{:S(2)}, u32[]{:S(2)}) collective-permute-start(bf16[64,640]{1,0:T(8,128)(2,1)S(1)} %collective-permute-done.16.refs_6_), channel_id=1, source_target_pairs={{0,224},{32,0},{64,32},{96,64},{128,96},{160,128},{192,160},{224,1... | collective-permute-start | bytes 245768 | tf_op jit(solution)/shard_map/ppermute | solution.py:21
  86.8 6.9 %collective-permute-start.14 = (bf16[64,640]{1,0:T(8,128)(2,1)S(1)}, bf16[64,640]{1,0:T(8,128)(2,1)S(1)}, u32[]{:S(2)}, u32[]{:S(2)}) collective-permute-start(bf16[64,640]{1,0:T(8,128)(2,1)S(1)} %collective-permute-done.13.refs_3_), channel_id=1, source_target_pairs={{0,32},{32,64},{64,96},{96,128},{128,160},{160,192},{192,224},{224... | collective-permute-start | bytes 245768 | tf_op jit(solution)/shard_map/ppermute | solution.py:21
  151.0 4.7 %collective-permute-start.25 = (bf16[64,640]{1,0:T(8,128)(2,1)}, bf16[64,640]{1,0:T(8,128)(2,1)S(1)}, u32[]{:S(2)}, u32[]{:S(2)}) collective-permute-start(bf16[64,640]{1,0:T(8,128)(2,1)} %merge.1.refs_0_), channel_id=1, source_target_pairs={{0,16},{16,0},{1,17},{17,1},{2,18},{18,2},{3,19},{19,3},{4,20},{20... | collective-permute-start | bytes 245768 | tf_op jit(solution)/shard_map/ppermute | solution.py:21
  152.2 3.5 %collective-permute-start.24 = (bf16[64,640]{1,0:T(8,128)(2,1)}, bf16[64,640]{1,0:T(8,128)(2,1)S(1)}, u32[]{:S(2)}, u32[]{:S(2)}) collective-permute-start(bf16[64,640]{1,0:T(8,128)(2,1)} %merge.1.refs_0_), channel_id=1, source_target_pairs={{0,8},{8,0},{1,9},{9,1},{2,10},{10,2},{3,11},{11,3},{4,12},{12,4},... | collective-permute-start | bytes 245768 | tf_op jit(solution)/shard_map/ppermute | solution.py:21
  155.7 1.3 collective-permute-start.26
  (21 other events, 232.5 us)
Sparse Core Ops, SparseCore 0:
  61.3 41.0 all-gather.1

commit v3 on v2

--- a/solution.py
+++ b/solution.py
@@ -30,7 +30,7 @@
         ahead.append(shift(ahead[-1], axis, 1))
         if step < (n - 1) // 2:
             behind.append(shift(behind[-1], axis, -1))
-        if beside and step == 0:
+        if beside and step < (n - 1) // 2:
             ahead[-1], behind[-1] = lax.optimization_barrier((ahead[-1], behind[-1]))
     return ahead + behind[:0:-1]
 
@@ -166,7 +166,7 @@
     )(length, keys)
 
 
-def attend(where, chunks, dists, keys, values, new_pairs):
+def attend(where, chunks, dists, keys, values, fresh_pair):
     n = len(chunks)
     t, width = chunks[0].shape
     each, d = values[0].shape
@@ -174,13 +174,13 @@
     room = ns * each + 2 * KEYS
     g = width // d
     rows = n * g * t
-    fresh = new_pairs[0][0].shape[0]
+    fresh = fresh_pair[0].shape[0]
 
     def kernel(where_ref, *refs):
         q_refs = refs[:n]
         k_in, v_in, refs = refs[n : n + ns], refs[n + ns : n + 2 * ns], refs[n + 2 * ns :]
-        nk0, nv0, nk1, nv1 = refs[:4]
-        out, q_all, m, l, acc, s_a, s_b, token, stats, k_ref, v_ref = refs[4:]
+        fresh_refs = refs[:2]
+        out, q_all, m, l, acc, s_a, s_b, token, stats, k_ref, v_ref = refs[2:]
         top_key = k_in[0][0:1, :]
         at = jnp.int32(0)
         counted = jnp.int32(0)
@@ -259,13 +259,14 @@
         extra = (blocks * KEYS - counted).astype(F32)
         first = nt(k_ref[0:8, :], q_all[...])[0:1]
         l[...] = l[...] - extra * jnp.exp(first - m[...])
-        for part, (nk, nv) in enumerate(((nk0, nv0), (nk1, nv1))):
+        for part, kv_ref in enumerate(fresh_refs):
+            new_keys, new_values = kv_ref[:, :d], kv_ref[:, d:]
             row = lax.broadcasted_iota(jnp.int32, (fresh, 1), 0)
             side = c if part == 0 else 1 - c
             key_token = z * (4 * t) + (row // t) * (2 * t) + side * t + lax.rem(row, t)
             for cs in spans:
-                s = nt(nk[...], q_all[cs, :])
-                absorb(jnp.where(key_token <= token[:, cs], s, NEG), nv[...], cs)
+                s = nt(new_keys, q_all[cs, :])
+                absorb(jnp.where(key_token <= token[:, cs], s, NEG), new_values, cs)
         top = m[...]
         top_hi = top.astype(BF).astype(F32)
         top_lo = (top - top_hi).astype(BF).astype(F32)
@@ -287,7 +288,7 @@
     return pl.pallas_call(
         kernel,
         out_shape=jax.ShapeDtypeStruct((n, n, t // n, width + 128), BF),
-        in_specs=[SM] + [VM] * (n + 2 * ns + 4),
+        in_specs=[SM] + [VM] * (n + 2 * ns + 2),
         out_specs=VM,
         scratch_shapes=[
             pltpu.VMEM((rows, d), BF),
@@ -303,7 +304,7 @@
         ],
         compiler_params=params(),
         name="attend",
-    )(where, *chunks, *keys, *values, *new_pairs[0], *new_pairs[1])
+    )(where, *chunks, *keys, *values, *fresh_pair)
 
 
 def merge(parts, d):
@@ -401,7 +402,7 @@
     near = with_length(cache_keys[0], cache_len)
 
     weights = side_by_side([w_query, key_projection_weight, value_projection_weight])
-    links = {2: shift(near, "y", 1), 3: x}
+    links = {1: cut, 2: shift(near, "y", 1), 3: x}
     blocks = ring(weights, "z", links)
     beside, x = links[2], links[3]
 
@@ -418,7 +419,6 @@
     queries = (q_near + shift(q_away, "y", 1)).astype(BF)
     fresh = (kv + shift(kv, "y", 1)).astype(BF).reshape(2 * t, 2 * kv_cols)
     other = shift(fresh, "c", 1)
-    new_pairs = [(f[:, :kv_cols], f[:, kv_cols:]) for f in (fresh, other)]
 
     token = lax.axis_index(BLK) * t + jnp.arange(t, dtype=jnp.int32)
     positions = stretch_start[0] + token
@@ -428,7 +428,7 @@
     ).astype(BF)
 
     chunks = ring(scaled, "z")
-    partial = attend(where, chunks, list(range(nz)), keys, values, new_pairs)
+    partial = attend(where, chunks, list(range(nz)), keys, values, (fresh, other))
     returned = lax.all_to_all(partial, "z", 0, 0, tiled=True)
     context = merge(returned.reshape(nz, t, -1), d)
     context_y = shift(context, "y", 1)

time: 204 us -> 202 us (level); the launches traced: 204 us -> 198 us
  Pallas kernels: 48.3 us -> 44.6 us
  waiting for transfers between devices: 41.4 us -> 37.8 us
    pallas_call x1, Pallas kernels: 28.9 us -> 25.2 us  [attend(): pl.pallas_call(kernel, out_shape=jax.ShapeDtypeStruct((n, n, t // n, widt...]
    ppermute x27, waiting for transfers between devices: 41.3 us -> 37.8 us  [shift(): return lax.ppermute(x, axis, [(i, (i + d) % n) for i in range(n)])]
  transfers between devices with their start and end apart: 29 -> 29, of which waited for: 16 -> 16; matrix products, arithmetic and copies ran while one was open for 2% -> 1% of each run, Pallas kernels for 19% -> 19%
where the time goes in v3:
time: 202 us; the launch traced here: 198 us
  blocking collectives  58.7 us (29%)
  Pallas kernels  44.6 us (22%)
  waiting for transfers between devices  37.8 us (19%)
  starting transfers between devices  35.5 us (18%)
  between operations  15 us (7%)
  local copies, waits for them, and re-layouts  4.23 us (2%)
  other arithmetic  2.61 us (1%)
    ppermute x27, waiting for transfers between devices, shift(): return lax.ppermute(x, axis, [(i, (i + d) % n) for i in range(n)])  37.8 us
    ppermute x27, starting transfers between devices, shift(): return lax.ppermute(x, axis, [(i, (i + d) % n) for i in range(n)])  31.9 us
    all_to_all x1, blocking collectives, per_device(): returned = lax.all_to_all(partial, 'z', 0, 0, tiled=True)  26.6 us
    pallas_call x1, Pallas kernels, attend(): pl.pallas_call(kernel, out_shape=jax.ShapeDtypeStruct((n, n, t // n, widt...  25.2 us
    all_to_all x1, blocking collectives, per_device(): shares = lax.all_to_all(terms, 'head', 0, 0, tiled=True)  19.8 us
    all_to_all x1, blocking collectives, per_device(): final = lax.all_to_all(sum_heads(shares, nz), 'z', 0, 0, tiled=True)  12.3 us
  transfers between devices with their start and end apart: 29, of which 16 were waited for; matrix products, arithmetic and copies ran while one was open for 1% of the time, Pallas kernels for 19%

profile of v3, /device:TPU:2, one launch (start us, length us, event | category | flops | bytes accessed | tf_op | source)
XLA Modules:
  0.0 198.4 jit_solution(13226129514189595289)
XLA Ops:
  6.5 1.7 side_by_side.1.refs_0_
  8.3 1.9 collective-permute-start
  10.2 3.9 %collective-permute-start.1 = (bf16[160,896]{1,0:T(8,128)(2,1)}, bf16[160,896]{1,0:T(8,128)(2,1)S(1)}, u32[]{:S(2)}, u32[]{:S(2)}) collective-permute-start(bf16[160,896]{1,0:T(8,128)(2,1)} %side_by_side.1.refs_0_), channel_id=1, source_target_pairs={{0,224},{32,0},{64,32},{96,64},{128,96},{160,128},{192,160},{224,1... | collective-permute-start | bytes 860168 | tf_op jit(solution)/shard_map/ppermute | solution.py:21
  14.8 1.9 with_length.1.refs_8_
  16.7 1.6 collective-permute-start.4
  18.3 2.4 %norm_cut.1 = bf16[4,64,1280]{2,1,0:T(8,128)(2,1)} custom-call(bf16[64,5120]{1,0:T(8,128)(2,1)} %h_ref.1, f32[1,5120]{1,0:T(1,128)} %bitcast.27), custom_call_target="tpu_custom_call" | custom-call | tf_op jit(solution)/shard_map/norm_cut/pallas_call | solution.py:137
  21.2 3.2 %collective-permute-start.3 = (bf16[160,896]{1,0:T(8,128)(2,1)S(1)}, bf16[160,896]{1,0:T(8,128)(2,1)S(1)}, u32[]{:S(2)}, u32[]{:S(2)}) collective-permute-start(bf16[160,896]{1,0:T(8,128)(2,1)S(1)} %collective-permute-done.1.refs_7_), channel_id=1, source_target_pairs={{0,224},{32,0},{64,32},{96,64},{128,96},{160,128},{192,160},{224,1... | collective-permute-start | bytes 860168 | tf_op jit(solution)/shard_map/ppermute | solution.py:21
  24.5 3.5 %all-to-all-start = ((bf16[4,64,1280]{2,1,0:T(8,128)(2,1)}), bf16[4,64,1280]{2,1,0:T(8,128)(2,1)S(1)}, u32[]{:S(2)}, u32[]{:S(2)}) async-start(bf16[4,64,1280]{2,1,0:T(8,128)(2,1)} %norm_cut.1), calls=%async_computation | async-start | bytes 1310720 | tf_op jit(solution)/shard_map/all_to_all | solution.py:401
  28.0 2.5 %collective-permute-done.2.refs_2_ = bf16[160,896]{1,0:T(8,128)(2,1)S(1)} collective-permute-done((bf16[160,896]{1,0:T(8,128)(2,1)S(1)}, bf16[160,896]{1,0:T(8,128)(2,1)S(1)}, u32[]{:S(2)}, u32[]{:S(2)}) %collective-permute-start.2) | collective-permute-done | bytes 286752 | tf_op jit(solution)/shard_map/ppermute | solution.py:21
  30.5 1.8 collective-permute-start.5
  33.8 5.2 %collective-permute-done.5.refs_3_ = bf16[160,896]{1,0:T(8,128)(2,1)S(1)} collective-permute-done((bf16[160,896]{1,0:T(8,128)(2,1)S(1)}, bf16[160,896]{1,0:T(8,128)(2,1)S(1)}, u32[]{:S(2)}, u32[]{:S(2)}) %collective-permute-start.5) | collective-permute-done | bytes 286752 | tf_op jit(solution)/shard_map/ppermute | solution.py:21
  40.8 1.6 collective-permute-start.8
  43.0 5.2 %collective-permute-done.7.refs_4_ = bf16[160,896]{1,0:T(8,128)(2,1)} collective-permute-done((bf16[160,896]{1,0:T(8,128)(2,1)}, bf16[160,896]{1,0:T(8,128)(2,1)}, u32[]{:S(2)}, u32[]{:S(2)}) %collective-permute-start.7) | collective-permute-done | bytes 286752 | tf_op jit(solution)/shard_map/ppermute | solution.py:21
  48.2 3.8 %project.1 = (f32[2,64,896]{2,1,0:T(8,128)}, f32[2,64,896]{2,1,0:T(8,128)}) custom-call(s32[4]{0:T(128)} %pad_add_fusion.where_ref, bf16[256,1280]{1,0:T(8,128)(2,1)} %bitcast.17, bf16[160,896]{1,0:T(8,128)(2,1)} %side_by_side.1.refs_0_, bf16[160,896]{1,0:T(8,128)(2,1)} %copy-done.11, bf16[160,896]{1,0:T(8,128)(2,1)} %copy-done.13, ...), custom_call_target="tpu_custom_call" | custom-call | tf_op jit(solution)/shard_map/project/pallas_call | solution.py:92
  52.0 2.0 collective-permute-done.9.b_ref
  54.8 2.0 %sum_cores.1 = (f32[64,640]{1,0:T(8,128)}, f32[64,640]{1,0:T(8,128)}, f32[2,64,256]{2,1,0:T(8,128)}) custom-call(s32[4]{0:T(128)} %pad_add_fusion.where_ref, f32[2,64,896]{2,1,0:T(8,128)} %get-tuple-element.37.a_ref, f32[2,64,896]{2,1,0:T(8,128)} %copy-done.9), custom_call_target="tpu_custom_call" | custom-call | tf_op jit(solution)/shard_map/sum_cores/pallas_call | solution.py:113
  60.1 4.0 %collective-permute-done.10 = f32[64,640]{1,0:T(8,128)S(1)} collective-permute-done((f32[64,640]{1,0:T(8,128)}, f32[64,640]{1,0:T(8,128)S(1)}, u32[]{:S(2)}, u32[]{:S(2)}) %collective-permute-start.10) | collective-permute-done | bytes 163872 | tf_op jit(solution)/shard_map/ppermute | solution.py:21
  66.1 2.9 %collective-permute-start.15 = (bf16[64,640]{1,0:T(8,128)(2,1)S(1)}, bf16[64,640]{1,0:T(8,128)(2,1)S(1)}, u32[]{:S(2)}, u32[]{:S(2)}) collective-permute-start(bf16[64,640]{1,0:T(8,128)(2,1)S(1)} %multiply_convert_fusion.refs_0_), channel_id=1, source_target_pairs={{0,224},{32,0},{64,32},{96,64},{128,96},{160,128},{192,160},{224,1... | collective-permute-start | bytes 245768 | tf_op jit(solution)/shard_map/ppermute | solution.py:21
  68.9 3.1 %collective-permute-done.11.refs_1_ = bf16[64,640]{1,0:T(8,128)(2,1)S(1)} collective-permute-done((bf16[64,640]{1,0:T(8,128)(2,1)S(1)}, bf16[64,640]{1,0:T(8,128)(2,1)S(1)}, u32[]{:S(2)}, u32[]{:S(2)}) %collective-permute-start.11) | collective-permute-done | bytes 81952 | tf_op jit(solution)/shard_map/ppermute | solution.py:21
  72.8 3.7 %collective-permute-start.16 = (bf16[64,640]{1,0:T(8,128)(2,1)S(1)}, bf16[64,640]{1,0:T(8,128)(2,1)S(1)}, u32[]{:S(2)}, u32[]{:S(2)}) collective-permute-start(bf16[64,640]{1,0:T(8,128)(2,1)S(1)} %collective-permute-done.15.refs_7_), channel_id=1, source_target_pairs={{0,224},{32,0},{64,32},{96,64},{128,96},{160,128},{192,160},{224,1... | collective-permute-start | bytes 245768 | tf_op jit(solution)/shard_map/ppermute | solution.py:21
  76.5 2.3 %collective-permute-done.12.refs_2_ = bf16[64,640]{1,0:T(8,128)(2,1)S(1)} collective-permute-done((bf16[64,640]{1,0:T(8,128)(2,1)S(1)}, bf16[64,640]{1,0:T(8,128)(2,1)S(1)}, u32[]{:S(2)}, u32[]{:S(2)}) %collective-permute-start.12) | collective-permute-done | bytes 81952 | tf_op jit(solution)/shard_map/ppermute | solution.py:21
  79.2 3.7 %collective-permute-start.17 = (bf16[64,640]{1,0:T(8,128)(2,1)S(1)}, bf16[64,640]{1,0:T(8,128)(2,1)S(1)}, u32[]{:S(2)}, u32[]{:S(2)}) collective-permute-start(bf16[64,640]{1,0:T(8,128)(2,1)S(1)} %collective-permute-done.16.refs_6_), channel_id=1, source_target_pairs={{0,224},{32,0},{64,32},{96,64},{128,96},{160,128},{192,160},{224,1... | collective-permute-start | bytes 245768 | tf_op jit(solution)/shard_map/ppermute | solution.py:21
  82.9 2.6 %collective-permute-done.13.refs_3_ = bf16[64,640]{1,0:T(8,128)(2,1)S(1)} collective-permute-done((bf16[64,640]{1,0:T(8,128)(2,1)S(1)}, bf16[64,640]{1,0:T(8,128)(2,1)S(1)}, u32[]{:S(2)}, u32[]{:S(2)}) %collective-permute-start.13) | collective-permute-done | bytes 81952 | tf_op jit(solution)/shard_map/ppermute | solution.py:21
  87.8 3.6 %collective-permute-done.14.refs_4_ = bf16[64,640]{1,0:T(8,128)(2,1)S(1)} collective-permute-done((bf16[64,640]{1,0:T(8,128)(2,1)S(1)}, bf16[64,640]{1,0:T(8,128)(2,1)S(1)}, u32[]{:S(2)}, u32[]{:S(2)}) %collective-permute-start.14) | collective-permute-done | bytes 81952 | tf_op jit(solution)/shard_map/ppermute | solution.py:21
  92.8 25.2 %attend.1 = bf16[8,8,8,768]{3,2,1,0:T(8,128)(2,1)} custom-call(s32[4]{0:T(128)} %pad_add_fusion.where_ref, bf16[64,640]{1,0:T(8,128)(2,1)} %copy-done.10, bf16[64,640]{1,0:T(8,128)(2,1)} %copy-done.20, bf16[64,640]{1,0:T(8,128)(2,1)} %copy-done.22, bf16[64,640]{1,0:T(8,128)(2,1)} %copy-done.24, bf16[64,640]{1,0:T(8,128)(2,1)} %copy-done.26, ...), custom_call_target="tpu_custom_call" | custom-call | tf_op jit(solution)/shard_map/attend/pallas_call | solution.py:288
  118.1 26.6 %all_to_all.20 = bf16[8,8,8,768]{3,2,1,0:T(8,128)(2,1)} all-to-all(bf16[8,8,8,768]{3,2,1,0:T(8,128)(2,1)} %attend.1), channel_id=1, replica_groups=mesh['z'=8,'y'=2,'c'=2,'head'=8] {'z'}, dimensions={0} | all-to-all | bytes 1572864 | tf_op jit(solution)/shard_map/all_to_all | solution.py:432
  144.6 2.4 %merge.1.refs_0_ = bf16[64,640]{1,0:T(8,128)(2,1)} custom-call(bf16[8,64,768]{2,1,0:T(8,128)(2,1)} %bitcast.16), custom_call_target="tpu_custom_call" | custom-call | tf_op jit(solution)/shard_map/merge/pallas_call | solution.py:325
  148.4 3.2 %collective-permute-done.25.refs_2_ = bf16[64,640]{1,0:T(8,128)(2,1)S(1)} collective-permute-done((bf16[64,640]{1,0:T(8,128)(2,1)}, bf16[64,640]{1,0:T(8,128)(2,1)S(1)}, u32[]{:S(2)}, u32[]{:S(2)}) %collective-permute-start.25) | collective-permute-done | bytes 81952 | tf_op jit(solution)/shard_map/ppermute | solution.py:21
  153.6 3.2 %project_out.1 = bf16[8,32,1280]{2,1,0:T(8,128)(2,1)} custom-call(s32[4]{0:T(128)} %pad_add_fusion.where_ref, bf16[64,640]{1,0:T(8,128)(2,1)} %merge.1.refs_0_, bf16[64,640]{1,0:T(8,128)(2,1)} %copy-done.18, bf16[64,640]{1,0:T(8,128)(2,1)} %copy-done.17, bf16[64,640]{1,0:T(8,128)(2,1)} %copy-done.19, bf16[1280,640]{1,0:T(8,128)(2,1)} %all-gather.2.cloned.1.call-done.refs_4_), custom_call_target="tpu_custom_call" | custom-call | tf_op jit(solution)/shard_map/project_out/pallas_call | solution.py:348
  156.8 19.8 %all_to_all.21.p_ref = bf16[8,32,1280]{2,1,0:T(8,128)(2,1)} all-to-all(bf16[8,32,1280]{2,1,0:T(8,128)(2,1)} %project_out.1), channel_id=1, replica_groups=mesh['z'=8,'y'=2,'c'=2,'head'=8] {'head'}, dimensions={0} | all-to-all | bytes 1310720 | tf_op jit(solution)/shard_map/all_to_all | solution.py:437
  176.5 1.9 sum_heads.1
  178.4 12.3 %all_to_all.22 = bf16[8,32,160]{2,1,0:T(8,128)(2,1)S(1)} all-to-all(bf16[8,32,160]{2,1,0:T(8,128)(2,1)} %sum_heads.1), channel_id=1, replica_groups=mesh['z'=8,'y'=2,'c'=2,'head'=8] {'z'}, dimensions={0} | all-to-all | bytes 163840 | tf_op jit(solution)/shard_map/all_to_all | solution.py:438
  (102 shorter events, 18.7 us)
Async XLA Ops:
  8.3 12.9 %collective-permute-start = (bf16[160,896]{1,0:T(8,128)(2,1)}, bf16[160,896]{1,0:T(8,128)(2,1)S(1)}, u32[]{:S(2)}, u32[]{:S(2)}) collective-permute-start(bf16[160,896]{1,0:T(8,128)(2,1)} %side_by_side.1.refs_0_), channel_id=1, source_target_pairs={{0,32},{32,64},{64,96},{96,128},{128,160},{160,192},{192,224},{224... | collective-permute-start | bytes 860168 | tf_op jit(solution)/shard_map/ppermute | solution.py:21
  10.2 11.0 %collective-permute-start.1 = (bf16[160,896]{1,0:T(8,128)(2,1)}, bf16[160,896]{1,0:T(8,128)(2,1)S(1)}, u32[]{:S(2)}, u32[]{:S(2)}) collective-permute-start(bf16[160,896]{1,0:T(8,128)(2,1)} %side_by_side.1.refs_0_), channel_id=1, source_target_pairs={{0,224},{32,0},{64,32},{96,64},{128,96},{160,128},{192,160},{224,1... | collective-permute-start | bytes 860168 | tf_op jit(solution)/shard_map/ppermute | solution.py:21
  16.7 13.8 %collective-permute-start.4 = (bf16[2064,128]{1,0:T(8,128)(2,1)}, bf16[2064,128]{1,0:T(8,128)(2,1)S(1)}, u32[]{:S(2)}, u32[]{:S(2)}) collective-permute-start(bf16[2064,128]{1,0:T(8,128)(2,1)} %with_length.1.refs_8_), channel_id=1, source_target_pairs={{0,16},{16,0},{1,17},{17,1},{2,18},{18,2},{3,19},{19,3},{4,20},{20... | collective-permute-start | bytes 1585160 | tf_op jit(solution)/shard_map/ppermute | solution.py:21
  21.2 27.0 %copy-start.11 = (bf16[160,896]{1,0:T(8,128)(2,1)}, bf16[160,896]{1,0:T(8,128)(2,1)S(1)}, u32[]{:S(2)}) copy-start(bf16[160,896]{1,0:T(8,128)(2,1)S(1)} %collective-permute-done.refs_1_) | copy-start | bytes 860164
  21.2 9.3 %collective-permute-start.2 = (bf16[160,896]{1,0:T(8,128)(2,1)S(1)}, bf16[160,896]{1,0:T(8,128)(2,1)S(1)}, u32[]{:S(2)}, u32[]{:S(2)}) collective-permute-start(bf16[160,896]{1,0:T(8,128)(2,1)S(1)} %collective-permute-done.refs_1_), channel_id=1, source_target_pairs={{0,32},{32,64},{64,96},{96,128},{128,160},{160,192},{192,224},{224... | collective-permute-start | bytes 860168 | tf_op jit(solution)/shard_map/ppermute | solution.py:21
  21.2 9.2 %collective-permute-start.3 = (bf16[160,896]{1,0:T(8,128)(2,1)S(1)}, bf16[160,896]{1,0:T(8,128)(2,1)S(1)}, u32[]{:S(2)}, u32[]{:S(2)}) collective-permute-start(bf16[160,896]{1,0:T(8,128)(2,1)S(1)} %collective-permute-done.1.refs_7_), channel_id=1, source_target_pairs={{0,224},{32,0},{64,32},{96,64},{128,96},{160,128},{192,160},{224,1... | collective-permute-start | bytes 860168 | tf_op jit(solution)/shard_map/ppermute | solution.py:21
  24.5 15.2 %all-to-all-start = ((bf16[4,64,1280]{2,1,0:T(8,128)(2,1)}), bf16[4,64,1280]{2,1,0:T(8,128)(2,1)S(1)}, u32[]{:S(2)}, u32[]{:S(2)}) async-start(bf16[4,64,1280]{2,1,0:T(8,128)(2,1)} %norm_cut.1), calls=%async_computation | async-start | bytes 1310720 | tf_op jit(solution)/shard_map/all_to_all | solution.py:401
  28.0 125.0 %all-gather.2.cloned.1.call-start = ((), (), s32[]{:S(2)}) async-start(), calls=%async_computation.4 | async-start | bytes 1843200 | tf_op jit(solution)/shard_map/all_gather | solution.py:413
  30.5 60.9 %copy-start.2 = (bf16[2064,128]{1,0:T(8,128)(2,1)}, bf16[2064,128]{1,0:T(8,128)(2,1)S(1)}, u32[]{:S(2)}) copy-start(bf16[2064,128]{1,0:T(8,128)(2,1)S(1)} %collective-permute-done.4.refs_9_) | copy-start | bytes 1585156
  30.5 8.5 %collective-permute-start.5 = (bf16[160,896]{1,0:T(8,128)(2,1)S(1)}, bf16[160,896]{1,0:T(8,128)(2,1)S(1)}, u32[]{:S(2)}, u32[]{:S(2)}) collective-permute-start(bf16[160,896]{1,0:T(8,128)(2,1)S(1)} %collective-permute-done.2.refs_2_), channel_id=1, source_target_pairs={{0,32},{32,64},{64,96},{96,128},{128,160},{160,192},{192,224},{224... | collective-permute-start | bytes 860168 | tf_op jit(solution)/shard_map/ppermute | solution.py:21
  32.3 7.4 %collective-permute-start.6 = (bf16[160,896]{1,0:T(8,128)(2,1)S(1)}, bf16[160,896]{1,0:T(8,128)(2,1)}, u32[]{:S(2)}, u32[]{:S(2)}) collective-permute-start(bf16[160,896]{1,0:T(8,128)(2,1)S(1)} %collective-permute-done.3.refs_6_), channel_id=1, source_target_pairs={{0,224},{32,0},{64,32},{96,64},{128,96},{160,128},{192,160},{224,1... | collective-permute-start | bytes 860168 | tf_op jit(solution)/shard_map/ppermute | solution.py:21
  39.7 8.5 %collective-permute-start.7 = (bf16[160,896]{1,0:T(8,128)(2,1)}, bf16[160,896]{1,0:T(8,128)(2,1)}, u32[]{:S(2)}, u32[]{:S(2)}) collective-permute-start(bf16[160,896]{1,0:T(8,128)(2,1)} %copy-done.15), channel_id=1, source_target_pairs={{0,32},{32,64},{64,96},{96,128},{128,160},{160,192},{192,224},{224... | collective-permute-start | bytes 860168 | tf_op jit(solution)/shard_map/ppermute | solution.py:21
  40.8 11.2 %collective-permute-start.8 = (bf16[2048,128]{1,0:T(8,128)(2,1)S(1)}, bf16[2048,128]{1,0:T(8,128)(2,1)S(1)}, u32[]{:S(2)}, u32[]{:S(2)}) collective-permute-start(bf16[2048,128]{1,0:T(8,128)(2,1)S(1)} %bitcast.19), channel_id=1, source_target_pairs={{0,16},{16,0},{1,17},{17,1},{2,18},{18,2},{3,19},{19,3},{4,20},{20... | collective-permute-start | bytes 1572872 | tf_op jit(solution)/shard_map/ppermute | solution.py:21
  52.0 2.0 %collective-permute-start.9 = (f32[2,64,896]{2,1,0:T(8,128)}, f32[2,64,896]{2,1,0:T(8,128)S(1)}, u32[]{:S(2)}, u32[]{:S(2)}) collective-permute-start(f32[2,64,896]{2,1,0:T(8,128)} %get-tuple-element.39), channel_id=1, source_target_pairs={{0,8},{8,0},{1,9},{9,1},{2,10},{10,2},{3,11},{11,3},{4,12},{12,4},... | collective-permute-start | bytes 1376264 | tf_op jit(solution)/shard_map/ppermute | solution.py:21
  52.0 39.4 %copy-start.6 = (bf16[2048,128]{1,0:T(8,128)(2,1)}, bf16[2048,128]{1,0:T(8,128)(2,1)S(1)}, u32[]{:S(2)}) copy-start(bf16[2048,128]{1,0:T(8,128)(2,1)S(1)} %collective-permute-done.8.refs_13_) | copy-start | bytes 1572868
  56.8 7.3 %collective-permute-start.10 = (f32[64,640]{1,0:T(8,128)}, f32[64,640]{1,0:T(8,128)S(1)}, u32[]{:S(2)}, u32[]{:S(2)}) collective-permute-start(f32[64,640]{1,0:T(8,128)} %get-tuple-element.42), channel_id=1, source_target_pairs={{0,16},{16,0},{1,17},{17,1},{2,18},{18,2},{3,19},{19,3},{4,20},{20... | collective-permute-start | bytes 491528 | tf_op jit(solution)/shard_map/ppermute | solution.py:21
  58.1 7.3 %collective-permute-start.18 = (bf16[2064,128]{1,0:T(8,128)(2,1)S(1)}, bf16[2064,128]{1,0:T(8,128)(2,1)S(1)}, u32[]{:S(2)}, u32[]{:S(2)}) collective-permute-start(bf16[2064,128]{1,0:T(8,128)(2,1)S(1)} %copy-done.1), channel_id=1, source_target_pairs={{0,8},{8,0},{1,9},{9,1},{2,10},{10,2},{3,11},{11,3},{4,12},{12,4},... | collective-permute-start | bytes 1585160 | tf_op jit(solution)/shard_map/ppermute | solution.py:21
  58.8 27.6 %collective-permute-start.19 = (bf16[2064,128]{1,0:T(8,128)(2,1)S(1)}, bf16[2064,128]{1,0:T(8,128)(2,1)S(1)}, u32[]{:S(2)}, u32[]{:S(2)}) collective-permute-start(bf16[2064,128]{1,0:T(8,128)(2,1)S(1)} %collective-permute-done.4.refs_9_), channel_id=1, source_target_pairs={{0,8},{8,0},{1,9},{9,1},{2,10},{10,2},{3,11},{11,3},{4,12},{12,4},... | collective-permute-start | bytes 1585160 | tf_op jit(solution)/shard_map/ppermute | solution.py:21
  59.4 6.7 %collective-permute-start.22 = (f32[2,64,256]{2,1,0:T(8,128)}, f32[2,64,256]{2,1,0:T(8,128)S(1)}, u32[]{:S(2)}, u32[]{:S(2)}) collective-permute-start(f32[2,64,256]{2,1,0:T(8,128)} %get-tuple-element.45), channel_id=1, source_target_pairs={{0,16},{16,0},{1,17},{17,1},{2,18},{18,2},{3,19},{19,3},{4,20},{20... | collective-permute-start | bytes 393224 | tf_op jit(solution)/shard_map/ppermute | solution.py:21
  65.1 6.9 %collective-permute-start.11 = (bf16[64,640]{1,0:T(8,128)(2,1)S(1)}, bf16[64,640]{1,0:T(8,128)(2,1)S(1)}, u32[]{:S(2)}, u32[]{:S(2)}) collective-permute-start(bf16[64,640]{1,0:T(8,128)(2,1)S(1)} %multiply_convert_fusion.refs_0_), channel_id=1, source_target_pairs={{0,32},{32,64},{64,96},{96,128},{128,160},{160,192},{192,224},{224... | collective-permute-start | bytes 245768 | tf_op jit(solution)/shard_map/ppermute | solution.py:21
  65.2 21.4 %collective-permute-start.20 = (bf16[2048,128]{1,0:T(8,128)(2,1)S(1)}, bf16[2048,128]{1,0:T(8,128)(2,1)S(1)}, u32[]{:S(2)}, u32[]{:S(2)}) collective-permute-start(bf16[2048,128]{1,0:T(8,128)(2,1)S(1)} %bitcast.20), channel_id=1, source_target_pairs={{0,8},{8,0},{1,9},{9,1},{2,10},{10,2},{3,11},{11,3},{4,12},{12,4},... | collective-permute-start | bytes 1572872 | tf_op jit(solution)/shard_map/ppermute | solution.py:21
  65.5 25.9 %collective-permute-start.21 = (bf16[2048,128]{1,0:T(8,128)(2,1)S(1)}, bf16[2048,128]{1,0:T(8,128)(2,1)S(1)}, u32[]{:S(2)}, u32[]{:S(2)}) collective-permute-start(bf16[2048,128]{1,0:T(8,128)(2,1)S(1)} %collective-permute-done.8.refs_13_), channel_id=1, source_target_pairs={{0,8},{8,0},{1,9},{9,1},{2,10},{10,2},{3,11},{11,3},{4,12},{12,4},... | collective-permute-start | bytes 1572872 | tf_op jit(solution)/shard_map/ppermute | solution.py:21
  66.1 6.7 %collective-permute-start.15 = (bf16[64,640]{1,0:T(8,128)(2,1)S(1)}, bf16[64,640]{1,0:T(8,128)(2,1)S(1)}, u32[]{:S(2)}, u32[]{:S(2)}) collective-permute-start(bf16[64,640]{1,0:T(8,128)(2,1)S(1)} %multiply_convert_fusion.refs_0_), channel_id=1, source_target_pairs={{0,224},{32,0},{64,32},{96,64},{128,96},{160,128},{192,160},{224,1... | collective-permute-start | bytes 245768 | tf_op jit(solution)/shard_map/ppermute | solution.py:21
  72.0 6.8 %collective-permute-start.12 = (bf16[64,640]{1,0:T(8,128)(2,1)S(1)}, bf16[64,640]{1,0:T(8,128)(2,1)S(1)}, u32[]{:S(2)}, u32[]{:S(2)}) collective-permute-start(bf16[64,640]{1,0:T(8,128)(2,1)S(1)} %collective-permute-done.11.refs_1_), channel_id=1, source_target_pairs={{0,32},{32,64},{64,96},{96,128},{128,160},{160,192},{192,224},{224... | collective-permute-start | bytes 245768 | tf_op jit(solution)/shard_map/ppermute | solution.py:21
  72.8 6.4 %collective-permute-start.16 = (bf16[64,640]{1,0:T(8,128)(2,1)S(1)}, bf16[64,640]{1,0:T(8,128)(2,1)S(1)}, u32[]{:S(2)}, u32[]{:S(2)}) collective-permute-start(bf16[64,640]{1,0:T(8,128)(2,1)S(1)} %collective-permute-done.15.refs_7_), channel_id=1, source_target_pairs={{0,224},{32,0},{64,32},{96,64},{128,96},{160,128},{192,160},{224,1... | collective-permute-start | bytes 245768 | tf_op jit(solution)/shard_map/ppermute | solution.py:21
  78.8 6.6 %collective-permute-start.13 = (bf16[64,640]{1,0:T(8,128)(2,1)S(1)}, bf16[64,640]{1,0:T(8,128)(2,1)S(1)}, u32[]{:S(2)}, u32[]{:S(2)}) collective-permute-start(bf16[64,640]{1,0:T(8,128)(2,1)S(1)} %collective-permute-done.12.refs_2_), channel_id=1, source_target_pairs={{0,32},{32,64},{64,96},{96,128},{128,160},{160,192},{192,224},{224... | collective-permute-start | bytes 245768 | tf_op jit(solution)/shard_map/ppermute | solution.py:21
  79.2 8.7 %collective-permute-start.17 = (bf16[64,640]{1,0:T(8,128)(2,1)S(1)}, bf16[64,640]{1,0:T(8,128)(2,1)S(1)}, u32[]{:S(2)}, u32[]{:S(2)}) collective-permute-start(bf16[64,640]{1,0:T(8,128)(2,1)S(1)} %collective-permute-done.16.refs_6_), channel_id=1, source_target_pairs={{0,224},{32,0},{64,32},{96,64},{128,96},{160,128},{192,160},{224,1... | collective-permute-start | bytes 245768 | tf_op jit(solution)/shard_map/ppermute | solution.py:21
  85.5 5.9 %collective-permute-start.14 = (bf16[64,640]{1,0:T(8,128)(2,1)S(1)}, bf16[64,640]{1,0:T(8,128)(2,1)S(1)}, u32[]{:S(2)}, u32[]{:S(2)}) collective-permute-start(bf16[64,640]{1,0:T(8,128)(2,1)S(1)} %collective-permute-done.13.refs_3_), channel_id=1, source_target_pairs={{0,32},{32,64},{64,96},{96,128},{128,160},{160,192},{192,224},{224... | collective-permute-start | bytes 245768 | tf_op jit(solution)/shard_map/ppermute | solution.py:21
  86.5 1.3 collective-permute-start.23
  147.0 4.7 %collective-permute-start.25 = (bf16[64,640]{1,0:T(8,128)(2,1)}, bf16[64,640]{1,0:T(8,128)(2,1)S(1)}, u32[]{:S(2)}, u32[]{:S(2)}) collective-permute-start(bf16[64,640]{1,0:T(8,128)(2,1)} %merge.1.refs_0_), channel_id=1, source_target_pairs={{0,16},{16,0},{1,17},{17,1},{2,18},{18,2},{3,19},{19,3},{4,20},{20... | collective-permute-start | bytes 245768 | tf_op jit(solution)/shard_map/ppermute | solution.py:21
  148.4 3.3 %collective-permute-start.24 = (bf16[64,640]{1,0:T(8,128)(2,1)}, bf16[64,640]{1,0:T(8,128)(2,1)S(1)}, u32[]{:S(2)}, u32[]{:S(2)}) collective-permute-start(bf16[64,640]{1,0:T(8,128)(2,1)} %merge.1.refs_0_), channel_id=1, source_target_pairs={{0,8},{8,0},{1,9},{9,1},{2,10},{10,2},{3,11},{11,3},{4,12},{12,4},... | collective-permute-start | bytes 245768 | tf_op jit(solution)/shard_map/ppermute | solution.py:21
  151.7 1.3 collective-permute-start.26
  (25 other events, 248.8 us)
Sparse Core Ops, SparseCore 0:
  52.1 41.7 all-gather.1

commit v4 on v3

--- a/solution.py
+++ b/solution.py
@@ -427,7 +427,7 @@
         lax.optimization_barrier(queries).astype(F32) * (temper * d ** (-0.5))[:, None]
     ).astype(BF)
 
-    chunks = ring(scaled, "z")
+    chunks = ring(scaled, "z", {nz: scaled})
     partial = attend(where, chunks, list(range(nz)), keys, values, (fresh, other))
     returned = lax.all_to_all(partial, "z", 0, 0, tiled=True)
     context = merge(returned.reshape(nz, t, -1), d)

time: 202 us -> 213 us (1.054); the launches traced: 198 us -> 214 us
  waiting for transfers between devices: 37.8 us -> 45.4 us
  blocking collectives: 58.7 us -> 65.7 us
    ppermute x27, waiting for transfers between devices: 37.8 us -> 45.3 us  [shift(): return lax.ppermute(x, axis, [(i, (i + d) % n) for i in range(n)])]
    all_to_all x1, blocking collectives: 26.6 us -> 33.7 us  [per_device(): returned = lax.all_to_all(partial, 'z', 0, 0, tiled=True)]
  transfers between devices with their start and end apart: 29 -> 29, of which waited for: 16 -> 15; matrix products, arithmetic and copies ran while one was open for 1% -> 1% of each run, Pallas kernels for 19% -> 17%
where the time goes in v4:
time: 213 us; the launch traced here: 214 us
  blocking collectives  65.7 us (31%)
  waiting for transfers between devices  45.4 us (21%)
  Pallas kernels  44.5 us (21%)
  starting transfers between devices  36.7 us (17%)
  between operations  15 us (7%)
  local copies, waits for them, and re-layouts  4.23 us (2%)
  other arithmetic  2.57 us (1%)
    ppermute x27, waiting for transfers between devices, shift(): return lax.ppermute(x, axis, [(i, (i + d) % n) for i in range(n)])  45.3 us
    all_to_all x1, blocking collectives, per_device(): returned = lax.all_to_all(partial, 'z', 0, 0, tiled=True)  33.7 us
    ppermute x27, starting transfers between devices, shift(): return lax.ppermute(x, axis, [(i, (i + d) % n) for i in range(n)])  33.2 us
    pallas_call x1, Pallas kernels, attend(): pl.pallas_call(kernel, out_shape=jax.ShapeDtypeStruct((n, n, t // n, widt...  25.2 us
    all_to_all x1, blocking collectives, per_device(): shares = lax.all_to_all(terms, 'head', 0, 0, tiled=True)  19.7 us
    all_to_all x1, blocking collectives, per_device(): final = lax.all_to_all(sum_heads(shares, nz), 'z', 0, 0, tiled=True)  12.3 us
  transfers between devices with their start and end apart: 29, of which 15 were waited for; matrix products, arithmetic and copies ran while one was open for 1% of the time, Pallas kernels for 17%

profile of v4, /device:TPU:2, one launch (start us, length us, event | category | flops | bytes accessed | tf_op | source)
XLA Modules:
  0.0 214.1 jit_solution(17891451075232492062)
XLA Ops:
  6.5 1.7 side_by_side.1.refs_0_
  8.2 1.9 collective-permute-start
  10.1 3.9 %collective-permute-start.1 = (bf16[160,896]{1,0:T(8,128)(2,1)}, bf16[160,896]{1,0:T(8,128)(2,1)S(1)}, u32[]{:S(2)}, u32[]{:S(2)}) collective-permute-start(bf16[160,896]{1,0:T(8,128)(2,1)} %side_by_side.1.refs_0_), channel_id=1, source_target_pairs={{0,224},{32,0},{64,32},{96,64},{128,96},{160,128},{192,160},{224,1... | collective-permute-start | bytes 860168 | tf_op jit(solution)/shard_map/ppermute | solution.py:21
  14.7 1.9 with_length.1.refs_8_
  18.2 2.4 %norm_cut.1 = bf16[4,64,1280]{2,1,0:T(8,128)(2,1)} custom-call(bf16[64,5120]{1,0:T(8,128)(2,1)} %h_ref.1, f32[1,5120]{1,0:T(1,128)} %bitcast.27), custom_call_target="tpu_custom_call" | custom-call | tf_op jit(solution)/shard_map/norm_cut/pallas_call | solution.py:137
  21.2 3.2 %collective-permute-start.3 = (bf16[160,896]{1,0:T(8,128)(2,1)S(1)}, bf16[160,896]{1,0:T(8,128)(2,1)S(1)}, u32[]{:S(2)}, u32[]{:S(2)}) collective-permute-start(bf16[160,896]{1,0:T(8,128)(2,1)S(1)} %collective-permute-done.1.refs_7_), channel_id=1, source_target_pairs={{0,224},{32,0},{64,32},{96,64},{128,96},{160,128},{192,160},{224,1... | collective-permute-start | bytes 860168 | tf_op jit(solution)/shard_map/ppermute | solution.py:21
  24.4 3.5 %all-to-all-start = ((bf16[4,64,1280]{2,1,0:T(8,128)(2,1)}), bf16[4,64,1280]{2,1,0:T(8,128)(2,1)S(1)}, u32[]{:S(2)}, u32[]{:S(2)}) async-start(bf16[4,64,1280]{2,1,0:T(8,128)(2,1)} %norm_cut.1), calls=%async_computation | async-start | bytes 1310720 | tf_op jit(solution)/shard_map/all_to_all | solution.py:401
  28.0 2.5 %collective-permute-done.2.refs_2_ = bf16[160,896]{1,0:T(8,128)(2,1)S(1)} collective-permute-done((bf16[160,896]{1,0:T(8,128)(2,1)S(1)}, bf16[160,896]{1,0:T(8,128)(2,1)S(1)}, u32[]{:S(2)}, u32[]{:S(2)}) %collective-permute-start.2) | collective-permute-done | bytes 286752 | tf_op jit(solution)/shard_map/ppermute | solution.py:21
  30.4 1.8 collective-permute-start.5
  33.8 5.2 %collective-permute-done.5.refs_3_ = bf16[160,896]{1,0:T(8,128)(2,1)S(1)} collective-permute-done((bf16[160,896]{1,0:T(8,128)(2,1)S(1)}, bf16[160,896]{1,0:T(8,128)(2,1)S(1)}, u32[]{:S(2)}, u32[]{:S(2)}) %collective-permute-start.5) | collective-permute-done | bytes 286752 | tf_op jit(solution)/shard_map/ppermute | solution.py:21
  42.9 5.2 %collective-permute-done.7.refs_4_ = bf16[160,896]{1,0:T(8,128)(2,1)} collective-permute-done((bf16[160,896]{1,0:T(8,128)(2,1)}, bf16[160,896]{1,0:T(8,128)(2,1)}, u32[]{:S(2)}, u32[]{:S(2)}) %collective-permute-start.7) | collective-permute-done | bytes 286752 | tf_op jit(solution)/shard_map/ppermute | solution.py:21
  48.2 3.8 %project.1 = (f32[2,64,896]{2,1,0:T(8,128)}, f32[2,64,896]{2,1,0:T(8,128)}) custom-call(s32[4]{0:T(128)} %pad_add_fusion.where_ref, bf16[256,1280]{1,0:T(8,128)(2,1)} %bitcast.17, bf16[160,896]{1,0:T(8,128)(2,1)} %side_by_side.1.refs_0_, bf16[160,896]{1,0:T(8,128)(2,1)} %copy-done.11, bf16[160,896]{1,0:T(8,128)(2,1)} %copy-done.13, ...), custom_call_target="tpu_custom_call" | custom-call | tf_op jit(solution)/shard_map/project/pallas_call | solution.py:92
  51.9 2.0 collective-permute-done.9.b_ref
  54.7 2.0 sum_cores.1
  58.8 4.4 %collective-permute-done.10 = f32[64,640]{1,0:T(8,128)S(1)} collective-permute-done((f32[64,640]{1,0:T(8,128)}, f32[64,640]{1,0:T(8,128)S(1)}, u32[]{:S(2)}, u32[]{:S(2)}) %collective-permute-start.10) | collective-permute-done | bytes 163872 | tf_op jit(solution)/shard_map/ppermute | solution.py:21
  64.3 3.2 %collective-permute-start.12 = (bf16[64,640]{1,0:T(8,128)(2,1)S(1)}, bf16[64,640]{1,0:T(8,128)(2,1)S(1)}, u32[]{:S(2)}, u32[]{:S(2)}) collective-permute-start(bf16[64,640]{1,0:T(8,128)(2,1)S(1)} %multiply_convert_fusion.refs_0_), channel_id=1, source_target_pairs={{0,224},{32,0},{64,32},{96,64},{128,96},{160,128},{192,160},{224,1... | collective-permute-start | bytes 245768 | tf_op jit(solution)/shard_map/ppermute | solution.py:21
  67.5 2.4 %collective-permute-done.11.refs_1_ = bf16[64,640]{1,0:T(8,128)(2,1)S(1)} collective-permute-done((bf16[64,640]{1,0:T(8,128)(2,1)S(1)}, bf16[64,640]{1,0:T(8,128)(2,1)S(1)}, u32[]{:S(2)}, u32[]{:S(2)}) %collective-permute-start.11) | collective-permute-done | bytes 81952 | tf_op jit(solution)/shard_map/ppermute | solution.py:21
  70.2 3.1 %collective-permute-start.14 = (bf16[64,640]{1,0:T(8,128)(2,1)S(1)}, bf16[64,640]{1,0:T(8,128)(2,1)S(1)}, u32[]{:S(2)}, u32[]{:S(2)}) collective-permute-start(bf16[64,640]{1,0:T(8,128)(2,1)S(1)} %collective-permute-done.12.refs_7_), channel_id=1, source_target_pairs={{0,224},{32,0},{64,32},{96,64},{128,96},{160,128},{192,160},{224,1... | collective-permute-start | bytes 245768 | tf_op jit(solution)/shard_map/ppermute | solution.py:21
  73.2 3.3 %collective-permute-done.13.refs_2_ = bf16[64,640]{1,0:T(8,128)(2,1)S(1)} collective-permute-done((bf16[64,640]{1,0:T(8,128)(2,1)S(1)}, bf16[64,640]{1,0:T(8,128)(2,1)S(1)}, u32[]{:S(2)}, u32[]{:S(2)}) %collective-permute-start.13) | collective-permute-done | bytes 81952 | tf_op jit(solution)/shard_map/ppermute | solution.py:21
  76.5 3.0 %collective-permute-start.15 = (bf16[64,640]{1,0:T(8,128)(2,1)S(1)}, bf16[64,640]{1,0:T(8,128)(2,1)S(1)}, u32[]{:S(2)}, u32[]{:S(2)}) collective-permute-start(bf16[64,640]{1,0:T(8,128)(2,1)S(1)} %collective-permute-done.13.refs_2_), channel_id=1, source_target_pairs={{0,32},{32,64},{64,96},{96,128},{128,160},{160,192},{192,224},{224... | collective-permute-start | bytes 245768 | tf_op jit(solution)/shard_map/ppermute | solution.py:21
  80.1 3.6 %collective-permute-done.15.refs_3_ = bf16[64,640]{1,0:T(8,128)(2,1)S(1)} collective-permute-done((bf16[64,640]{1,0:T(8,128)(2,1)S(1)}, bf16[64,640]{1,0:T(8,128)(2,1)S(1)}, u32[]{:S(2)}, u32[]{:S(2)}) %collective-permute-start.15) | collective-permute-done | bytes 81952 | tf_op jit(solution)/shard_map/ppermute | solution.py:21
  85.2 4.1 %collective-permute-done.16.refs_5_ = bf16[64,640]{1,0:T(8,128)(2,1)S(1)} collective-permute-done((bf16[64,640]{1,0:T(8,128)(2,1)S(1)}, bf16[64,640]{1,0:T(8,128)(2,1)S(1)}, u32[]{:S(2)}, u32[]{:S(2)}) %collective-permute-start.16) | collective-permute-done | bytes 81952 | tf_op jit(solution)/shard_map/ppermute | solution.py:21
  90.7 3.7 %collective-permute-done.22 = f32[2,64,256]{2,1,0:T(8,128)S(1)} collective-permute-done((f32[2,64,256]{2,1,0:T(8,128)}, f32[2,64,256]{2,1,0:T(8,128)S(1)}, u32[]{:S(2)}, u32[]{:S(2)}) %collective-permute-start.22) | collective-permute-done | bytes 131104 | tf_op jit(solution)/shard_map/ppermute | solution.py:21
  97.7 2.4 %collective-permute-done.17.refs_4_ = bf16[64,640]{1,0:T(8,128)(2,1)S(1)} collective-permute-done((bf16[64,640]{1,0:T(8,128)(2,1)S(1)}, bf16[64,640]{1,0:T(8,128)(2,1)S(1)}, u32[]{:S(2)}, u32[]{:S(2)}) %collective-permute-start.17) | collective-permute-done | bytes 81952 | tf_op jit(solution)/shard_map/ppermute | solution.py:21
  101.5 25.2 %attend.1 = bf16[8,8,8,768]{3,2,1,0:T(8,128)(2,1)} custom-call(s32[4]{0:T(128)} %pad_add_fusion.where_ref, bf16[64,640]{1,0:T(8,128)(2,1)} %copy-done.10, bf16[64,640]{1,0:T(8,128)(2,1)} %copy-done.20, bf16[64,640]{1,0:T(8,128)(2,1)} %copy-done.22, bf16[64,640]{1,0:T(8,128)(2,1)} %copy-done.24, bf16[64,640]{1,0:T(8,128)(2,1)} %copy-done.26, ...), custom_call_target="tpu_custom_call" | custom-call | tf_op jit(solution)/shard_map/attend/pallas_call | solution.py:288
  126.8 33.7 %all_to_all.20 = bf16[8,8,8,768]{3,2,1,0:T(8,128)(2,1)} all-to-all(bf16[8,8,8,768]{3,2,1,0:T(8,128)(2,1)} %attend.1), channel_id=1, replica_groups=mesh['z'=8,'y'=2,'c'=2,'head'=8] {'z'}, dimensions={0} | all-to-all | bytes 1572864 | tf_op jit(solution)/shard_map/all_to_all | solution.py:432
  160.4 2.4 %merge.1.refs_0_ = bf16[64,640]{1,0:T(8,128)(2,1)} custom-call(bf16[8,64,768]{2,1,0:T(8,128)(2,1)} %bitcast.16), custom_call_target="tpu_custom_call" | custom-call | tf_op jit(solution)/shard_map/merge/pallas_call | solution.py:325
  163.8 3.6 %collective-permute-done.25.refs_2_ = bf16[64,640]{1,0:T(8,128)(2,1)S(1)} collective-permute-done((bf16[64,640]{1,0:T(8,128)(2,1)}, bf16[64,640]{1,0:T(8,128)(2,1)S(1)}, u32[]{:S(2)}, u32[]{:S(2)}) %collective-permute-start.25) | collective-permute-done | bytes 81952 | tf_op jit(solution)/shard_map/ppermute | solution.py:21
  169.4 3.2 %project_out.1 = bf16[8,32,1280]{2,1,0:T(8,128)(2,1)} custom-call(s32[4]{0:T(128)} %pad_add_fusion.where_ref, bf16[64,640]{1,0:T(8,128)(2,1)} %merge.1.refs_0_, bf16[64,640]{1,0:T(8,128)(2,1)} %copy-done.18, bf16[64,640]{1,0:T(8,128)(2,1)} %copy-done.17, bf16[64,640]{1,0:T(8,128)(2,1)} %copy-done.19, bf16[1280,640]{1,0:T(8,128)(2,1)} %all-gather.2.cloned.1.call-done.refs_4_), custom_call_target="tpu_custom_call" | custom-call | tf_op jit(solution)/shard_map/project_out/pallas_call | solution.py:348
  172.6 19.7 %all_to_all.21.p_ref = bf16[8,32,1280]{2,1,0:T(8,128)(2,1)} all-to-all(bf16[8,32,1280]{2,1,0:T(8,128)(2,1)} %project_out.1), channel_id=1, replica_groups=mesh['z'=8,'y'=2,'c'=2,'head'=8] {'head'}, dimensions={0} | all-to-all | bytes 1310720 | tf_op jit(solution)/shard_map/all_to_all | solution.py:437
  192.3 1.9 sum_heads.1
  194.2 12.3 %all_to_all.22 = bf16[8,32,160]{2,1,0:T(8,128)(2,1)S(1)} all-to-all(bf16[8,32,160]{2,1,0:T(8,128)(2,1)} %sum_heads.1), channel_id=1, replica_groups=mesh['z'=8,'y'=2,'c'=2,'head'=8] {'z'}, dimensions={0} | all-to-all | bytes 163840 | tf_op jit(solution)/shard_map/all_to_all | solution.py:438
  (102 shorter events, 22.8 us)
Async XLA Ops:
  8.2 12.9 %collective-permute-start = (bf16[160,896]{1,0:T(8,128)(2,1)}, bf16[160,896]{1,0:T(8,128)(2,1)S(1)}, u32[]{:S(2)}, u32[]{:S(2)}) collective-permute-start(bf16[160,896]{1,0:T(8,128)(2,1)} %side_by_side.1.refs_0_), channel_id=1, source_target_pairs={{0,32},{32,64},{64,96},{96,128},{128,160},{160,192},{192,224},{224... | collective-permute-start | bytes 860168 | tf_op jit(solution)/shard_map/ppermute | solution.py:21
  10.1 11.0 %collective-permute-start.1 = (bf16[160,896]{1,0:T(8,128)(2,1)}, bf16[160,896]{1,0:T(8,128)(2,1)S(1)}, u32[]{:S(2)}, u32[]{:S(2)}) collective-permute-start(bf16[160,896]{1,0:T(8,128)(2,1)} %side_by_side.1.refs_0_), channel_id=1, source_target_pairs={{0,224},{32,0},{64,32},{96,64},{128,96},{160,128},{192,160},{224,1... | collective-permute-start | bytes 860168 | tf_op jit(solution)/shard_map/ppermute | solution.py:21
  16.7 13.8 %collective-permute-start.4 = (bf16[2064,128]{1,0:T(8,128)(2,1)}, bf16[2064,128]{1,0:T(8,128)(2,1)S(1)}, u32[]{:S(2)}, u32[]{:S(2)}) collective-permute-start(bf16[2064,128]{1,0:T(8,128)(2,1)} %with_length.1.refs_8_), channel_id=1, source_target_pairs={{0,16},{16,0},{1,17},{17,1},{2,18},{18,2},{3,19},{19,3},{4,20},{20... | collective-permute-start | bytes 1585160 | tf_op jit(solution)/shard_map/ppermute | solution.py:21
  21.1 9.3 %collective-permute-start.2 = (bf16[160,896]{1,0:T(8,128)(2,1)S(1)}, bf16[160,896]{1,0:T(8,128)(2,1)S(1)}, u32[]{:S(2)}, u32[]{:S(2)}) collective-permute-start(bf16[160,896]{1,0:T(8,128)(2,1)S(1)} %collective-permute-done.refs_1_), channel_id=1, source_target_pairs={{0,32},{32,64},{64,96},{96,128},{128,160},{160,192},{192,224},{224... | collective-permute-start | bytes 860168 | tf_op jit(solution)/shard_map/ppermute | solution.py:21
  21.2 9.2 %collective-permute-start.3 = (bf16[160,896]{1,0:T(8,128)(2,1)S(1)}, bf16[160,896]{1,0:T(8,128)(2,1)S(1)}, u32[]{:S(2)}, u32[]{:S(2)}) collective-permute-start(bf16[160,896]{1,0:T(8,128)(2,1)S(1)} %collective-permute-done.1.refs_7_), channel_id=1, source_target_pairs={{0,224},{32,0},{64,32},{96,64},{128,96},{160,128},{192,160},{224,1... | collective-permute-start | bytes 860168 | tf_op jit(solution)/shard_map/ppermute | solution.py:21
  24.4 15.2 %all-to-all-start = ((bf16[4,64,1280]{2,1,0:T(8,128)(2,1)}), bf16[4,64,1280]{2,1,0:T(8,128)(2,1)S(1)}, u32[]{:S(2)}, u32[]{:S(2)}) async-start(bf16[4,64,1280]{2,1,0:T(8,128)(2,1)} %norm_cut.1), calls=%async_computation | async-start | bytes 1310720 | tf_op jit(solution)/shard_map/all_to_all | solution.py:401
  27.9 140.8 %all-gather.2.cloned.1.call-start = ((), (), s32[]{:S(2)}) async-start(), calls=%async_computation.4 | async-start | bytes 1843200 | tf_op jit(solution)/shard_map/all_gather | solution.py:413
  30.4 69.7 %copy-start.2 = (bf16[2064,128]{1,0:T(8,128)(2,1)}, bf16[2064,128]{1,0:T(8,128)(2,1)S(1)}, u32[]{:S(2)}) copy-start(bf16[2064,128]{1,0:T(8,128)(2,1)S(1)} %collective-permute-done.4.refs_9_) | copy-start | bytes 1585156
  30.4 8.5 %collective-permute-start.5 = (bf16[160,896]{1,0:T(8,128)(2,1)S(1)}, bf16[160,896]{1,0:T(8,128)(2,1)S(1)}, u32[]{:S(2)}, u32[]{:S(2)}) collective-permute-start(bf16[160,896]{1,0:T(8,128)(2,1)S(1)} %collective-permute-done.2.refs_2_), channel_id=1, source_target_pairs={{0,32},{32,64},{64,96},{96,128},{128,160},{160,192},{192,224},{224... | collective-permute-start | bytes 860168 | tf_op jit(solution)/shard_map/ppermute | solution.py:21
  32.3 7.4 %collective-permute-start.6 = (bf16[160,896]{1,0:T(8,128)(2,1)S(1)}, bf16[160,896]{1,0:T(8,128)(2,1)}, u32[]{:S(2)}, u32[]{:S(2)}) collective-permute-start(bf16[160,896]{1,0:T(8,128)(2,1)S(1)} %collective-permute-done.3.refs_6_), channel_id=1, source_target_pairs={{0,224},{32,0},{64,32},{96,64},{128,96},{160,128},{192,160},{224,1... | collective-permute-start | bytes 860168 | tf_op jit(solution)/shard_map/ppermute | solution.py:21
  39.7 8.5 %collective-permute-start.7 = (bf16[160,896]{1,0:T(8,128)(2,1)}, bf16[160,896]{1,0:T(8,128)(2,1)}, u32[]{:S(2)}, u32[]{:S(2)}) collective-permute-start(bf16[160,896]{1,0:T(8,128)(2,1)} %copy-done.15), channel_id=1, source_target_pairs={{0,32},{32,64},{64,96},{96,128},{128,160},{160,192},{192,224},{224... | collective-permute-start | bytes 860168 | tf_op jit(solution)/shard_map/ppermute | solution.py:21
  40.8 11.2 %collective-permute-start.8 = (bf16[2048,128]{1,0:T(8,128)(2,1)S(1)}, bf16[2048,128]{1,0:T(8,128)(2,1)S(1)}, u32[]{:S(2)}, u32[]{:S(2)}) collective-permute-start(bf16[2048,128]{1,0:T(8,128)(2,1)S(1)} %bitcast.19), channel_id=1, source_target_pairs={{0,16},{16,0},{1,17},{17,1},{2,18},{18,2},{3,19},{19,3},{4,20},{20... | collective-permute-start | bytes 1572872 | tf_op jit(solution)/shard_map/ppermute | solution.py:21
  51.9 2.0 collective-permute-start.9
  51.9 48.2 %copy-start.6 = (bf16[2048,128]{1,0:T(8,128)(2,1)}, bf16[2048,128]{1,0:T(8,128)(2,1)S(1)}, u32[]{:S(2)}) copy-start(bf16[2048,128]{1,0:T(8,128)(2,1)S(1)} %collective-permute-done.8.refs_13_) | copy-start | bytes 1572868
  56.7 6.5 %collective-permute-start.10 = (f32[64,640]{1,0:T(8,128)}, f32[64,640]{1,0:T(8,128)S(1)}, u32[]{:S(2)}, u32[]{:S(2)}) collective-permute-start(f32[64,640]{1,0:T(8,128)} %get-tuple-element.48), channel_id=1, source_target_pairs={{0,16},{16,0},{1,17},{17,1},{2,18},{18,2},{3,19},{19,3},{4,20},{20... | collective-permute-start | bytes 491528 | tf_op jit(solution)/shard_map/ppermute | solution.py:21
  64.2 36.0 %copy-start.10 = (bf16[64,640]{1,0:T(8,128)(2,1)}, bf16[64,640]{1,0:T(8,128)(2,1)S(1)}, u32[]{:S(2)}) copy-start(bf16[64,640]{1,0:T(8,128)(2,1)S(1)} %multiply_convert_fusion.refs_0_) | copy-start | bytes 245764
  64.2 5.7 %collective-permute-start.11 = (bf16[64,640]{1,0:T(8,128)(2,1)S(1)}, bf16[64,640]{1,0:T(8,128)(2,1)S(1)}, u32[]{:S(2)}, u32[]{:S(2)}) collective-permute-start(bf16[64,640]{1,0:T(8,128)(2,1)S(1)} %multiply_convert_fusion.refs_0_), channel_id=1, source_target_pairs={{0,32},{32,64},{64,96},{96,128},{128,160},{160,192},{192,224},{224... | collective-permute-start | bytes 245768 | tf_op jit(solution)/shard_map/ppermute | solution.py:21
  64.3 5.6 %collective-permute-start.12 = (bf16[64,640]{1,0:T(8,128)(2,1)S(1)}, bf16[64,640]{1,0:T(8,128)(2,1)S(1)}, u32[]{:S(2)}, u32[]{:S(2)}) collective-permute-start(bf16[64,640]{1,0:T(8,128)(2,1)S(1)} %multiply_convert_fusion.refs_0_), channel_id=1, source_target_pairs={{0,224},{32,0},{64,32},{96,64},{128,96},{160,128},{192,160},{224,1... | collective-permute-start | bytes 245768 | tf_op jit(solution)/shard_map/ppermute | solution.py:21
  69.9 6.6 %collective-permute-start.13 = (bf16[64,640]{1,0:T(8,128)(2,1)S(1)}, bf16[64,640]{1,0:T(8,128)(2,1)S(1)}, u32[]{:S(2)}, u32[]{:S(2)}) collective-permute-start(bf16[64,640]{1,0:T(8,128)(2,1)S(1)} %collective-permute-done.11.refs_1_), channel_id=1, source_target_pairs={{0,32},{32,64},{64,96},{96,128},{128,160},{160,192},{192,224},{224... | collective-permute-start | bytes 245768 | tf_op jit(solution)/shard_map/ppermute | solution.py:21
  70.2 6.4 %collective-permute-start.14 = (bf16[64,640]{1,0:T(8,128)(2,1)S(1)}, bf16[64,640]{1,0:T(8,128)(2,1)S(1)}, u32[]{:S(2)}, u32[]{:S(2)}) collective-permute-start(bf16[64,640]{1,0:T(8,128)(2,1)S(1)} %collective-permute-done.12.refs_7_), channel_id=1, source_target_pairs={{0,224},{32,0},{64,32},{96,64},{128,96},{160,128},{192,160},{224,1... | collective-permute-start | bytes 245768 | tf_op jit(solution)/shard_map/ppermute | solution.py:21
  73.2 23.1 %collective-permute-start.18 = (bf16[2064,128]{1,0:T(8,128)(2,1)S(1)}, bf16[2064,128]{1,0:T(8,128)(2,1)S(1)}, u32[]{:S(2)}, u32[]{:S(2)}) collective-permute-start(bf16[2064,128]{1,0:T(8,128)(2,1)S(1)} %copy-done.1), channel_id=1, source_target_pairs={{0,8},{8,0},{1,9},{9,1},{2,10},{10,2},{3,11},{11,3},{4,12},{12,4},... | collective-permute-start | bytes 1585160 | tf_op jit(solution)/shard_map/ppermute | solution.py:21
  76.5 7.1 %collective-permute-start.15 = (bf16[64,640]{1,0:T(8,128)(2,1)S(1)}, bf16[64,640]{1,0:T(8,128)(2,1)S(1)}, u32[]{:S(2)}, u32[]{:S(2)}) collective-permute-start(bf16[64,640]{1,0:T(8,128)(2,1)S(1)} %collective-permute-done.13.refs_2_), channel_id=1, source_target_pairs={{0,32},{32,64},{64,96},{96,128},{128,160},{160,192},{192,224},{224... | collective-permute-start | bytes 245768 | tf_op jit(solution)/shard_map/ppermute | solution.py:21
  79.6 16.9 %collective-permute-start.19 = (bf16[2064,128]{1,0:T(8,128)(2,1)S(1)}, bf16[2064,128]{1,0:T(8,128)(2,1)S(1)}, u32[]{:S(2)}, u32[]{:S(2)}) collective-permute-start(bf16[2064,128]{1,0:T(8,128)(2,1)S(1)} %collective-permute-done.4.refs_9_), channel_id=1, source_target_pairs={{0,8},{8,0},{1,9},{9,1},{2,10},{10,2},{3,11},{11,3},{4,12},{12,4},... | collective-permute-start | bytes 1585160 | tf_op jit(solution)/shard_map/ppermute | solution.py:21
  79.6 16.9 %collective-permute-start.20 = (bf16[2048,128]{1,0:T(8,128)(2,1)S(1)}, bf16[2048,128]{1,0:T(8,128)(2,1)S(1)}, u32[]{:S(2)}, u32[]{:S(2)}) collective-permute-start(bf16[2048,128]{1,0:T(8,128)(2,1)S(1)} %bitcast.20), channel_id=1, source_target_pairs={{0,8},{8,0},{1,9},{9,1},{2,10},{10,2},{3,11},{11,3},{4,12},{12,4},... | collective-permute-start | bytes 1572872 | tf_op jit(solution)/shard_map/ppermute | solution.py:21
  80.1 20.0 %collective-permute-start.21 = (bf16[2048,128]{1,0:T(8,128)(2,1)S(1)}, bf16[2048,128]{1,0:T(8,128)(2,1)S(1)}, u32[]{:S(2)}, u32[]{:S(2)}) collective-permute-start(bf16[2048,128]{1,0:T(8,128)(2,1)S(1)} %collective-permute-done.8.refs_13_), channel_id=1, source_target_pairs={{0,8},{8,0},{1,9},{9,1},{2,10},{10,2},{3,11},{11,3},{4,12},{12,4},... | collective-permute-start | bytes 1572872 | tf_op jit(solution)/shard_map/ppermute | solution.py:21
  83.7 5.6 %collective-permute-start.16 = (bf16[64,640]{1,0:T(8,128)(2,1)S(1)}, bf16[64,640]{1,0:T(8,128)(2,1)S(1)}, u32[]{:S(2)}, u32[]{:S(2)}) collective-permute-start(bf16[64,640]{1,0:T(8,128)(2,1)S(1)} %collective-permute-done.14.refs_6_), channel_id=1, source_target_pairs={{0,224},{32,0},{64,32},{96,64},{128,96},{160,128},{192,160},{224,1... | collective-permute-start | bytes 245768 | tf_op jit(solution)/shard_map/ppermute | solution.py:21
  89.3 5.2 %collective-permute-start.22 = (f32[2,64,256]{2,1,0:T(8,128)}, f32[2,64,256]{2,1,0:T(8,128)S(1)}, u32[]{:S(2)}, u32[]{:S(2)}) collective-permute-start(f32[2,64,256]{2,1,0:T(8,128)} %get-tuple-element.57), channel_id=1, source_target_pairs={{0,16},{16,0},{1,17},{17,1},{2,18},{18,2},{3,19},{19,3},{4,20},{20... | collective-permute-start | bytes 393224 | tf_op jit(solution)/shard_map/ppermute | solution.py:21
  94.5 5.7 %collective-permute-start.17 = (bf16[64,640]{1,0:T(8,128)(2,1)S(1)}, bf16[64,640]{1,0:T(8,128)(2,1)S(1)}, u32[]{:S(2)}, u32[]{:S(2)}) collective-permute-start(bf16[64,640]{1,0:T(8,128)(2,1)S(1)} %collective-permute-done.15.refs_3_), channel_id=1, source_target_pairs={{0,32},{32,64},{64,96},{96,128},{128,160},{160,192},{192,224},{224... | collective-permute-start | bytes 245768 | tf_op jit(solution)/shard_map/ppermute | solution.py:21
  96.4 1.3 collective-permute-start.23
  162.8 4.7 %collective-permute-start.25 = (bf16[64,640]{1,0:T(8,128)(2,1)}, bf16[64,640]{1,0:T(8,128)(2,1)S(1)}, u32[]{:S(2)}, u32[]{:S(2)}) collective-permute-start(bf16[64,640]{1,0:T(8,128)(2,1)} %merge.1.refs_0_), channel_id=1, source_target_pairs={{0,16},{16,0},{1,17},{17,1},{2,18},{18,2},{3,19},{19,3},{4,20},{20... | collective-permute-start | bytes 245768 | tf_op jit(solution)/shard_map/ppermute | solution.py:21
  163.8 3.6 %collective-permute-start.24 = (bf16[64,640]{1,0:T(8,128)(2,1)}, bf16[64,640]{1,0:T(8,128)(2,1)S(1)}, u32[]{:S(2)}, u32[]{:S(2)}) collective-permute-start(bf16[64,640]{1,0:T(8,128)(2,1)} %merge.1.refs_0_), channel_id=1, source_target_pairs={{0,8},{8,0},{1,9},{9,1},{2,10},{10,2},{3,11},{11,3},{4,12},{12,4},... | collective-permute-start | bytes 245768 | tf_op jit(solution)/shard_map/ppermute | solution.py:21
  167.5 1.3 collective-permute-start.26
  (25 other events, 300.1 us)
Sparse Core Ops, SparseCore 0:
  58.9 40.4 all-gather.1
